TPU v7x, 32 devices: a whole 2x2x4 slice. The times are simulated.
32 devices in a mesh: ctx: 8 (over y, x, core), seq: 4 (over z).
Axes of the slice: x: 2, y: 2, z: 4, core: 2. Of those that a mesh axis runs over, the one named last changes fastest.
Arguments:
- tokens: bfloat16 [4, 1024, 2560], P('seq', 'ctx'), may hold values from -6 to 6
- cotangent: bfloat16 [4, 1024, 2560], P('seq', 'ctx'), may hold values from -6 to 6
- gain_attn: bfloat16 [2560], P(('ctx', 'seq')), may hold values from 0.25 to 1.75
- w_query: bfloat16 [2560, 2560], P(('ctx', 'seq')), may hold values from -0.125 to 0.125
- w_keyval: bfloat16 [2560, 512], P(('ctx', 'seq')), may hold values from -0.125 to 0.125
- w_out: bfloat16 [2560, 2560], P(('ctx', 'seq')), may hold values from -6 to 6
- b_out: bfloat16 [2560], P(('ctx', 'seq')), may hold values from -4 to 4
- gain_ffn: bfloat16 [2560], P(('ctx', 'seq')), may hold values from 0.25 to 1.75
- w_gateup: bfloat16 [2560, 15360], P(('ctx', 'seq')), may hold values from -0.125 to 0.125
- w_down: bfloat16 [7680, 2560], P(('ctx', 'seq')), may hold values from -0.125 to 0.125
Outputs:
- output: bfloat16 [4, 1024, 2560], P('seq', 'ctx')
- input_grad: float32 [4, 1024, 2560], P('seq', 'ctx')
- gain_attn_grad: float32 [2560], P(('ctx', 'seq'))
- w_query_grad: float32 [2560, 2560], P('seq', 'ctx')
- w_keyval_grad: float32 [2560, 512], P('seq', 'ctx')
- w_out_grad: float32 [2560, 2560], P('ctx', 'seq')
- b_out_grad: float32 [2560], P(('ctx', 'seq'))
- gain_ffn_grad: float32 [2560], P(('ctx', 'seq'))
- w_gateup_grad: float32 [2560, 15360], P('seq', 'ctx')
- w_down_grad: float32 [7680, 2560], P('ctx', 'seq')
All inputs are finite; a program needn't handle non-finite values.
Results may differ from a plain program's by a relative error of at most 0.017.
Values may be sent and summed in bfloat16 or wider, within the bound.
No kernel may reach another device: no remote copies, remote signals or barrier semaphores. Data moves between devices by JAX's collectives and lax.ppermute only.
A program may use at most 640 MiB of HBM per device.

v0:
```python
import jax
import jax.numpy as jnp
from jax import lax
from jax.sharding import PartitionSpec as P

NH = 10
HD = 256
FF = 7680
WINDOW = 2048


EPS = 1e-06
NEG = -1e30


def from_behind(value, axis, steps):
    count = lax.axis_size(axis)
    leading, last = (max(0, -steps), min(count, count - steps))
    return lax.ppermute(value, axis, [(source, source + steps) for source in range(leading, last)])


def norm_forward(residual, gain_vec):
    scale = lax.rsqrt(jnp.mean(residual * residual, axis=-1, keepdims=True) + EPS)
    normed = residual * scale
    return (normed, scale, (normed * gain_vec.astype(jnp.float32)).astype(jnp.bfloat16))


def norm_backward(d_in, normed, scale, gain_vec):
    d_normed = d_in * gain_vec.astype(jnp.float32)
    d_gain = jnp.sum(d_in * normed, axis=0)
    d_resid = scale * (d_normed - normed * jnp.mean(d_normed * normed, axis=-1, keepdims=True))
    return (d_resid, d_gain)


def gelu_parts(gate_pre):
    gelu_val, pullback = jax.vjp(lambda v: jax.nn.gelu(v, approximate=True), gate_pre)
    return (gelu_val, pullback(jnp.ones_like(gate_pre))[0])


def dot_last(left, right):
    return lax.dot_general(
        left, right, (((1,), (1,)), ((), ())), preferred_element_type=jnp.float32
    )


def dot_first(left, right):
    return lax.dot_general(
        left, right, (((0,), (0,)), ((), ())), preferred_element_type=jnp.float32
    )


def allowed_mask(query_pos, key_pos):
    spacing = query_pos[:, None] - key_pos[None, :]
    return (spacing >= 0) & (spacing < WINDOW) & (key_pos[None, :] >= 0)


def halo_hops(halo_blocks):
    return [1] + [2**level for level in range(halo_blocks.bit_length() - 1)]


def gather_window(keyval, halo_blocks):
    stacked = keyval
    for level, hop_size in enumerate(halo_hops(halo_blocks)):
        moved = from_behind(stacked, "ctx", hop_size)
        stacked = moved if level == 0 else jnp.concatenate([moved, stacked], axis=0)
    window_kv = jnp.concatenate([stacked, keyval], axis=0)
    return window_kv


def return_window(d_window, block_len, halo_blocks):
    own_part = d_window[halo_blocks * block_len :]
    pending = d_window[: halo_blocks * block_len]
    hops = halo_hops(halo_blocks)
    for level in range(len(hops) - 1, -1, -1):
        hop_size = hops[level]
        moved = from_behind(
            pending[: hop_size * block_len].astype(jnp.bfloat16), "ctx", -hop_size
        ).astype(jnp.float32)
        if level > 0:
            pending = pending[hop_size * block_len :] + moved
        else:
            own_part = own_part + moved
    return own_part


def score_block(query, window_kv, allowed):
    scores = jnp.einsum("qhd,kd->hqk", query, window_kv[:, :HD], preferred_element_type=jnp.float32)
    return jnp.where(allowed[None], scores, NEG)


def per_device(
    tokens, cotangent, gain_attn, w_query, w_keyval, w_out, b_out, gain_ffn, w_gateup, w_down
):
    block_len = tokens.shape[1]
    width = tokens.shape[2]
    q_scale = HD ** (-0.5)
    halo_blocks = WINDOW // block_len
    position = lax.axis_index("ctx")
    residual = tokens.reshape(block_len, width).astype(jnp.float32)
    full_gain1, full_query, full_keyval, full_out, full_bias = (
        lax.all_gather(gain_attn, ("ctx", "seq"), axis=0, tiled=True),
        lax.all_gather(w_query, ("ctx", "seq"), axis=0, tiled=True),
        lax.all_gather(w_keyval, ("ctx", "seq"), axis=0, tiled=True),
        lax.all_gather(w_out, ("ctx", "seq"), axis=0, tiled=True),
        lax.all_gather(b_out, ("ctx", "seq"), axis=0, tiled=True),
    )
    normed1, scale1, hidden1 = norm_forward(residual, full_gain1)
    query = (
        (jnp.dot(hidden1, full_query, preferred_element_type=jnp.float32) * q_scale)
        .astype(jnp.bfloat16)
        .reshape(block_len, NH, HD)
    )
    keyval = jnp.dot(hidden1, full_keyval, preferred_element_type=jnp.float32).astype(jnp.bfloat16)
    window_kv = gather_window(keyval, halo_blocks)
    query_pos = position * block_len + jnp.arange(block_len, dtype=jnp.int32)
    key_pos = (position - halo_blocks) * block_len + jnp.arange(
        (halo_blocks + 1) * block_len, dtype=jnp.int32
    )
    allowed = allowed_mask(query_pos, key_pos)
    value_part = window_kv[:, HD:]
    scores = score_block(query, window_kv, allowed)
    maximum = jnp.max(scores, axis=-1, keepdims=True)
    log_total = maximum + jnp.log(jnp.sum(jnp.exp(scores - maximum), axis=-1, keepdims=True))
    probs_low = jnp.exp(scores - log_total).astype(jnp.bfloat16)
    mixed = jnp.einsum(
        "hqk,kd->qhd", probs_low, value_part, preferred_element_type=jnp.float32
    ).astype(jnp.bfloat16)
    mixed_flat = mixed.reshape(block_len, NH * HD)
    middle = (
        residual
        + jnp.dot(mixed_flat, full_out, preferred_element_type=jnp.float32)
        + full_bias.astype(jnp.float32)
    )
    full_gain2, full_gateup, full_down = (
        lax.all_gather(gain_ffn, ("ctx", "seq"), axis=0, tiled=True),
        lax.all_gather(w_gateup, ("ctx", "seq"), axis=0, tiled=True),
        lax.all_gather(w_down, ("ctx", "seq"), axis=0, tiled=True),
    )
    normed2, scale2, hidden2 = norm_forward(middle, full_gain2)
    gateup = jnp.dot(hidden2, full_gateup, preferred_element_type=jnp.float32)
    gate_pre = gateup[:, :FF]
    up_pre = gateup[:, FF:]
    gelu_val, gelu_slope = gelu_parts(gate_pre)
    inner = (gelu_val * up_pre).astype(jnp.bfloat16)
    output = (middle + jnp.dot(inner, full_down, preferred_element_type=jnp.float32)).astype(
        jnp.bfloat16
    )
    full_gain2, full_gateup, full_down, full_gain1, full_query, full_keyval, full_out = (
        lax.all_gather(gain_ffn, ("ctx", "seq"), axis=0, tiled=True),
        lax.all_gather(w_gateup, ("ctx", "seq"), axis=0, tiled=True),
        lax.all_gather(w_down, ("ctx", "seq"), axis=0, tiled=True),
        lax.all_gather(gain_attn, ("ctx", "seq"), axis=0, tiled=True),
        lax.all_gather(w_query, ("ctx", "seq"), axis=0, tiled=True),
        lax.all_gather(w_keyval, ("ctx", "seq"), axis=0, tiled=True),
        lax.all_gather(w_out, ("ctx", "seq"), axis=0, tiled=True),
    )
    d_final = cotangent.reshape(block_len, width)
    d_inner = dot_last(d_final, full_down)
    d_gateup = jnp.concatenate([d_inner * up_pre * gelu_slope, d_inner * gelu_val], axis=1).astype(
        jnp.bfloat16
    )
    hidden_rows, final_rows = (
        lax.all_gather(hidden2, "ctx", axis=0, tiled=True),
        lax.all_gather(d_final, "ctx", axis=0, tiled=True),
    )
    gateup_cols, inner_cols = (
        lax.all_to_all(d_gateup, "ctx", split_axis=1, concat_axis=0, tiled=True),
        lax.all_to_all(inner, "ctx", split_axis=1, concat_axis=0, tiled=True),
    )
    gateup_share = dot_first(hidden_rows, gateup_cols)
    down_share = dot_first(inner_cols, final_rows)
    gateup_grad, down_grad = (
        lax.psum_scatter(
            gateup_share.astype(jnp.bfloat16), "seq", scatter_dimension=0, tiled=True
        ).astype(jnp.float32),
        lax.psum_scatter(
            down_share.astype(jnp.bfloat16), "seq", scatter_dimension=1, tiled=True
        ).astype(jnp.float32),
    )
    d_hidden2 = dot_last(d_gateup, full_gateup)
    d_middle_norm, d_gain2 = norm_backward(d_hidden2, normed2, scale2, full_gain2)
    d_middle = d_final.astype(jnp.float32) + d_middle_norm
    d_bias = jnp.sum(d_middle, axis=0)
    d_low = d_middle.astype(jnp.bfloat16)
    d_mixed = dot_last(d_low, full_out).astype(jnp.bfloat16).reshape(block_len, NH, HD)
    scores = score_block(query, window_kv, allowed)
    probs = jnp.exp(scores - log_total)
    probs_again = probs.astype(jnp.bfloat16)
    d_probs = jnp.einsum("qhd,kd->hqk", d_mixed, value_part, preferred_element_type=jnp.float32)
    delta = jnp.sum(probs * d_probs, axis=-1, keepdims=True)
    d_scores = (probs * (d_probs - delta)).astype(jnp.bfloat16)
    d_query = (
        jnp.einsum("hqk,kd->qhd", d_scores, window_kv[:, :HD], preferred_element_type=jnp.float32)
        * q_scale
    )
    d_keys = jnp.einsum("hqk,qhd->kd", d_scores, query, preferred_element_type=jnp.float32)
    d_values = jnp.einsum("hqk,qhd->kd", probs_again, d_mixed, preferred_element_type=jnp.float32)
    d_window = jnp.concatenate([d_keys, d_values], axis=1)
    d_keyval = return_window(d_window, block_len, halo_blocks)
    d_query_low = d_query.reshape(block_len, NH * HD).astype(jnp.bfloat16)
    d_keyval_low = d_keyval.astype(jnp.bfloat16)
    d_hidden1 = dot_last(d_query_low, full_query) + dot_last(d_keyval_low, full_keyval)
    d_input_norm, d_gain1 = norm_backward(d_hidden1, normed1, scale1, full_gain1)
    d_input = d_middle + d_input_norm
    normed_rows, low_rows = (
        lax.all_gather(hidden1, "ctx", axis=0, tiled=True),
        lax.all_gather(d_low, "ctx", axis=0, tiled=True),
    )
    query_cols, keyval_cols, mixed_cols = (
        lax.all_to_all(d_query_low, "ctx", split_axis=1, concat_axis=0, tiled=True),
        lax.all_to_all(d_keyval_low, "ctx", split_axis=1, concat_axis=0, tiled=True),
        lax.all_to_all(mixed_flat, "ctx", split_axis=1, concat_axis=0, tiled=True),
    )
    query_share = dot_first(normed_rows, query_cols)
    keyval_share = dot_first(normed_rows, keyval_cols)
    out_share = dot_first(mixed_cols, low_rows)
    query_grad, keyval_grad, out_grad = (
        lax.psum_scatter(
            query_share.astype(jnp.bfloat16), "seq", scatter_dimension=0, tiled=True
        ).astype(jnp.float32),
        lax.psum_scatter(
            keyval_share.astype(jnp.bfloat16), "seq", scatter_dimension=0, tiled=True
        ).astype(jnp.float32),
        lax.psum_scatter(
            out_share.astype(jnp.bfloat16), "seq", scatter_dimension=1, tiled=True
        ).astype(jnp.float32),
    )
    gain1_grad, bias_grad, gain2_grad = (
        lax.psum_scatter(d_gain1, ("ctx", "seq"), scatter_dimension=0, tiled=True),
        lax.psum_scatter(d_bias, ("ctx", "seq"), scatter_dimension=0, tiled=True),
        lax.psum_scatter(d_gain2, ("ctx", "seq"), scatter_dimension=0, tiled=True),
    )
    return (
        output.reshape(1, block_len, width),
        d_input.reshape(1, block_len, width),
        gain1_grad,
        query_grad,
        keyval_grad,
        out_grad,
        bias_grad,
        gain2_grad,
        gateup_grad,
        down_grad,
    )


def solution(mesh):
    return jax.shard_map(
        per_device,
        mesh=mesh,
        in_specs=(
            P("seq", "ctx", None),
            P("seq", "ctx", None),
            P(("ctx", "seq")),
            P(("ctx", "seq"), None),
            P(("ctx", "seq"), None),
            P(("ctx", "seq"), None),
            P(("ctx", "seq")),
            P(("ctx", "seq")),
            P(("ctx", "seq"), None),
            P(("ctx", "seq"), None),
        ),
        out_specs=(
            P("seq", "ctx", None),
            P("seq", "ctx", None),
            P(("ctx", "seq")),
            P("seq", "ctx"),
            P("seq", "ctx"),
            P("ctx", "seq"),
            P(("ctx", "seq")),
            P(("ctx", "seq")),
            P("seq", "ctx"),
            P("ctx", "seq"),
        ),
        check_vma=False,
    )
```

profile of v0, /device:TPU:0, one launch (start us, length us, event | category | flops | bytes accessed | tf_op | source)
XLA Modules:
  0.0 1485.1 jit_solution(17343134293406402455)
XLA Ops:
  11.4 42.4 %all-reduce.7 = (bf16[2560]{0:T(1024)(128)(2,1)S(1)}, bf16[2560]{0:T(1024)(128)(2,1)S(1)}, bf16[2560]{0:T(1024)(128)(2,1)S(1)}) all-reduce(bf16[2560]{0:T(1024)(128)(2,1)S(1)} %dynamic-update-slice, bf16[2560]{0:T(1024)(128)(2,1)S(1)} %dynamic-update-slice.1, ...), channel_id=1, replica_groups=mesh['ctx'=8,'seq'=4] {'ctx','seq'}, use_global_device_ids=true, to_apply=%add | all-reduce | flops 7680 | bytes 30720
  55.5 16.2 %all-gather.11.cloned.1.call-done = bf16[2560,512]{1,0:T(8,128)(2,1)} async-done(((bf16[80,512]{1,0:T(8,128)(2,1)}), bf16[2560,512]{1,0:T(8,128)(2,1)}) %all-gather.11.cloned.1.call-update) | async-done | bytes 2621456 | tf_op jit(solution)/shard_map/all_gather | solution.py:103
  82.3 9.1 collective-permute-start.2
  101.8 14.6 collective-permute-done.3
  128.2 45.6 %all-gather.13.cloned.1.call-done = bf16[2560,2560]{1,0:T(8,128)(2,1)} async-done(((bf16[80,2560]{1,0:T(8,128)(2,1)}), bf16[2560,2560]{1,0:T(8,128)(2,1)}) %all-gather.13.cloned.1.call-update) | async-done | bytes 13107216 | tf_op jit(solution)/shard_map/all_gather | solution.py:102
  173.8 6.6 fusion.19
  192.4 81.0 %all-gather.15.cloned.1.call-done = bf16[2560,2560]{1,0:T(8,128)(2,1)} async-done(((bf16[80,2560]{1,0:T(8,128)(2,1)}), bf16[2560,2560]{1,0:T(8,128)(2,1)}) %all-gather.15.cloned.1.call-update) | async-done | bytes 13107216 | tf_op jit(solution)/shard_map/all_gather | solution.py:104
  273.4 7.0 multiply_reduce_fusion.2
  280.6 405.2 %all-gather.17.cloned.1.call-done = bf16[2560,15360]{1,0:T(8,128)(2,1)} async-done(((bf16[80,15360]{1,0:T(8,128)(2,1)}), bf16[2560,15360]{1,0:T(8,128)(2,1)}) %all-gather.17.cloned.1.call-update) | async-done | bytes 78643216 | tf_op jit(solution)/shard_map/all_gather | solution.py:136
  685.8 31.8 %fusion.62 = f32[128,15360]{1,0:T(8,128)} fusion(bf16[128,2560]{1,0:T(8,128)(2,1)S(1)} %multiply_convert_fusion.2, bf16[2560,15360]{1,0:T(8,128)(2,1)} %all-gather.17.cloned.1.call-done), kind=kOutput, calls=%fused_computation.127 | convolution fusion | flops 10066329600 | bytes 87162880 | tf_op jit(solution)/shard_map/dot_general | solution.py:140
  717.6 191.6 %all-gather.19.cloned.1.call-done = bf16[7680,2560]{1,0:T(8,128)(2,1)} async-done(((bf16[240,2560]{1,0:T(8,128)(2,1)}), bf16[7680,2560]{1,0:T(8,128)(2,1)}) %all-gather.19.cloned.1.call-update) | async-done | bytes 39321616 | tf_op jit(solution)/shard_map/all_gather | solution.py:137
  909.1 21.2 %fusion.13 = (bf16[128,7680]{1,0:T(8,128)(2,1)S(1)}, bf16[128,7680]{1,0:T(8,128)(2,1)}, bf16[128,7680]{1,0:T(8,128)(2,1)}) fusion(f32[128,15360]{1,0:T(8,128)} %fusion.62, bf16[7680,2560]{1,0:T(8,128)(2,1)} %all-gather.19.cloned.1.call-done, bf16[1,128,2560]{2,1,0:T(8,128)(2,1)} %param.11), kind=kOutput, calls=%fused_computation.30 | convolution fusion | flops 5057740800 | bytes 53739520 | tf_op jit(solution)/shard_map/dot_general | solution.py:41
  930.4 36.0 %multiply_reduce_fusion = (f32[2560]{0:T(1024)}, f32[128]{0:T(128)}, f32[128,2560]{1,0:T(8,128)}) fusion(f32[128,2560]{1,0:T(8,128)S(1)} %get-tuple-element.28, f32[128]{0:T(128)} %copy-done.17, f32[2560]{0:T(1024)} %convert_element_type.138, bf16[2560,15360]{1,0:T(8,128)(2,1)} %all-gather.17.cloned.1.call-done, bf16[128,7680]{1,0:T(8,128)(2,1)} %get-tuple-element.23, ...), kind=kOutput, calls=%fused_computation.76 | convolution fusion | flops 10076157952 | bytes 85218304 | tf_op jit(solution)/shard_map/dot_general | solution.py:41
  971.2 10.1 convolution_convert_fusion.4
  982.8 7.6 fusion
  1004.5 20.7 %collective-permute-done.6 = bf16[512,512]{0,1:T(8,128)(2,1)S(1)} collective-permute-done((bf16[512,512]{0,1:T(8,128)(2,1)S(1)}, bf16[512,512]{0,1:T(8,128)(2,1)S(1)}, u32[]{:S(2)}, u32[]{:S(2)}) %collective-permute-start.6) | collective-permute-done | bytes 524320 | tf_op jit(solution)/shard_map/ppermute | solution.py:19
  1026.7 14.9 %collective-permute-done.7 = bf16[256,512]{0,1:T(8,128)(2,1)S(1)} collective-permute-done((bf16[256,512]{0,1:T(8,128)(2,1)S(1)}, bf16[256,512]{0,1:T(8,128)(2,1)S(1)}, u32[]{:S(2)}, u32[]{:S(2)}) %collective-permute-start.7) | collective-permute-done | bytes 262176 | tf_op jit(solution)/shard_map/ppermute | solution.py:19
  1046.3 5.9 collective-permute-done.9
  1052.9 6.8 all-to-all-start.1
  1059.7 5.9 fusion.31
  1075.6 8.6 all-to-all-done
  1084.2 5.8 convolution_convert_fusion.2
  1102.3 25.2 %all-to-all-done.4 = bf16[128,8,960]{0,2,1:T(8,128)(2,1)} async-done(((bf16[128,8,960]{0,2,1:T(8,128)(2,1)}), bf16[128,8,960]{0,2,1:T(8,128)(2,1)}, u32[]{:S(2)}, u32[]{:S(2)}) %all-to-all-start.4) | async-done | bytes 1966112 | tf_op jit(solution)/shard_map/all_to_all | solution.py:168
  1127.4 10.2 convolution_convert_fusion.1
  1137.7 7.9 copy.80
  1154.1 6.1 all-to-all-done.2
  1174.3 36.7 %all-to-all-done.3 = bf16[128,8,1920]{2,0,1:T(8,128)(2,1)} async-done(((bf16[128,8,1920]{2,0,1:T(8,128)(2,1)}), bf16[128,8,1920]{2,0,1:T(8,128)(2,1)}, u32[]{:S(2)}, u32[]{:S(2)}) %all-to-all-start.3) | async-done | bytes 3932192 | tf_op jit(solution)/shard_map/all_to_all | solution.py:167
  1211.1 16.5 %convolution_convert_fusion = bf16[2560,1920]{1,0:T(8,128)(2,1)} fusion(bf16[1024,2560]{1,0:T(8,128)(2,1)} %all-gather.25.cloned.1.call-done, bf16[1024,1920]{1,0:T(8,128)(2,1)} %bitcast.26), kind=kOutput, calls=%fused_computation | convolution fusion | flops 10071244800 | bytes 19005440 | tf_op jit(solution)/shard_map/dot_general | solution.py:47
  1227.5 10.5 fusion.63
  1238.1 16.6 %fusion.21 = bf16[1,128,2560]{2,1,0:T(8,128)(2,1)} fusion(f32[128,2560]{1,0:T(8,128)S(1)} %get-tuple-element.28, bf16[128,7680]{1,0:T(8,128)(2,1)} %get-tuple-element.24, bf16[7680,2560]{1,0:T(8,128)(2,1)} %all-gather.19.cloned.1.call-done), kind=kOutput, calls=%fused_computation.47 | convolution fusion | flops 5033820160 | bytes 43253760 | tf_op jit(solution)/shard_map/dot_general | solution.py:145
  1257.3 42.8 %all-reduce.6 = (f32[2560]{0:T(1024)S(1)}, f32[2560]{0:T(1024)S(1)}, f32[2560]{0:T(1024)S(1)}) all-reduce(f32[2560]{0:T(1024)S(1)} %get-tuple-element.12, f32[2560]{0:T(1024)S(1)} %copy-done.16, f32[2560]{0:T(1024)S(1)} %copy-done.15), channel_id=3, replica_groups=mesh['ctx'=8,'seq'=4] {'ctx','seq'}, use_global_device_ids=true, to_apply=%region_8.9.clone | all-reduce | flops 7680 | bytes 61440
  1313.2 160.8 %reduce-scatter.14.cloned.1.call-done = bf16[640,1920]{1,0:T(8,128)(2,1)} async-done(((bf16[2560,1920]{1,0:T(8,128)(2,1)}), bf16[640,1920]{1,0:T(8,128)(2,1)}) %reduce-scatter.14.cloned.1.call-update) | async-done | bytes 2457616 | tf_op jit(solution)/shard_map/reduce_scatter | solution.py:173
  (181 shorter events, 142.7 us)
Async XLA Ops:
  7.2 64.5 %all-gather.11.cloned.1.call-start = ((), (), s32[]{:S(2)}) async-start(), calls=%async_computation.10 | async-start | bytes 2703360 | tf_op jit(solution)/shard_map/all_gather | solution.py:103
  8.0 165.8 %all-gather.13.cloned.1.call-start = ((), (), s32[]{:S(2)}) async-start(), calls=%async_computation.11 | async-start | bytes 13516800 | tf_op jit(solution)/shard_map/all_gather | solution.py:102
  8.7 264.7 %all-gather.15.cloned.1.call-start = ((), (), s32[]{:S(2)}) async-start(), calls=%async_computation.12 | async-start | bytes 13516800 | tf_op jit(solution)/shard_map/all_gather | solution.py:104
  9.4 676.4 %all-gather.17.cloned.1.call-start = ((), (), s32[]{:S(2)}) async-start(), calls=%async_computation.13 | async-start | bytes 81100800 | tf_op jit(solution)/shard_map/all_gather | solution.py:136
  10.0 899.1 %all-gather.19.cloned.1.call-start = ((), (), s32[]{:S(2)}) async-start(), calls=%async_computation.14 | async-start | bytes 40550400 | tf_op jit(solution)/shard_map/all_gather | solution.py:137
  10.6 1060.3 %all-gather.21.cloned.1.call-start = ((), (), s32[]{:S(2)}) async-start(), calls=%async_computation.15 | async-start | bytes 5898240 | tf_op jit(solution)/shard_map/all_gather | solution.py:206
  55.5 1046.8 %all-gather.27.cloned.1.call-start = ((), (), s32[]{:S(2)}) async-start(), calls=%async_computation.19 | async-start | bytes 5898240 | tf_op jit(solution)/shard_map/all_gather | solution.py:164
  74.2 3.1 collective-permute-start
  77.3 4.9 collective-permute-start.1
  82.3 14.1 collective-permute-start.2
  96.5 19.9 %collective-permute-start.3 = (bf16[512,512]{1,0:T(8,128)(2,1)S(1)}, bf16[512,512]{1,0:T(8,128)(2,1)S(1)}, u32[]{:S(2)}, u32[]{:S(2)}) collective-permute-start(bf16[512,512]{1,0:T(8,128)(2,1)S(1)} %pad_maximum_fusion.3), channel_id=1, source_target_pairs={{0,16},{4,20},{8,24},{12,28},{1,17},{5,21},{9,25},{13,29},{2,18},{... | collective-permute-start | bytes 1572872 | tf_op jit(solution)/shard_map/ppermute | solution.py:19
  117.4 5.0 collective-permute-start.4
  119.0 1045.8 %all-gather.23.cloned.1.call-start = ((), (), s32[]{:S(2)}) async-start(), calls=%async_computation.16 | async-start | bytes 5898240 | tf_op jit(solution)/shard_map/all_gather | solution.py:207
  187.9 85.4 %copy-start.14 = (f32[2560]{0:T(1024)S(1)}, f32[2560]{0:T(1024)}, u32[]{:S(2)}) copy-start(f32[2560]{0:T(1024)} %convert_element_type.137) | copy-start | bytes 30724
  280.4 437.2 %copy-start.17 = (f32[128]{0:T(128)}, f32[128]{0:T(128)S(1)}, u32[]{:S(2)}) copy-start(f32[128]{0:T(128)S(1)} %add_rsqrt_fusion) | copy-start | bytes 1540
  280.6 437.0 %copy-start.6 = (bf16[128,2560]{1,0:T(8,128)(2,1)}, bf16[128,2560]{1,0:T(8,128)(2,1)S(1)}, u32[]{:S(2)}) copy-start(bf16[128,2560]{1,0:T(8,128)(2,1)S(1)} %multiply_convert_fusion.2) | copy-start | bytes 1966084
  970.5 203.8 %all-gather.25.cloned.1.call-start = ((), (), s32[]{:S(2)}) async-start(), calls=%async_computation.17 | async-start | bytes 5898240 | tf_op jit(solution)/shard_map/all_gather | solution.py:163
  1002.1 0.7 collective-permute-start.5
  1003.2 22.0 %collective-permute-start.6 = (bf16[512,512]{0,1:T(8,128)(2,1)S(1)}, bf16[512,512]{0,1:T(8,128)(2,1)S(1)}, u32[]{:S(2)}, u32[]{:S(2)}) collective-permute-start(bf16[512,512]{0,1:T(8,128)(2,1)S(1)} %slice.124), channel_id=1, source_target_pairs={{16,0},{20,4},{24,8},{28,12},{17,1},{21,5},{25,9},{29,13},{18,2},{... | collective-permute-start | bytes 1572872 | tf_op jit(solution)/shard_map/ppermute | solution.py:19
  1025.4 16.2 %collective-permute-start.7 = (bf16[256,512]{0,1:T(8,128)(2,1)S(1)}, bf16[256,512]{0,1:T(8,128)(2,1)S(1)}, u32[]{:S(2)}, u32[]{:S(2)}) collective-permute-start(bf16[256,512]{0,1:T(8,128)(2,1)S(1)} %slice.125), channel_id=1, source_target_pairs={{8,0},{12,4},{16,8},{20,12},{24,16},{28,20},{9,1},{13,5},{17,9},{2... | collective-permute-start | bytes 786440 | tf_op jit(solution)/shard_map/ppermute | solution.py:19
  1041.7 3.2 collective-permute-start.8
  1045.0 7.2 collective-permute-start.9
  1052.9 13.7 all-to-all-start.1
  1066.7 17.6 %all-to-all-start = ((bf16[128,8,320]{0,2,1:T(8,128)(2,1)}), bf16[128,8,320]{0,2,1:T(8,128)(2,1)}, u32[]{:S(2)}, u32[]{:S(2)}) async-start(bf16[128,8,320]{0,2,1:T(8,128)(2,1)} %bitcast.19), calls=%async_computation | async-start | bytes 1310720 | tf_op jit(solution)/shard_map/all_to_all | solution.py:210
  1070.8 232.5 %reduce-scatter.18.cloned.1.call-start = ((), (), s32[]{:S(2)}) async-start(), calls=%async_computation.21 | async-start | bytes 819200
  1075.6 229.5 %reduce-scatter.16.cloned.1.call-start = ((), (), s32[]{:S(2)}) async-start(), calls=%async_computation.20 | async-start | bytes 2457600
  1097.8 29.6 %all-to-all-start.4 = ((bf16[128,8,960]{0,2,1:T(8,128)(2,1)}), bf16[128,8,960]{0,2,1:T(8,128)(2,1)}, u32[]{:S(2)}, u32[]{:S(2)}) async-start(bf16[128,8,960]{0,2,1:T(8,128)(2,1)} %bitcast.159), calls=%async_computation.5 | async-start | bytes 3932160 | tf_op jit(solution)/shard_map/all_to_all | solution.py:168
  1102.2 205.1 %reduce-scatter.22.cloned.1.call-start = ((), (), s32[]{:S(2)}) async-start(), calls=%async_computation.23 | async-start | bytes 6553600
  1145.5 14.6 all-to-all-start.2
  1160.2 50.9 %all-to-all-start.3 = ((bf16[128,8,1920]{2,0,1:T(8,128)(2,1)}), bf16[128,8,1920]{2,0,1:T(8,128)(2,1)}, u32[]{:S(2)}, u32[]{:S(2)}) async-start(bf16[128,8,1920]{2,0,1:T(8,128)(2,1)} %pad_maximum_fusion), calls=%async_computation.3 | async-start | bytes 7864320 | tf_op jit(solution)/shard_map/all_to_all | solution.py:167
  1164.7 146.3 %reduce-scatter.20.cloned.1.call-start = ((), (), s32[]{:S(2)}) async-start(), calls=%async_computation.22 | async-start | bytes 2457600
  1174.2 299.7 %reduce-scatter.14.cloned.1.call-start = ((), (), s32[]{:S(2)}) async-start(), calls=%async_computation.18 | async-start | bytes 12288000 | tf_op jit(solution)/shard_map/reduce_scatter | solution.py:173
  (23 other events, 295.1 us)
Sparse Core Ops, SparseCore 0:
  10.9 60.7 all-gather.10
  74.5 99.2 all-gather.12
  176.6 96.6 all-gather.14
  276.0 409.7 all-gather.16
  688.5 220.6 all-gather.18
  911.5 39.2 all-gather.20
  952.7 41.1 all-gather.26
  996.3 53.9 all-gather.22
  1052.2 44.6 all-gather.24
  1099.0 22.1 reduce-scatter.17
  1124.1 40.3 reduce-scatter.15
  1166.6 92.9 reduce-scatter.21
  1262.0 43.0 reduce-scatter.19
  1307.2 166.7 reduce-scatter.13
where the time goes:
time: 1490 us
  waiting for transfers between devices  1050 us (70%)
  matrix products  214 us (14%)
  blocking collectives  85.2 us (6%)
  starting transfers between devices  52.5 us (4%)
  local copies, waits for them, and re-layouts  42.1 us (3%)
  other arithmetic  29.4 us (2%)
    all_gather x1, waiting for transfers between devices, per_device(): lax.all_gather(w_gateup, ('ctx', 'seq'), axis=0, tiled=True)  405 us
    all_gather x1, waiting for transfers between devices, per_device(): lax.all_gather(w_down, ('ctx', 'seq'), axis=0, tiled=True)  192 us
    reduce_scatter x1, waiting for transfers between devices, per_device(): lax.psum_scatter(gateup_share.astype(jnp.bfloat16), 'seq', scatter_dimens...  161 us
    unnamed x2, blocking collectives  85.2 us
    all_gather x1, waiting for transfers between devices, per_device(): lax.all_gather(w_out, ('ctx', 'seq'), axis=0, tiled=True)  81 us
    dot_general x5, matrix products, dot_last(): lax.dot_general(left, right, (((1,), (1,)), ((), ())), preferred_element_...  80.3 us
    ppermute x10, waiting for transfers between devices, from_behind(): lax.ppermute(value, axis, [(source, source + steps) for source in range(l...  65 us
    all_gather x1, waiting for transfers between devices, per_device(): lax.all_gather(w_query, ('ctx', 'seq'), axis=0, tiled=True)  45.6 us
  transfers between devices with their start and end apart: 29, of which 19 were waited for; matrix products, arithmetic and copies ran while one was open for 19% of the time, Pallas kernels for 0%

commit v1 on v0

v1 whole, which is shorter than its diff:
```python
import math

import jax
import jax.numpy as jnp
from jax import lax
from jax.sharding import Mesh, PartitionSpec as P

NH = 10
HD = 256
FF = 7680
WINDOW = 2048

EPS = 1e-06
NEG = -1e30

F32 = jnp.float32
BF16 = jnp.bfloat16

CHIP = ("hi", "lo")
CTX = ("hi", "lo", "core")
GROUP = ("hi", "lo", "core", "far")
SEQ = ("far", "near")
EVERY = ("hi", "lo", "core", "far", "near")


def dot(left, right):
    return jnp.dot(left, right, preferred_element_type=F32)


def dot_last(left, right):
    return lax.dot_general(left, right, (((1,), (1,)), ((), ())), preferred_element_type=F32)


def dot_first(left, right):
    return lax.dot_general(left, right, (((0,), (0,)), ((), ())), preferred_element_type=F32)


def swap(value, axis):
    count = lax.axis_size(axis)
    return lax.ppermute(value, axis, [(i, (i + 1) % count) for i in range(count)])


def chip_shifts():
    side_h, side_l = lax.axis_size("hi"), lax.axis_size("lo")
    return [(dh, dl) for dh in range(side_h) for dl in range(side_l)]


def to_chip(value, dh, dl):
    side_h, side_l = lax.axis_size("hi"), lax.axis_size("lo")
    if dh == 0 and dl == 0:
        return value
    pairs = []
    for h in range(side_h):
        for l in range(side_l):
            pairs.append((h * side_l + l, (h + dh) % side_h * side_l + (l + dl) % side_l))
    return lax.ppermute(value, CHIP, pairs)


def chip_from(dh, dl):
    side_h, side_l = lax.axis_size("hi"), lax.axis_size("lo")
    h, l = lax.axis_index("hi"), lax.axis_index("lo")
    return (h - dh) % side_h * side_l + (l - dl) % side_l


def chip_to(dh, dl):
    side_h, side_l = lax.axis_size("hi"), lax.axis_size("lo")
    h, l = lax.axis_index("hi"), lax.axis_index("lo")
    return (h + dh) % side_h * side_l + (l + dl) % side_l


def gather_ctx(block):
    core = lax.axis_index("core")
    shifts = chip_shifts()
    out = jnp.zeros((len(shifts), 2) + block.shape, block.dtype)
    for dh, dl in shifts:
        came = to_chip(block, dh, dl)
        chip = chip_from(dh, dl)
        out = lax.dynamic_update_slice(out, came[None, None], (chip, core, 0, 0))
        other = swap(came, "core")
        out = lax.dynamic_update_slice(out, other[None, None], (chip, 1 - core, 0, 0))
    return out.reshape((2 * len(shifts),) + block.shape)


def scatter_ctx(parts):
    core = lax.axis_index("core")
    shifts = chip_shifts()
    parts = parts.reshape((len(shifts), 2) + parts.shape[1:])
    mine = lax.dynamic_index_in_dim(parts, core, 1, False)
    theirs = lax.dynamic_index_in_dim(parts, 1 - core, 1, False)
    pair = mine.astype(F32) + swap(theirs, "core").astype(F32)
    low = pair.astype(BF16)
    total = lax.dynamic_index_in_dim(pair, chip_to(0, 0), 0, False)
    for dh, dl in shifts[1:]:
        piece = lax.dynamic_index_in_dim(low, chip_to(dh, dl), 0, False)
        total = total + to_chip(piece, dh, dl).astype(F32)
    return total


def exchange(value, axes):
    return lax.all_to_all(value, axes, split_axis=0, concat_axis=0, tiled=True)


def norm_scale(value):
    return lax.rsqrt(jnp.mean(value * value, axis=-1, keepdims=True) + EPS)


def norm_backward(d_in, normed, scale, gain_vec):
    d_normed = d_in * gain_vec.astype(F32)
    d_gain = jnp.sum(d_in * normed, axis=0)
    d_resid = scale * (d_normed - normed * jnp.mean(d_normed * normed, axis=-1, keepdims=True))
    return (d_resid, d_gain)


def gelu_parts(gate_pre):
    gelu_val, pullback = jax.vjp(lambda v: jax.nn.gelu(v, approximate=True), gate_pre)
    return (gelu_val, pullback(jnp.ones_like(gate_pre))[0])


def per_device(
    tokens, cotangent, gain_attn, w_query, w_keyval, w_out, b_out, gain_ffn, w_gateup, w_down
):
    block_len, width = tokens.shape[1:]
    n_ctx = lax.axis_size("hi") * lax.axis_size("lo") * lax.axis_size("core")
    n_far, n_near = lax.axis_size("far"), lax.axis_size("near")
    n_seq = n_far * n_near
    n_all = n_ctx * n_seq
    n_group = n_ctx * n_far
    rows = w_query.shape[0]
    length = n_ctx * block_len
    q_scale = HD ** (-0.5)
    position = (lax.axis_index("hi") * lax.axis_size("lo") + lax.axis_index("lo")) * 2 + lax.axis_index("core")
    far, near = lax.axis_index("far"), lax.axis_index("near")
    q_cols = NH * HD // n_ctx
    kv_cols = 2 * HD // n_ctx
    share = FF // n_group

    block = tokens.reshape(block_len, width)
    d_final = cotangent.reshape(block_len, width)

    vectors = jnp.stack([gain_attn, b_out, gain_ffn])
    vectors = exchange(jnp.broadcast_to(vectors[None], (n_all, 3, rows)), EVERY)
    vectors = vectors.transpose(1, 0, 2).reshape(3, width)
    gain1, bias, gain2 = vectors[0], vectors[1], vectors[2]
    qkv_send = jnp.concatenate(
        [w_query.reshape(rows, n_ctx, q_cols), w_keyval.reshape(rows, n_ctx, kv_cols)], axis=2
    ).transpose(1, 0, 2)
    qkv_send = jnp.broadcast_to(qkv_send[:, None], (n_ctx, n_seq) + qkv_send.shape[1:])
    w_qkv = exchange(qkv_send.reshape((n_all,) + qkv_send.shape[2:]), EVERY)
    w_qkv = w_qkv.reshape(width, q_cols + kv_cols)
    full_tokens = gather_ctx(block).reshape(length, width).astype(F32)
    full_out = lax.all_gather(w_out, EVERY, axis=0, tiled=True)

    gateup_send = w_gateup.reshape(rows, 2, n_group, share).transpose(2, 0, 1, 3)
    own_half = exchange(gateup_send.reshape(n_group, rows, 2 * share), GROUP)
    other_half = swap(own_half, "near")
    w_gu = jnp.zeros((n_group, n_near, rows, 2 * share), BF16)
    w_gu = lax.dynamic_update_slice(w_gu, own_half[:, None], (0, near, 0, 0))
    w_gu = lax.dynamic_update_slice(w_gu, other_half[:, None], (0, 1 - near, 0, 0))
    w_gu = w_gu.reshape(width, 2 * share)
    w_dn = jnp.zeros((n_near,) + w_down.shape, BF16)
    w_dn = lax.dynamic_update_slice(w_dn, w_down[None], (near, 0, 0))
    w_dn = lax.dynamic_update_slice(w_dn, swap(w_down, "near")[None], (1 - near, 0, 0))
    w_dn = w_dn.reshape(share, width)

    full_scale = norm_scale(full_tokens)
    hidden1 = (full_tokens * full_scale * gain1.astype(F32)).astype(BF16)
    qkv = dot(hidden1, w_qkv)
    q_part = (qkv[:, :q_cols] * q_scale).astype(BF16)
    kv_part = qkv[:, q_cols:].astype(BF16)
    query = exchange(q_part.reshape(n_ctx, block_len, q_cols), CTX)
    query = query.transpose(1, 0, 2).reshape(block_len, NH, HD)
    keyval = exchange(jnp.broadcast_to(kv_part[None], (n_ctx, length, kv_cols)), CTX)
    keyval = keyval.transpose(1, 0, 2).reshape(length, 2 * HD)
    key, value = keyval[:, :HD], keyval[:, HD:]
    spacing = (position * block_len + jnp.arange(block_len, dtype=jnp.int32))[:, None] - jnp.arange(
        length, dtype=jnp.int32
    )[None, :]
    allowed = (spacing >= 0) & (spacing < WINDOW)
    scores = jnp.einsum("qhd,kd->hqk", query, key, preferred_element_type=F32)
    scores = jnp.where(allowed[None], scores, NEG)
    maximum = jnp.max(scores, axis=-1, keepdims=True)
    log_total = maximum + jnp.log(jnp.sum(jnp.exp(scores - maximum), axis=-1, keepdims=True))
    probs_low = jnp.exp(scores - log_total).astype(BF16)
    mixed = jnp.einsum("hqk,kd->qhd", probs_low, value, preferred_element_type=F32).astype(BF16)
    mixed = mixed.reshape(block_len, NH * HD)
    residual = block.astype(F32)
    middle = residual + dot(mixed, full_out) + bias.astype(F32)

    scale2 = norm_scale(middle)
    normed2 = middle * scale2
    hidden2 = (normed2 * gain2.astype(F32)).astype(BF16)

    def gather_group(mine):
        theirs = swap(mine, "far")
        return [gather_ctx(v).reshape(length, width) for v in (mine, theirs)]

    def scatter_group(pieces):
        mine, theirs = [
            scatter_ctx(p.astype(BF16).reshape(n_ctx, block_len, width)) for p in pieces
        ]
        return mine + swap(theirs.astype(BF16), "far").astype(F32)

    final_rows = gather_group(d_final)
    hidden_rows = gather_group(hidden2)
    outs, backs, inners, d_gus = [], [], [], []
    for hidden, final in zip(hidden_rows, final_rows):
        gateup = dot(hidden, w_gu)
        gate_pre, up_pre = gateup[:, :share], gateup[:, share:]
        gelu_val, gelu_slope = gelu_parts(gate_pre)
        inner = (gelu_val * up_pre).astype(BF16)
        d_inner = dot_last(final, w_dn)
        d_gu = jnp.concatenate(
            [d_inner * up_pre * gelu_slope, d_inner * gelu_val], axis=1
        ).astype(BF16)
        outs.append(dot(inner, w_dn))
        backs.append(dot_last(d_gu, w_gu))
        inners.append(inner)
        d_gus.append(d_gu)
    d_hidden2 = scatter_group(backs)
    output = (middle + scatter_group(outs)).astype(BF16)

    inner_rows, d_gu_rows = jnp.concatenate(inners), jnp.concatenate(d_gus)
    hidden_all, final_all = jnp.concatenate(hidden_rows), jnp.concatenate(final_rows)
    gu_grad = dot_first(hidden_all, d_gu_rows).astype(BF16)
    down_grad = dot_first(inner_rows, final_all).astype(BF16)
    quarter = width // n_seq
    gu_grad = gu_grad.reshape(n_far, n_near, quarter, 2 * share)
    theirs = lax.dynamic_index_in_dim(gu_grad, 1 - near, 1, False)
    mine = lax.dynamic_index_in_dim(gu_grad, near, 1, False)
    gu_sum = (mine.astype(F32) + swap(theirs, "near").astype(F32)).astype(BF16)
    count = n_ctx // 2
    odd = position % 2
    gateup_grad = jnp.zeros((quarter, 2, n_far, share), BF16)
    for flip in range(2):
        for step in range(n_far):
            to_far = (far + step) % n_far
            part = lax.dynamic_index_in_dim(gu_sum, to_far, 0, False)
            which = odd ^ flip
            part = jnp.where(which == 0, part[:, :share], part[:, share:])
            pairs = []
            for c in range(n_ctx):
                for f in range(n_far):
                    pairs.append((c * n_far + f, (((c % 2) ^ flip) * count + c // 2) * n_far + (f + step) % n_far))
            came = lax.ppermute(part, GROUP, pairs)
            side = (position // count) ^ flip
            source_far = (far - step) % n_far
            gateup_grad = lax.dynamic_update_slice(
                gateup_grad, came[:, None, None], (0, side, source_far, 0)
            )
    gateup_grad = gateup_grad.reshape(quarter, 2 * n_far * share).astype(F32)
    down_grad = down_grad.reshape(share, n_far, n_near, width // n_seq)
    theirs = lax.dynamic_index_in_dim(down_grad, 1 - near, 2, False)
    mine = lax.dynamic_index_in_dim(down_grad, near, 2, False)
    down_sum = (mine.astype(F32) + swap(theirs, "near").astype(F32)).astype(BF16)
    down_sum = exchange(down_sum.transpose(1, 0, 2), ("far",))
    down_grad = down_sum.reshape(n_far * share, width // n_seq).astype(F32)

    d_middle_norm, d_gain2 = norm_backward(d_hidden2, normed2, scale2, gain2)
    d_middle = d_final.astype(F32) + d_middle_norm
    d_bias = jnp.sum(d_middle, axis=0)
    d_low = d_middle.astype(BF16)
    d_mixed = dot_last(d_low, full_out).astype(BF16).reshape(block_len, NH, HD)
    scores = jnp.einsum("qhd,kd->hqk", query, key, preferred_element_type=F32)
    scores = jnp.where(allowed[None], scores, NEG)
    probs = jnp.exp(scores - log_total)
    probs_again = probs.astype(BF16)
    d_probs = jnp.einsum("qhd,kd->hqk", d_mixed, value, preferred_element_type=F32)
    delta = jnp.sum(probs * d_probs, axis=-1, keepdims=True)
    d_scores = (probs * (d_probs - delta)).astype(BF16)
    d_query = jnp.einsum("hqk,kd->qhd", d_scores, key, preferred_element_type=F32) * q_scale
    d_key = jnp.einsum("hqk,qhd->kd", d_scores, query, preferred_element_type=F32)
    d_value = jnp.einsum("hqk,qhd->kd", probs_again, d_mixed, preferred_element_type=F32)
    d_query = d_query.reshape(block_len, n_ctx, q_cols).astype(BF16).transpose(1, 0, 2)
    d_query = exchange(d_query, CTX).reshape(length, q_cols)
    d_keyval = jnp.concatenate([d_key, d_value], axis=1).astype(BF16)
    d_keyval = exchange(d_keyval.reshape(length, n_ctx, kv_cols).transpose(1, 0, 2), CTX)
    d_keyval = jnp.sum(d_keyval.astype(F32), axis=0).astype(BF16)
    d_qkv = jnp.concatenate([d_query, d_keyval], axis=1)
    d_hidden1 = scatter_ctx(dot_last(d_qkv, w_qkv).astype(BF16).reshape(n_ctx, block_len, width))
    scale1 = norm_scale(residual)
    d_input_norm, d_gain1 = norm_backward(d_hidden1, residual * scale1, scale1, gain1)
    d_input = d_middle + d_input_norm

    qkv_grad = lax.psum_scatter(
        dot_first(hidden1, d_qkv).astype(BF16), SEQ, scatter_dimension=0, tiled=True
    ).astype(F32)
    low_rows = gather_ctx(d_low).reshape(length, width)
    mixed_cols = exchange(mixed.reshape(block_len, n_ctx, q_cols).transpose(1, 0, 2), CTX)
    mixed_cols = mixed_cols.reshape(length, q_cols)
    out_grad = lax.psum_scatter(
        dot_first(mixed_cols, low_rows).astype(BF16), SEQ, scatter_dimension=1, tiled=True
    ).astype(F32)
    sums = jnp.stack([d_gain1, d_bias, d_gain2]).reshape(3, n_all, rows).transpose(1, 0, 2)
    sums = jnp.sum(exchange(sums, EVERY), axis=0)
    return (
        output.reshape(1, block_len, width),
        d_input.reshape(1, block_len, width),
        sums[0],
        qkv_grad[:, :q_cols],
        qkv_grad[:, q_cols:],
        out_grad,
        sums[1],
        sums[2],
        gateup_grad,
        down_grad,
    )


def solution(mesh):
    n_ctx, n_seq = mesh.shape["ctx"], mesh.shape["seq"]
    side = math.isqrt(n_ctx // 2)
    fine = Mesh(
        mesh.devices.reshape(n_ctx // 2 // side, side, 2, n_seq // 2, 2), EVERY
    )
    whole = P(EVERY)
    return jax.shard_map(
        per_device,
        mesh=fine,
        in_specs=(
            P(SEQ, CTX, None),
            P(SEQ, CTX, None),
            whole,
            whole,
            whole,
            whole,
            whole,
            whole,
            whole,
            whole,
        ),
        out_specs=(
            P(SEQ, CTX, None),
            P(SEQ, CTX, None),
            whole,
            P(SEQ, CTX),
            P(SEQ, CTX),
            P(CTX, SEQ),
            whole,
            whole,
            P(SEQ, CTX),
            P(CTX, SEQ),
        ),
        check_vma=False,
    )
```

time: 1490 us -> 945 us (0.63)
  waiting for transfers between devices: 1050 us -> 454 us
  local copies, waits for them, and re-layouts: 42.1 us -> 172 us
  matrix products: 214 us -> 120 us
  blocking collectives: 85.2 us -> 0 us
  starting transfers between devices: 52.5 us -> 109 us
  other arithmetic: 29.4 us -> 63.8 us
    all_gather x9 -> x1, waiting for transfers between devices: 740 us -> 0.01 us  [per_device(): full_out = lax.all_gather(w_out, EVERY, axis=0, tiled=True)]
    ppermute x10 -> x74, waiting for transfers between devices: 65 us -> 335 us  [the longest x33 151 us: to_chip(): return lax.ppermute(value, CHIP, pairs)]
    reduce_scatter x1, waiting for transfers between devices: 161 us -> 0.01 us  [per_device(): lax.psum_scatter(dot_first(hidden1, d_qkv).astype(BF16), SEQ, scatter_dim...]
    unnamed x2 -> x0, blocking collectives: 85.2 us -> none
    dynamic_update_slice x0 -> x54, local copies, waits for them, and re-layouts: none -> 54.5 us  [the longest x22 23.6 us: gather_ctx(): out = lax.dynamic_update_slice(out, came[None, None], (chip, core, 0, 0))]
    dot_general x11 -> x12, matrix products: 92.3 us -> 47.3 us  [the longest x6 30 us: dot(): return jnp.dot(left, right, preferred_element_type=F32)]
    dot_general x5 -> x6, matrix products: 80.3 us -> 38.8 us  [dot_last(): lax.dot_general(left, right, (((1,), (1,)), ((), ())), preferred_element_...]
    all_to_all x5 -> x10, waiting for transfers between devices: 77.7 us -> 118 us  [exchange(): return lax.all_to_all(value, axes, split_axis=0, concat_axis=0, tiled=True)]
  transfers between devices with their start and end apart: 29 -> 87, of which waited for: 19 -> 31; matrix products, arithmetic and copies ran while one was open for 19% -> 35% of each run, Pallas kernels for 0% -> 0%
where the time goes in v1:
time: 945 us; the launch traced here: 935 us
  waiting for transfers between devices  454 us (48%)
  local copies, waits for them, and re-layouts  172 us (18%)
  matrix products  120 us (13%)
  starting transfers between devices  109 us (12%)
  other arithmetic  63.8 us (7%)
  between operations  15.6 us (2%)
    ppermute x33, waiting for transfers between devices, to_chip(): return lax.ppermute(value, CHIP, pairs)  151 us
    ppermute x37, waiting for transfers between devices, swap(): lax.ppermute(value, axis, [(i, (i + 1) % count) for i in range(count)])  150 us
    all_to_all x10, waiting for transfers between devices, exchange(): return lax.all_to_all(value, axes, split_axis=0, concat_axis=0, tiled=True)  118 us
    ppermute x33, starting transfers between devices, to_chip(): return lax.ppermute(value, CHIP, pairs)  45.3 us
    all_to_all x10, starting transfers between devices, exchange(): return lax.all_to_all(value, axes, split_axis=0, concat_axis=0, tiled=True)  42.9 us
    dot_general x6, matrix products, dot_last(): lax.dot_general(left, right, (((1,), (1,)), ((), ())), preferred_element_...  38.8 us
    ppermute x4, waiting for transfers between devices, per_device(): came = lax.ppermute(part, GROUP, pairs)  34.2 us
    dot_general x4, matrix products, dot_first(): lax.dot_general(left, right, (((0,), (0,)), ((), ())), preferred_element_...  33.8 us
  transfers between devices with their start and end apart: 87, of which 31 were waited for; matrix products, arithmetic and copies ran while one was open for 35% of the time, Pallas kernels for 0%

profile of v1, /device:TPU:0, one launch (start us, length us, event | category | flops | bytes accessed | tf_op | source)
XLA Modules:
  0.0 935.2 jit_solution(7096816136542933556)
XLA Ops:
  13.9 6.3 all-to-all-start
  69.1 31.4 %collective-permute-done.34 = bf16[128,2560]{1,0:T(8,128)(2,1)S(1)} collective-permute-done((bf16[128,2560]{1,0:T(8,128)(2,1)S(1)}, bf16[128,2560]{1,0:T(8,128)(2,1)S(1)}, u32[]{:S(2)}, u32[]{:S(2)}) %collective-permute-start.34) | collective-permute-done | bytes 655392 | tf_op jit(solution)/shard_map/ppermute | solution.py:56
  102.5 76.8 %collective-permute-done.44 = bf16[128,2560]{1,0:T(8,128)(2,1)} collective-permute-done((bf16[128,2560]{1,0:T(8,128)(2,1)S(1)}, bf16[128,2560]{1,0:T(8,128)(2,1)}, u32[]{:S(2)}, u32[]{:S(2)}) %collective-permute-start.44) | collective-permute-done | bytes 655392 | tf_op jit(solution)/shard_map/ppermute | solution.py:40
  217.7 6.7 all-to-all-done.3
  231.8 8.8 collective-permute-done.50
  251.2 39.1 %all-to-all-done.4 = bf16[16,80,960]{2,1,0:T(8,128)(2,1)S(1)} async-done(((bf16[16,80,960]{2,1,0:T(8,128)(2,1)}), bf16[16,80,960]{2,1,0:T(8,128)(2,1)S(1)}, u32[]{:S(2)}, u32[]{:S(2)}) %all-to-all-start.4) | async-done | bytes 2457632 | tf_op jit(solution)/shard_map/all_to_all | solution.py:100
  300.1 11.0 %all-to-all-done.2 = bf16[8,1024,64]{1,2,0:T(8,128)(2,1)} async-done(((bf16[8,1024,64]{1,2,0:T(8,128)(2,1)}), bf16[8,1024,64]{1,2,0:T(8,128)(2,1)}, u32[]{:S(2)}, u32[]{:S(2)}) %all-to-all-start.2) | async-done | bytes 1048608 | tf_op jit(solution)/shard_map/all_to_all | solution.py:100
  318.7 7.0 multiply_reduce_fusion.3
  328.3 45.0 %collective-permute-done.14 = bf16[16,80,960]{2,1,0:T(8,128)(2,1)} collective-permute-done((bf16[16,80,960]{2,1,0:T(8,128)(2,1)S(1)}, bf16[16,80,960]{2,1,0:T(8,128)(2,1)}, u32[]{:S(2)}, u32[]{:S(2)}) %collective-permute-start.14) | collective-permute-done | bytes 2457632 | tf_op jit(solution)/shard_map/ppermute | solution.py:40
  379.9 25.9 %collective-permute-done.10 = bf16[128,2560]{1,0:T(8,128)(2,1)S(1)} collective-permute-done((bf16[128,2560]{1,0:T(8,128)(2,1)S(1)}, bf16[128,2560]{1,0:T(8,128)(2,1)S(1)}, u32[]{:S(2)}, u32[]{:S(2)}) %collective-permute-start.10) | collective-permute-done | bytes 655392 | tf_op jit(solution)/shard_map/ppermute | solution.py:56
  417.0 6.4 fusion.42
  429.6 6.4 convolution_convert_fusion.4
  457.1 8.2 fusion.18
  470.7 6.6 constant_dynamic-slice_fusion.1
  477.6 14.5 %fusion.10 = bf16[2560,960]{0,1:T(8,128)(2,1)} fusion(bf16[1024,2560]{1,0:T(8,128)(2,1)} %bitcast.506, bf16[1024,2560]{1,0:T(8,128)(2,1)} %bitcast.494, bf16[1024,480]{0,1:T(8,128)(2,1)S(1)} %copy-done.66, bf16[1024,480]{0,1:T(8,128)(2,1)S(1)} %copy-done.64, bf16[1024,480]{0,1:T(8,128)(2,1)S(1)} %copy-done.63, bf16[1024,480]{0,1:T(8,128)(2,1)S(1)} %copy-done.61), kind=kOutput, calls=%fused_computation.18 | convolution fusion | flops 10105487360 | bytes 19333120 | tf_op jit(solution)/shard_map/dot_general | solution.py:35
  492.1 11.0 %reshape.257 = bf16[2,2,640,960]{2,1,0,3:T(2,128)(2,1)} reshape(bf16[2560,960]{0,1:T(8,128)(2,1)} %fusion.10) | data formatting | bytes 9830400 | tf_op jit(solution)/shard_map/reshape | solution.py:227
  503.1 11.9 %constant_dynamic-slice_fusion.3 = (bf16[2,1,640,960]{2,1,0,3:T(2,128)(2,1)S(1)}, bf16[2,1,640,960]{2,1,0,3:T(2,128)(2,1)S(1)}) fusion(bf16[2,2,640,960]{2,1,0,3:T(2,128)(2,1)} %reshape.257, s32[]{:T(128)S(6)} %select_n.446, s32[]{:T(128)S(6)} %select_n.447), kind=kLoop, calls=%fused_computation.249 | loop fusion | bytes 9830408 | tf_op jit(solution)/shard_map/jit(dynamic_index_in_dim)/dynamic_slice | solution.py:229
  518.8 6.0 convolution_convert_fusion.3
  554.4 7.7 collective-permute-done.29
  563.6 13.7 %collective-permute-done.30 = bf16[128,2560]{1,0:T(8,128)(2,1)} collective-permute-done((bf16[128,2560]{1,0:T(8,128)(2,1)}, bf16[128,2560]{1,0:T(8,128)(2,1)}, u32[]{:S(2)}, u32[]{:S(2)}) %collective-permute-start.30) | collective-permute-done | bytes 655392 | tf_op jit(solution)/shard_map/ppermute | solution.py:56
  581.3 8.9 collective-permute-done.53
  591.7 13.5 %collective-permute-done.54 = bf16[128,2560]{1,0:T(8,128)(2,1)S(1)} collective-permute-done((bf16[128,2560]{1,0:T(8,128)(2,1)S(1)}, bf16[128,2560]{1,0:T(8,128)(2,1)S(1)}, u32[]{:S(2)}, u32[]{:S(2)}) %collective-permute-start.54) | collective-permute-done | bytes 655392 | tf_op jit(solution)/shard_map/ppermute | solution.py:56
  609.1 9.2 collective-permute-done.17
  619.8 17.1 %collective-permute-done.18 = bf16[128,2560]{1,0:T(8,128)(2,1)S(1)} collective-permute-done((bf16[128,2560]{1,0:T(8,128)(2,1)S(1)}, bf16[128,2560]{1,0:T(8,128)(2,1)S(1)}, u32[]{:S(2)}, u32[]{:S(2)}) %collective-permute-start.18) | collective-permute-done | bytes 655392 | tf_op jit(solution)/shard_map/ppermute | solution.py:56
  646.5 14.4 %collective-permute-done.42 = bf16[128,2560]{1,0:T(8,128)(2,1)S(1)} collective-permute-done((bf16[128,2560]{1,0:T(8,128)(2,1)}, bf16[128,2560]{1,0:T(8,128)(2,1)S(1)}, u32[]{:S(2)}, u32[]{:S(2)}) %collective-permute-start.42) | collective-permute-done | bytes 655392 | tf_op jit(solution)/shard_map/ppermute | solution.py:56
  660.9 9.0 collective-permute-done.32
  669.9 7.7 collective-permute-done.56
  687.2 10.1 %convolution_convert_fusion.7 = bf16[128,2560]{1,0:T(8,128)(2,1)} fusion(bf16[128,2560]{1,0:T(8,128)(2,1)} %get-tuple-element.58, bf16[2560,2560]{1,0:T(8,128)(2,1)} %all-gather.2.cloned.1.call-done), kind=kOutput, calls=%fused_computation.47 | convolution fusion | flops 1678049280 | bytes 14417920 | tf_op jit(solution)/shard_map/dot_general | solution.py:31
  734.8 8.4 all-to-all-done.6
  783.3 6.0 fusion.9
  797.2 46.7 %all-to-all-done.9 = bf16[2,480,640]{2,1,0:T(8,128)(2,1)S(1)} async-done(((bf16[2,480,640]{2,1,0:T(8,128)(2,1)}), bf16[2,480,640]{2,1,0:T(8,128)(2,1)S(1)}, u32[]{:S(2)}, u32[]{:S(2)}) %all-to-all-start.9) | async-done | bytes 1228832 | tf_op jit(solution)/shard_map/all_to_all | solution.py:100
  867.4 34.1 %collective-permute-done.72 = bf16[640,480]{0,1:T(8,128)(2,1)} collective-permute-done((bf16[640,480]{0,1:T(8,128)(2,1)}, bf16[640,480]{0,1:T(8,128)(2,1)}, u32[]{:S(2)}, u32[]{:S(2)}) %collective-permute-start.72) | collective-permute-done | bytes 614432 | tf_op jit(solution)/shard_map/ppermute | solution.py:244
  (484 shorter events, 383.9 us)
Async XLA Ops:
  7.2 311.5 %all-gather.2.cloned.1.call-start = ((), (), s32[]{:S(2)}) async-start(), calls=%async_computation.12 | async-start | bytes 13516800 | tf_op jit(solution)/shard_map/all_gather | solution.py:151
  7.9 50.4 %collective-permute-start = (bf16[128,2560]{1,0:T(8,128)(2,1)}, bf16[128,2560]{1,0:T(8,128)(2,1)}, u32[]{:S(2)}, u32[]{:S(2)}) collective-permute-start(bf16[128,2560]{1,0:T(8,128)(2,1)} %bitcast.471), channel_id=1, source_target_pairs={{0,4},{4,0},{1,5},{5,1},{2,6},{6,2},{3,7},{7,3},{8,12},{12,8},{9,1... | collective-permute-start | bytes 1966088 | tf_op jit(solution)/shard_map/ppermute | solution.py:40
  8.4 57.2 %collective-permute-start.1 = (bf16[128,2560]{1,0:T(8,128)(2,1)}, bf16[128,2560]{1,0:T(8,128)(2,1)}, u32[]{:S(2)}, u32[]{:S(2)}) collective-permute-start(bf16[128,2560]{1,0:T(8,128)(2,1)} %bitcast.472), channel_id=1, source_target_pairs={{0,8},{8,0},{16,24},{24,16},{1,9},{9,1},{17,25},{25,17},{2,10},{10... | collective-permute-start | bytes 1966088 | tf_op jit(solution)/shard_map/ppermute | solution.py:56
  11.0 172.9 %collective-permute-start.3 = (bf16[128,2560]{1,0:T(8,128)(2,1)}, bf16[128,2560]{1,0:T(8,128)(2,1)}, u32[]{:S(2)}, u32[]{:S(2)}) collective-permute-start(bf16[128,2560]{1,0:T(8,128)(2,1)} %bitcast.473), channel_id=1, source_target_pairs={{0,16},{8,24},{16,0},{24,8},{1,17},{9,25},{17,1},{25,9},{2,18},{10... | collective-permute-start | bytes 1966088 | tf_op jit(solution)/shard_map/ppermute | solution.py:56
  12.5 174.9 %collective-permute-start.5 = (bf16[128,2560]{1,0:T(8,128)(2,1)}, bf16[128,2560]{1,0:T(8,128)(2,1)}, u32[]{:S(2)}, u32[]{:S(2)}) collective-permute-start(bf16[128,2560]{1,0:T(8,128)(2,1)} %bitcast.474), channel_id=1, source_target_pairs={{0,24},{8,16},{16,8},{24,0},{1,25},{9,17},{17,9},{25,1},{2,26},{10... | collective-permute-start | bytes 1966088 | tf_op jit(solution)/shard_map/ppermute | solution.py:56
  51.4 150.4 %all-to-all-start.1 = ((bf16[32,80,384]{2,1,0:T(8,128)(2,1)}), bf16[32,80,384]{2,1,0:T(8,128)(2,1)S(1)}, u32[]{:S(2)}, u32[]{:S(2)}) async-start(bf16[32,80,384]{2,1,0:T(8,128)(2,1)} %bitcast.15), calls=%async_computation.1 | async-start | bytes 3932160 | tf_op jit(solution)/shard_map/all_to_all | solution.py:100
  62.2 131.5 %collective-permute-start.36 = (bf16[128,2560]{1,0:T(8,128)(2,1)S(1)}, bf16[128,2560]{1,0:T(8,128)(2,1)}, u32[]{:S(2)}, u32[]{:S(2)}) collective-permute-start(bf16[128,2560]{1,0:T(8,128)(2,1)S(1)} %bitcast.511), channel_id=1, source_target_pairs={{0,16},{8,24},{16,0},{24,8},{1,17},{9,25},{17,1},{25,9},{2,18},{10... | collective-permute-start | bytes 1966088 | tf_op jit(solution)/shard_map/ppermute | solution.py:56
  65.7 118.0 %collective-permute-start.15 = (bf16[240,2560]{1,0:T(8,128)(2,1)}, bf16[240,2560]{1,0:T(8,128)(2,1)S(1)}, u32[]{:S(2)}, u32[]{:S(2)}) collective-permute-start(bf16[240,2560]{1,0:T(8,128)(2,1)} %param.19), channel_id=1, source_target_pairs={{0,1},{1,0},{2,3},{3,2},{4,5},{5,4},{6,7},{7,6},{8,9},{9,8},{10,11... | collective-permute-start | bytes 3686408 | tf_op jit(solution)/shard_map/ppermute | solution.py:40
  100.5 78.8 %collective-permute-start.44 = (bf16[128,2560]{1,0:T(8,128)(2,1)S(1)}, bf16[128,2560]{1,0:T(8,128)(2,1)}, u32[]{:S(2)}, u32[]{:S(2)}) collective-permute-start(bf16[128,2560]{1,0:T(8,128)(2,1)S(1)} %bitcast.512), channel_id=1, source_target_pairs={{0,2},{2,0},{1,3},{3,1},{4,6},{6,4},{5,7},{7,5},{8,10},{10,8},{9,1... | collective-permute-start | bytes 1966088 | tf_op jit(solution)/shard_map/ppermute | solution.py:40
  187.4 53.1 %collective-permute-start.45 = (bf16[128,2560]{1,0:T(8,128)(2,1)}, bf16[128,2560]{1,0:T(8,128)(2,1)}, u32[]{:S(2)}, u32[]{:S(2)}) collective-permute-start(bf16[128,2560]{1,0:T(8,128)(2,1)} %collective-permute-done.44), channel_id=1, source_target_pairs={{0,4},{4,0},{1,5},{5,1},{2,6},{6,2},{3,7},{7,3},{8,12},{12,8},{9,1... | collective-permute-start | bytes 1966088 | tf_op jit(solution)/shard_map/ppermute | solution.py:40
  225.3 65.0 %all-to-all-start.4 = ((bf16[16,80,960]{2,1,0:T(8,128)(2,1)}), bf16[16,80,960]{2,1,0:T(8,128)(2,1)S(1)}, u32[]{:S(2)}, u32[]{:S(2)}) async-start(bf16[16,80,960]{2,1,0:T(8,128)(2,1)} %reshape.248), calls=%async_computation.4 | async-start | bytes 5242880 | tf_op jit(solution)/shard_map/all_to_all | solution.py:100
  240.5 57.6 %collective-permute-start.51 = (bf16[128,2560]{1,0:T(8,128)(2,1)}, bf16[128,2560]{1,0:T(8,128)(2,1)}, u32[]{:S(2)}, u32[]{:S(2)}) collective-permute-start(bf16[128,2560]{1,0:T(8,128)(2,1)} %collective-permute-done.50), channel_id=1, source_target_pairs={{0,4},{4,0},{1,5},{5,1},{2,6},{6,2},{3,7},{7,3},{8,12},{12,8},{9,1... | collective-permute-start | bytes 1966088 | tf_op jit(solution)/shard_map/ppermute | solution.py:40
  300.1 73.3 %collective-permute-start.14 = (bf16[16,80,960]{2,1,0:T(8,128)(2,1)S(1)}, bf16[16,80,960]{2,1,0:T(8,128)(2,1)}, u32[]{:S(2)}, u32[]{:S(2)}) collective-permute-start(bf16[16,80,960]{2,1,0:T(8,128)(2,1)S(1)} %all-to-all-done.4), channel_id=1, source_target_pairs={{0,1},{1,0},{2,3},{3,2},{4,5},{5,4},{6,7},{7,6},{8,9},{9,8},{10,11... | collective-permute-start | bytes 7372808 | tf_op jit(solution)/shard_map/ppermute | solution.py:40
  326.7 52.0 %collective-permute-start.7 = (bf16[128,2560]{1,0:T(8,128)(2,1)S(1)}, bf16[128,2560]{1,0:T(8,128)(2,1)S(1)}, u32[]{:S(2)}, u32[]{:S(2)}) collective-permute-start(bf16[128,2560]{1,0:T(8,128)(2,1)S(1)} %get-tuple-element.71), channel_id=1, source_target_pairs={{0,4},{4,0},{1,5},{5,1},{2,6},{6,2},{3,7},{7,3},{8,12},{12,8},{9,1... | collective-permute-start | bytes 1966088 | tf_op jit(solution)/shard_map/ppermute | solution.py:40
  326.7 52.4 %collective-permute-start.8 = (bf16[128,2560]{1,0:T(8,128)(2,1)S(1)}, bf16[128,2560]{1,0:T(8,128)(2,1)S(1)}, u32[]{:S(2)}, u32[]{:S(2)}) collective-permute-start(bf16[128,2560]{1,0:T(8,128)(2,1)S(1)} %get-tuple-element.71), channel_id=1, source_target_pairs={{0,8},{8,0},{16,24},{24,16},{1,9},{9,1},{17,25},{25,17},{2,10},{10... | collective-permute-start | bytes 1966088 | tf_op jit(solution)/shard_map/ppermute | solution.py:56
  327.3 51.4 %collective-permute-start.20 = (bf16[128,2560]{1,0:T(8,128)(2,1)S(1)}, bf16[128,2560]{1,0:T(8,128)(2,1)S(1)}, u32[]{:S(2)}, u32[]{:S(2)}) collective-permute-start(bf16[128,2560]{1,0:T(8,128)(2,1)S(1)} %get-tuple-element.71), channel_id=1, source_target_pairs={{0,2},{2,0},{1,3},{3,1},{4,6},{6,4},{5,7},{7,5},{8,10},{10,8},{9,1... | collective-permute-start | bytes 1966088 | tf_op jit(solution)/shard_map/ppermute | solution.py:40
  378.6 59.2 %collective-permute-start.21 = (bf16[128,2560]{1,0:T(8,128)(2,1)S(1)}, bf16[128,2560]{1,0:T(8,128)(2,1)S(1)}, u32[]{:S(2)}, u32[]{:S(2)}) collective-permute-start(bf16[128,2560]{1,0:T(8,128)(2,1)S(1)} %collective-permute-done.20), channel_id=1, source_target_pairs={{0,4},{4,0},{1,5},{5,1},{2,6},{6,2},{3,7},{7,3},{8,12},{12,8},{9,1... | collective-permute-start | bytes 1966088 | tf_op jit(solution)/shard_map/ppermute | solution.py:40
  378.7 59.3 %collective-permute-start.22 = (bf16[128,2560]{1,0:T(8,128)(2,1)S(1)}, bf16[128,2560]{1,0:T(8,128)(2,1)S(1)}, u32[]{:S(2)}, u32[]{:S(2)}) collective-permute-start(bf16[128,2560]{1,0:T(8,128)(2,1)S(1)} %collective-permute-done.20), channel_id=1, source_target_pairs={{0,8},{8,0},{16,24},{24,16},{1,9},{9,1},{17,25},{25,17},{2,10},{10... | collective-permute-start | bytes 1966088 | tf_op jit(solution)/shard_map/ppermute | solution.py:56
  428.4 103.9 %collective-permute-start.16 = (bf16[4,128,2560]{2,1,0:T(8,128)(2,1)}, bf16[4,128,2560]{2,1,0:T(8,128)(2,1)}, u32[]{:S(2)}, u32[]{:S(2)}) collective-permute-start(bf16[4,128,2560]{2,1,0:T(8,128)(2,1)} %dynamic-slice_bitcast_fusion.4), channel_id=1, source_target_pairs={{0,4},{4,0},{1,5},{5,1},{2,6},{6,2},{3,7},{7,3},{8,12},{12,8},{9,1... | collective-permute-start | bytes 7864328 | tf_op jit(solution)/shard_map/ppermute | solution.py:40
  437.9 97.6 %collective-permute-start.40 = (bf16[4,128,2560]{2,1,0:T(8,128)(2,1)}, bf16[4,128,2560]{2,1,0:T(8,128)(2,1)}, u32[]{:S(2)}, u32[]{:S(2)}) collective-permute-start(bf16[4,128,2560]{2,1,0:T(8,128)(2,1)} %dynamic-slice_bitcast_fusion.2), channel_id=1, source_target_pairs={{0,4},{4,0},{1,5},{5,1},{2,6},{6,2},{3,7},{7,3},{8,12},{12,8},{9,1... | collective-permute-start | bytes 7864328 | tf_op jit(solution)/shard_map/ppermute | solution.py:40
  477.5 129.5 %collective-permute-start.73 = (bf16[480,2,640]{2,0,1:T(8,128)(2,1)S(1)}, bf16[480,2,640]{2,0,1:T(8,128)(2,1)}, u32[]{:S(2)}, u32[]{:S(2)}) collective-permute-start(bf16[480,2,640]{2,0,1:T(8,128)(2,1)S(1)} %bitcast.520), channel_id=1, source_target_pairs={{0,1},{1,0},{2,3},{3,2},{4,5},{5,4},{6,7},{7,6},{8,9},{9,8},{10,11... | collective-permute-start | bytes 3686408 | tf_op jit(solution)/shard_map/ppermute | solution.py:40
  516.8 92.3 %collective-permute-start.68 = (bf16[2,640,960]{1,2,0:T(8,128)(2,1)}, bf16[2,640,960]{1,2,0:T(8,128)(2,1)}, u32[]{:S(2)}, u32[]{:S(2)}) collective-permute-start(bf16[2,640,960]{1,2,0:T(8,128)(2,1)} %bitcast.465), channel_id=1, source_target_pairs={{0,1},{1,0},{2,3},{3,2},{4,5},{5,4},{6,7},{7,6},{8,9},{9,8},{10,11... | collective-permute-start | bytes 7372808 | tf_op jit(solution)/shard_map/ppermute | solution.py:40
  609.1 51.8 %collective-permute-start.42 = (bf16[128,2560]{1,0:T(8,128)(2,1)}, bf16[128,2560]{1,0:T(8,128)(2,1)S(1)}, u32[]{:S(2)}, u32[]{:S(2)}) collective-permute-start(bf16[128,2560]{1,0:T(8,128)(2,1)} %get-tuple-element.87), channel_id=1, source_target_pairs={{0,16},{8,24},{16,0},{24,8},{1,17},{9,25},{17,1},{25,9},{2,18},{10... | collective-permute-start | bytes 1966088 | tf_op jit(solution)/shard_map/ppermute | solution.py:56
  683.2 47.7 %collective-permute-start.61 = (bf16[128,2560]{1,0:T(8,128)(2,1)}, bf16[128,2560]{1,0:T(8,128)(2,1)}, u32[]{:S(2)}, u32[]{:S(2)}) collective-permute-start(bf16[128,2560]{1,0:T(8,128)(2,1)} %get-tuple-element.58), channel_id=1, source_target_pairs={{0,4},{4,0},{1,5},{5,1},{2,6},{6,2},{3,7},{7,3},{8,12},{12,8},{9,1... | collective-permute-start | bytes 1966088 | tf_op jit(solution)/shard_map/ppermute | solution.py:40
  758.7 85.2 %all-to-all-start.9 = ((bf16[2,480,640]{2,1,0:T(8,128)(2,1)}), bf16[2,480,640]{2,1,0:T(8,128)(2,1)S(1)}, u32[]{:S(2)}, u32[]{:S(2)}) async-start(bf16[2,480,640]{2,1,0:T(8,128)(2,1)} %fusion.100), calls=%async_computation.10 | async-start | bytes 2457600 | tf_op jit(solution)/shard_map/all_to_all | solution.py:100
  762.3 160.6 %reduce-scatter.7.cloned.1.call-start = ((), (), s32[]{:S(2)}) async-start(), calls=%async_computation.14 | async-start | bytes 2457600
  771.9 153.2 %reduce-scatter.5.cloned.1.call-start = ((), (), s32[]{:S(2)}) async-start(), calls=%async_computation.13 | async-start | bytes 2457600 | tf_op jit(solution)/shard_map/reduce_scatter | solution.py:284
  780.6 72.3 %collective-permute-start.57 = (bf16[4,128,2560]{2,1,0:T(8,128)(2,1)}, bf16[4,128,2560]{2,1,0:T(8,128)(2,1)}, u32[]{:S(2)}, u32[]{:S(2)}) collective-permute-start(bf16[4,128,2560]{2,1,0:T(8,128)(2,1)} %dynamic-slice_bitcast_fusion), channel_id=1, source_target_pairs={{0,4},{4,0},{1,5},{5,1},{2,6},{6,2},{3,7},{7,3},{8,12},{12,8},{9,1... | collective-permute-start | bytes 7864328 | tf_op jit(solution)/shard_map/ppermute | solution.py:40
  781.6 64.0 %collective-permute-start.69 = (bf16[640,480]{0,1:T(8,128)(2,1)S(1)}, bf16[640,480]{0,1:T(8,128)(2,1)}, u32[]{:S(2)}, u32[]{:S(2)}) collective-permute-start(bf16[640,480]{0,1:T(8,128)(2,1)S(1)} %get-tuple-element.107), channel_id=1, source_target_pairs={{0,0},{2,2},{4,16},{6,18},{8,4},{10,6},{12,20},{14,22},{16,8},{18,... | collective-permute-start | bytes 1843208 | tf_op jit(solution)/shard_map/ppermute | solution.py:244
  790.4 73.0 %collective-permute-start.70 = (bf16[640,480]{0,1:T(8,128)(2,1)}, bf16[640,480]{0,1:T(8,128)(2,1)}, u32[]{:S(2)}, u32[]{:S(2)}) collective-permute-start(bf16[640,480]{0,1:T(8,128)(2,1)} %get-tuple-element.105), channel_id=1, source_target_pairs={{0,2},{2,0},{4,18},{6,16},{8,6},{10,4},{12,22},{14,20},{16,10},{18... | collective-permute-start | bytes 1843208 | tf_op jit(solution)/shard_map/ppermute | solution.py:244
  793.3 72.9 %collective-permute-start.71 = (bf16[640,480]{0,1:T(8,128)(2,1)}, bf16[640,480]{0,1:T(8,128)(2,1)}, u32[]{:S(2)}, u32[]{:S(2)}) collective-permute-start(bf16[640,480]{0,1:T(8,128)(2,1)} %get-tuple-element.106), channel_id=1, source_target_pairs={{0,16},{2,18},{4,0},{6,2},{8,20},{10,22},{12,4},{14,6},{16,24},{18... | collective-permute-start | bytes 1843208 | tf_op jit(solution)/shard_map/ppermute | solution.py:244
  796.8 104.7 %collective-permute-start.72 = (bf16[640,480]{0,1:T(8,128)(2,1)}, bf16[640,480]{0,1:T(8,128)(2,1)}, u32[]{:S(2)}, u32[]{:S(2)}) collective-permute-start(bf16[640,480]{0,1:T(8,128)(2,1)} %get-tuple-element.104), channel_id=1, source_target_pairs={{0,18},{2,16},{4,2},{6,0},{8,22},{10,20},{12,6},{14,4},{16,26},{18... | collective-permute-start | bytes 1843208 | tf_op jit(solution)/shard_map/ppermute | solution.py:244
  (135 other events, 3180.8 us)
Sparse Core Ops, SparseCore 0:
  10.9 173.9 all-gather.1
  772.0 77.5 reduce-scatter.6
  853.0 55.1 reduce-scatter.4

commit v2 on v1

v2 whole, which is shorter than its diff:
```python
import functools
import math

import jax
import jax.numpy as jnp
from jax import lax
from jax.experimental import pallas as pl
from jax.experimental.pallas import tpu as pltpu
from jax.sharding import Mesh, PartitionSpec as P

NH = 10
HD = 256
FF = 7680
WINDOW = 2048

EPS = 1e-06
NEG = -1e30

F32 = jnp.float32
BF16 = jnp.bfloat16

CTX = ("hi", "lo", "core")
GROUP = ("hi", "lo", "core", "far")
SEQ = ("far", "near")
EVERY = ("hi", "lo", "core", "far", "near")


def dot(left, right):
    return jnp.dot(left, right, preferred_element_type=F32)


def dot_last(left, right):
    return lax.dot_general(left, right, (((1,), (1,)), ((), ())), preferred_element_type=F32)


def dot_first(left, right):
    return lax.dot_general(left, right, (((0,), (0,)), ((), ())), preferred_element_type=F32)


def send(value, axis, step):
    count = lax.axis_size(axis)
    return lax.ppermute(value, axis, [(i, (i + step) % count) for i in range(count)])


def meet(*values):
    return lax.optimization_barrier(values)


def side():
    return lax.axis_size("lo")


def send_cross(value, step, second):
    k = side()
    pairs = []
    for h in range(k):
        for l in range(k):
            for c in range(2):
                along_lo = (c == 0) != second
                to_h, to_l = (h, (l + step) % k) if along_lo else ((h + step) % k, l)
                pairs.append(((h * k + l) * 2 + c, (to_h * k + to_l) * 2 + c))
    return lax.ppermute(value, CTX, pairs)


def gather_0(block):
    return jnp.concatenate([block, send(block, "core", 1)])


def gather_1(pair):
    return [send_cross(pair, i, False) for i in range(1, side())]


def gather_2(sides):
    rows = sides[0].shape[0] // 2
    return [send_cross(value[:rows], j, True) for value in sides for j in range(1, side())]


def gather_3(pair, sides, corners):
    own = jnp.concatenate(sides + corners)
    return own, send(own, "core", 1)


def gather_all(pair, halves):
    rows = pair.shape[0] // 2
    return jnp.concatenate([pair[:rows], halves[0], pair[rows:], halves[1]])


def add(*values):
    return sum((value.astype(F32) for value in values[1:]), values[0].astype(F32))


def block_of(value, at, rows):
    k = side()
    value = value.reshape(-1, k * k, rows, value.shape[-1])[:, at]
    return value.reshape(-1, value.shape[-1])


def scatter_1(keep, came, rows):
    k = side()
    back = []
    for i in range(k - 1):
        for j in range(1, k):
            at = 2 * k - 1 + i * (k - 1) + j - 1
            low = add(block_of(keep, at, rows), block_of(came, at, rows)).astype(BF16)
            back.append(send_cross(low, -j, True))
    return back


def scatter_2(keep, came, back, rows):
    k = side()
    sides = []
    for i in range(1, k):
        first = add(block_of(keep, 2 * i - 1, rows), block_of(came, 2 * i - 1, rows))
        first = add(first, *back[(i - 1) * (k - 1) : i * (k - 1)])
        second = add(block_of(keep, 2 * i, rows), block_of(came, 2 * i, rows))
        sides.append(send_cross(jnp.concatenate([first, second]).astype(BF16), -i, False))
    return sides


def scatter_3(sides):
    half = sides[0].shape[0] // 2
    return send(add(*[value[half:] for value in sides]).astype(BF16), "core", 1)


def scatter_4(keep, came, sides, other, rows):
    half = sides[0].shape[0] // 2
    return add(
        block_of(keep, 0, rows), block_of(came, 0, rows), other, *[value[:half] for value in sides]
    )


def copy_blocks(order_ref, from_ref, to_ref):
    for n in range(to_ref.shape[0]):
        to_ref[n] = from_ref[order_ref[n]]


def pick_blocks(blocks, order):
    shape = order.shape + blocks.shape[1:]
    return pl.pallas_call(
        copy_blocks,
        out_shape=jax.ShapeDtypeStruct(shape, blocks.dtype),
        in_specs=[pl.BlockSpec(memory_space=pltpu.SMEM), pl.BlockSpec(memory_space=pltpu.VMEM)],
        out_specs=pl.BlockSpec(memory_space=pltpu.VMEM),
        cost_estimate=pl.CostEstimate(
            flops=0, bytes_accessed=2 * blocks.size * blocks.dtype.itemsize, transcendentals=0
        ),
        name="pick_blocks",
    )(order, blocks)


def order_ctx(by_device):
    k = side()
    h, l, c = (lax.axis_index(axis) for axis in CTX)
    picked = []
    for n in range(2 * k * k):
        if by_device:
            ih, il, ic = n // (2 * k), n // 2 % k, n % 2
            dh, dl = (h - ih) % k, (l - il) % k
            on_lo, on_hi = (dh == 0) & (dl != 0), (dl == 0) & (dh != 0)
            charge = jnp.where(on_lo, 0, jnp.where(on_hi, 1, ic))
            i, j = (dl, dh) if ic == 0 else (dh, dl)
            at = 2 * k - 1 + (i - 1) * (k - 1) + j - 1
            at = jnp.where(on_lo, 2 * dl - 1 + (ic != 0), jnp.where(on_hi, 2 * dh - 1 + (ic != 1), at))
            at = jnp.where((dh == 0) & (dl == 0), 0, at)
            source = jnp.where(charge == c, 0, k * k) + at
        else:
            other, at = n // (k * k), n % (k * k)
            charge = c ^ other
            if at == 0:
                i, j, core = 0, 0, charge
            elif at < 2 * k - 1:
                i, j, core = (at + 1) // 2, 0, charge ^ ((at + 1) % 2)
            else:
                i, j, core = (at - 2 * k + 1) // (k - 1) + 1, (at - 2 * k + 1) % (k - 1) + 1, charge
            dh, dl = jnp.where(charge == 0, j, i), jnp.where(charge == 0, i, j)
            source = ((h - dh) % k * k + (l - dl) % k) * 2 + core
        picked.append(source)
    return jnp.stack(picked).astype(jnp.int32)


def exchange(value, axes):
    return lax.all_to_all(value, axes, split_axis=0, concat_axis=0, tiled=True)


def dot_rows(left, right):
    return lax.dot_general(left, right, (((1,), (1,)), ((), ())), preferred_element_type=F32)


def middle_kernel(
    share, wide, order_ref, hidden_ref, d_first_ref, d_second_ref, gate_ref, up_ref, inner_ref, d_gu_ref, keep_ref, give_ref
):
    hidden = hidden_ref[...]
    gate = jnp.dot(hidden, gate_ref[...], preferred_element_type=F32)
    up = jnp.dot(hidden, up_ref[...], preferred_element_type=F32)
    d_inner = jnp.concatenate([d_first_ref[0], d_second_ref[0]]).astype(F32)
    root = (2.0 / math.pi) ** 0.5
    square = gate * gate
    bent = jnp.tanh(root * gate * (1.0 + 0.044715 * square))
    half = 0.5 * (1.0 + bent)
    gelu = gate * half
    slope = half + 0.5 * gate * (1.0 - bent * bent) * (root * (1.0 + 3 * 0.044715 * square))
    d_gate = (d_inner * up * slope).astype(BF16)
    d_up = (d_inner * gelu).astype(BF16)
    inner_ref[:, :share] = (gelu * up).astype(BF16)
    d_gu_ref[:, :share] = d_gate
    d_gu_ref[:, wide : wide + share] = d_up
    if wide > share:
        rest = jnp.zeros((hidden.shape[0], wide - share), BF16)
        inner_ref[:, share:] = rest
        d_gu_ref[:, share:wide] = rest
        d_gu_ref[:, wide + share :] = rest
    back = (dot_rows(d_gate, gate_ref[...]) + dot_rows(d_up, up_ref[...])).astype(BF16)
    step, steps = pl.program_id(0), pl.num_programs(0)

    @pl.when(step < steps // 2)
    def _():
        keep_ref[...] = back

    @pl.when(step >= steps // 2)
    def _():
        give_ref[...] = back


def feed_forward(hidden, d_inner, order, w_gate, w_up, wide):
    length, width = hidden.shape
    block, share = d_inner.shape[1:]
    rows = 2 * block
    steps = length // rows
    weight = pl.BlockSpec((width, share), lambda n, order_ref: (0, 0), pipeline_mode=pl.Buffered(1))
    return pl.pallas_call(
        functools.partial(middle_kernel, share, wide),
        out_shape=(
            jax.ShapeDtypeStruct((length, wide), BF16),
            jax.ShapeDtypeStruct((length, 2 * wide), BF16),
            jax.ShapeDtypeStruct((length // 2, width), BF16),
            jax.ShapeDtypeStruct((length // 2, width), BF16),
        ),
        grid_spec=pltpu.PrefetchScalarGridSpec(
            num_scalar_prefetch=1,
            grid=(steps,),
            in_specs=[
                pl.BlockSpec((rows, width), lambda n, order_ref: (n, 0)),
                pl.BlockSpec((1, block, share), lambda n, order_ref: (order_ref[2 * n], 0, 0)),
                pl.BlockSpec((1, block, share), lambda n, order_ref: (order_ref[2 * n + 1], 0, 0)),
                weight,
                weight,
            ],
            out_specs=[
                pl.BlockSpec((rows, wide), lambda n, order_ref: (n, 0)),
                pl.BlockSpec((rows, 2 * wide), lambda n, order_ref: (n, 0)),
                pl.BlockSpec((rows, width), lambda n, order_ref: (jnp.minimum(n, steps // 2 - 1), 0)),
                pl.BlockSpec((rows, width), lambda n, order_ref: (jnp.maximum(n - steps // 2, 0), 0)),
            ],
        ),
        compiler_params=pltpu.CompilerParams(vmem_limit_bytes=48 * 2**20),
        cost_estimate=pl.CostEstimate(
            flops=8 * length * width * share,
            bytes_accessed=4 * length * width + 4 * width * share,
            transcendentals=length * share,
        ),
        name="feed_forward",
    )(order, hidden, d_inner, d_inner, w_gate, w_up)


def norm_scale(value):
    return lax.rsqrt(jnp.mean(value * value, axis=-1, keepdims=True) + EPS)


def norm_backward(d_normed, normed, scale):
    return scale * (d_normed - normed * jnp.mean(d_normed * normed, axis=-1, keepdims=True))


def with_gain(weight, gain):
    return (weight.astype(F32) * gain.astype(F32)[:, None]).astype(BF16)


def in_place(mine, other, at):
    both = jnp.zeros(mine.shape[:1] + (2,) + mine.shape[1:], mine.dtype)
    rest = (0,) * (mine.ndim - 1)
    both = lax.dynamic_update_slice(both, mine[:, None], (0, at) + rest)
    return lax.dynamic_update_slice(both, other[:, None], (0, 1 - at) + rest)


def per_device(
    tokens, cotangent, gain_attn, w_query, w_keyval, w_out, b_out, gain_ffn, w_gateup, w_down
):
    block_len, width = tokens.shape[1:]
    n_ctx = lax.axis_size("hi") * lax.axis_size("lo") * lax.axis_size("core")
    n_far, n_near = lax.axis_size("far"), lax.axis_size("near")
    n_seq = n_far * n_near
    n_all = n_ctx * n_seq
    n_group = n_ctx * n_far
    rows = w_query.shape[0]
    length = n_ctx * block_len
    q_scale = HD ** (-0.5)
    position = (lax.axis_index("hi") * lax.axis_size("lo") + lax.axis_index("lo")) * 2 + lax.axis_index("core")
    far, near = lax.axis_index("far"), lax.axis_index("near")
    q_cols = NH * HD // n_ctx
    kv_cols = 2 * HD // n_ctx
    share = FF // n_group
    quarter = width // n_seq

    block = tokens.reshape(block_len, width)
    d_final = cotangent.reshape(block_len, width)
    residual = block.astype(F32)

    qkv_send = jnp.concatenate(
        [
            with_gain(w_query, gain_attn).reshape(rows, n_ctx, q_cols),
            with_gain(w_keyval, gain_attn).reshape(rows, n_ctx, kv_cols),
        ],
        axis=2,
    ).transpose(1, 0, 2)
    qkv_send = jnp.broadcast_to(qkv_send[:, None], (n_ctx, n_seq) + qkv_send.shape[1:])
    scale1 = norm_scale(residual)
    normed1 = residual * scale1
    vectors = jnp.stack([gain_attn, b_out, gain_ffn])
    vectors = jnp.pad(vectors, ((0, 13), (0, width - rows)))
    out_send = jnp.concatenate([w_out, vectors])[None]
    out_near = send(out_send, "near", 1)
    out_far = send(out_send, "far", 1)
    out_both = lax.ppermute(out_send, SEQ, [(i, (i + n_near) % n_seq ^ 1) for i in range(n_seq)])
    hidden1 = lax.all_gather(normed1.astype(BF16), CTX, axis=0, tiled=True)
    w_qkv = exchange(qkv_send.reshape((n_all,) + qkv_send.shape[2:]), EVERY)
    gateup_send = with_gain(w_gateup, gain_ffn).reshape(rows, 2, n_group, share).transpose(1, 2, 0, 3)

    hidden1, w_qkv, gateup_send, out_near, out_far, out_both, d_start = meet(
        hidden1,
        w_qkv.reshape(width, q_cols + kv_cols),
        gateup_send,
        out_near,
        out_far,
        out_both,
        d_final,
    )
    gate_half = exchange(gateup_send[0], GROUP)
    f_theirs = send(d_start, "far", 1)

    def along_seq(part):
        mine = in_place(part(out_send), part(out_near), near)
        other = in_place(part(out_far), part(out_both), near)
        return in_place(mine, other, far)

    out_rows = along_seq(lambda value: value[:, :rows]).reshape(n_seq * rows, width)
    vectors = along_seq(lambda value: value[:, rows : rows + 3, :rows]).reshape(-1)
    full_out = lax.all_gather(out_rows, CTX, axis=0, tiled=True)
    down_other = send(w_down, "near", 1)

    qkv = dot(hidden1, w_qkv)
    qkv = jnp.concatenate([qkv[:, :q_cols] * q_scale, qkv[:, q_cols:]], axis=1).astype(BF16)
    qkv = qkv.reshape(n_ctx, block_len, q_cols + kv_cols)
    kv_send = qkv[:, :, q_cols:].transpose(1, 0, 2).reshape(block_len, 2 * HD)
    kv_send = jnp.broadcast_to(kv_send[None], (n_ctx, block_len, 2 * HD))
    spare = block_len * 8 - n_seq * 3 * rows
    extra = jnp.concatenate([vectors, jnp.zeros((spare,), BF16)]).reshape(1, block_len, 8)
    extra = jnp.broadcast_to(extra, (n_ctx, block_len, 8))
    q_send = jnp.concatenate([qkv[:, :, :q_cols], kv_send, extra], axis=2)
    q_send, gate_half = meet(q_send, gate_half)
    came = exchange(q_send, CTX)
    gate_other = send(gate_half, "near", 1)
    came, up_send = meet(came, gateup_send[1])
    up_half = exchange(up_send, GROUP)
    vectors = came[:, :, q_cols + 2 * HD :].reshape(n_ctx, -1)[:, : n_seq * 3 * rows]
    vectors = vectors.reshape(n_ctx * n_seq, 3, rows).transpose(1, 0, 2).reshape(3, width).astype(F32)
    gain1, bias, gain2 = vectors[0], vectors[1], vectors[2]
    query = came[:, :, :q_cols].transpose(1, 0, 2).reshape(block_len, NH, HD)
    keyval = came[:, :, q_cols : q_cols + 2 * HD].reshape(n_ctx, block_len, n_ctx, kv_cols).transpose(2, 1, 0, 3)
    keyval = keyval.reshape(length, 2 * HD)
    key, value = keyval[:, :HD], keyval[:, HD:]
    spacing = (position * block_len + jnp.arange(block_len, dtype=jnp.int32))[:, None] - jnp.arange(
        length, dtype=jnp.int32
    )[None, :]
    allowed = (spacing >= 0) & (spacing < WINDOW)
    scores = jnp.einsum("qhd,kd->hqk", query, key, preferred_element_type=F32)
    scores = jnp.where(allowed[None], scores, NEG)
    maximum = jnp.max(scores, axis=-1, keepdims=True)
    log_total = maximum + jnp.log(jnp.sum(jnp.exp(scores - maximum), axis=-1, keepdims=True))
    probs_low = jnp.exp(scores - log_total).astype(BF16)
    mixed = jnp.einsum("hqk,kd->qhd", probs_low, value, preferred_element_type=F32).astype(BF16)
    mixed = mixed.reshape(block_len, NH * HD)

    mixed, f_theirs, full_out, gate_other = meet(mixed, f_theirs, full_out, gate_other)
    final_rows = lax.all_gather(jnp.concatenate([d_start, f_theirs]), CTX, axis=0, tiled=True)
    middle = residual + dot(mixed, full_out) + bias

    scale2 = norm_scale(middle)
    normed2 = middle * scale2
    hidden2 = normed2.astype(BF16)
    m_pair = gather_0(hidden2)
    theirs = send(hidden2, "far", 1)
    m_sides = gather_1(m_pair)
    m_sides, theirs, up_half = meet(m_sides, theirs, up_half)
    up_other = send(up_half, "near", 1)
    m_corners = gather_2(m_sides)
    t_pair = gather_0(theirs)
    w_dn = in_place(w_down[None], down_other[None], near).reshape(share, width)
    devices = order_ctx(False)
    d_inner = dot_last(final_rows, w_dn).astype(BF16).reshape(2 * n_ctx, block_len, share)
    m_corners, t_pair, d_inner = meet(m_corners, t_pair, d_inner)
    m_halves = gather_3(m_pair, m_sides, m_corners)
    t_sides = gather_1(t_pair)
    m_halves, t_sides, up_other = meet(m_halves, t_sides, up_other)
    t_corners = gather_2(t_sides)
    hidden_m = gather_all(m_pair, m_halves)
    w_gate = in_place(gate_half, gate_other, near).reshape(width, share)
    t_halves = gather_3(t_pair, t_sides, t_corners)
    w_up = in_place(up_half, up_other, near).reshape(width, share)

    wide = -(-share // 128) * 128
    half = length // 2
    mixed_send = mixed.reshape(block_len, n_ctx, q_cols).transpose(1, 0, 2)
    mixed_send, t_halves = meet(mixed_send, t_halves)
    mixed_cols = exchange(mixed_send, CTX)
    inner_m, d_gu_m, m_keep, m_give = feed_forward(hidden_m, d_inner, 2 * devices, w_gate, w_up, wide)
    m_give, t_halves = meet(m_give, t_halves)
    m_came = send(m_give, "core", 1)
    hidden_t = gather_all(t_pair, t_halves)
    inner_t, d_gu_t, t_keep, t_give = feed_forward(hidden_t, d_inner, 2 * devices + 1, w_gate, w_up, wide)
    t_give, m_keep, m_came, mixed_cols = meet(t_give, m_keep, m_came, mixed_cols)
    t_came = send(t_give, "core", 1)
    m_back = scatter_1(m_keep, m_came, block_len)

    gu_grad = dot_first(hidden_m, d_gu_m)
    gu_grad, t_keep, t_came, m_back, m_keep, m_came = meet(gu_grad, t_keep, t_came, m_back, m_keep, m_came)
    t_back = scatter_1(t_keep, t_came, block_len)
    m_sides = scatter_2(m_keep, m_came, m_back, block_len)
    gu_grad = (gu_grad + dot_first(hidden_t, d_gu_t)).astype(BF16)
    gu_grad, t_back, t_keep, t_came = meet(gu_grad, t_back, t_keep, t_came)
    t_sides = scatter_2(t_keep, t_came, t_back, block_len)
    mixed_cols = pick_blocks(mixed_cols, devices).reshape(length, q_cols)
    places = order_ctx(True)
    inner_rows = jnp.concatenate([inner_m, inner_t]).reshape(2 * n_ctx, block_len, wide)
    inner_rows = pick_blocks(inner_rows, jnp.stack([places, places + n_ctx], axis=1).reshape(-1))
    down_grad = dot_first(final_rows, inner_rows.reshape(2 * length, wide)).astype(BF16)
    down_grad, t_sides, m_sides, mixed_cols = meet(down_grad, t_sides, m_sides, mixed_cols)
    t_other = scatter_3(t_sides)
    m_other = scatter_3(m_sides)
    ffn_grad = [value.reshape(n_far, n_near, quarter, -1) for value in (gu_grad, down_grad)]
    ffn_grad = jnp.stack(
        [jnp.concatenate([value[:, n] for value in ffn_grad], axis=2) for n in range(n_near)]
    )
    ffn_grad, t_other, t_keep, t_came, t_sides = meet(ffn_grad, t_other, t_keep, t_came, t_sides)
    ffn_grad = lax.psum_scatter(ffn_grad, "near", scatter_dimension=0, tiled=True)
    theirs = scatter_4(t_keep, t_came, t_sides, t_other, block_len).astype(BF16)
    theirs = send(theirs, "far", 1)
    out_give = dot(jnp.concatenate([inner_m[half:, :share], inner_t[half:, :share]]), w_dn).astype(BF16)
    out_keep = dot(jnp.concatenate([inner_m[:half, :share], inner_t[:half, :share]]), w_dn).astype(BF16)
    m_other, theirs, out_keep, out_give = meet(m_other, theirs, out_keep, out_give)
    d_hidden2 = scatter_4(m_keep, m_came, m_sides, m_other, block_len) + theirs.astype(F32)

    d_middle = d_final.astype(F32) + norm_backward(d_hidden2, normed2, scale2)
    d_gain2 = jnp.sum(d_hidden2 * normed2, axis=0) / gain2
    d_bias = jnp.sum(d_middle, axis=0)
    d_low = d_middle.astype(BF16)
    d_low, out_give = meet(d_low, out_give)
    l_pair = gather_0(d_low)
    l_pair, d_low, out_give = meet(l_pair, d_low, out_give)
    l_sides = gather_1(l_pair)
    o_came = send(out_give, "core", 1)
    d_mixed = dot_last(d_low, full_out).astype(BF16)
    d_mixed, o_came = meet(d_mixed, o_came)
    o_back = scatter_1(out_keep, o_came, block_len)
    d_mixed = d_mixed.reshape(block_len, NH, HD)
    scores = jnp.einsum("qhd,kd->hqk", query, key, preferred_element_type=F32)
    scores = jnp.where(allowed[None], scores, NEG)
    probs = jnp.exp(scores - log_total)
    probs_again = probs.astype(BF16)
    d_probs = jnp.einsum("qhd,kd->hqk", d_mixed, value, preferred_element_type=F32)
    delta = jnp.sum(probs * d_probs, axis=-1, keepdims=True)
    d_scores = (probs * (d_probs - delta)).astype(BF16)
    d_query = jnp.einsum("hqk,kd->qhd", d_scores, key, preferred_element_type=F32) * q_scale
    d_key = jnp.einsum("hqk,qhd->kd", d_scores, query, preferred_element_type=F32)
    d_value = jnp.einsum("hqk,qhd->kd", probs_again, d_mixed, preferred_element_type=F32)
    d_query = d_query.reshape(block_len, n_ctx, q_cols).astype(BF16).transpose(1, 0, 2)
    d_keyval = jnp.concatenate([d_key, d_value], axis=1).astype(BF16)
    d_keyval = d_keyval.reshape(n_ctx, block_len, n_ctx, kv_cols).transpose(2, 1, 0, 3)
    d_keyval = d_keyval.reshape(n_ctx, block_len, 2 * HD)
    d_send = jnp.concatenate([d_query, d_keyval], axis=2)
    d_send, l_sides, o_back, out_keep, o_came = meet(d_send, l_sides, o_back, out_keep, o_came)
    came = exchange(d_send, CTX)
    l_corners = gather_2(l_sides)
    o_sides = scatter_2(out_keep, o_came, o_back, block_len)
    came, l_corners, ffn_grad = meet(came, l_corners, ffn_grad)
    ffn_grad = ffn_grad[0]
    own_rows = lax.dynamic_index_in_dim(ffn_grad, far, 0, False)
    give = lax.dynamic_index_in_dim(ffn_grad, (far + 1) % n_far, 0, False)
    came, give = meet(came, give)
    by_far = lax.all_gather(give, "far", axis=0)
    l_halves = gather_3(l_pair, l_sides, l_corners)
    d_keyval = jnp.sum(came[:, :, q_cols:].astype(F32), axis=0).astype(BF16)
    d_keyval = d_keyval.reshape(block_len, n_ctx, kv_cols).transpose(1, 0, 2)
    d_qkv = jnp.concatenate([came[:, :, :q_cols], d_keyval], axis=2)
    d_back = pick_blocks(d_qkv, devices).reshape(length, q_cols + kv_cols)
    d_qkv = d_qkv.reshape(length, q_cols + kv_cols)
    e_came = send(dot_last(d_back[half:], w_qkv).astype(BF16), "core", 1)
    e_keep = dot_last(d_back[:half], w_qkv).astype(BF16)
    e_keep, e_came, l_halves, o_sides, d_qkv = meet(e_keep, e_came, l_halves, o_sides, d_qkv)
    e_back = scatter_1(e_keep, e_came, block_len)
    o_other = scatter_3(o_sides)
    out_grad = dot_first(gather_all(l_pair, l_halves), mixed_cols)
    qkv_grad = dot_first(hidden1, d_qkv)
    d_gain1 = jnp.sum(qkv_grad * w_qkv.astype(F32), axis=1) / gain1
    attn_grad = jnp.concatenate([qkv_grad.astype(BF16), out_grad.astype(BF16)], axis=1)
    e_back, o_other, out_keep, o_came = meet(e_back, o_other, out_keep, o_came)
    e_sides = scatter_2(e_keep, e_came, e_back, block_len)
    sums = jnp.stack([d_gain1, d_bias, d_gain2]).reshape(3, n_all, rows).transpose(1, 0, 2)
    e_sides, attn_grad, sums = meet(e_sides, attn_grad, sums)
    attn_grad = lax.psum_scatter(attn_grad, SEQ, scatter_dimension=0, tiled=True).astype(F32)
    e_other = scatter_3(e_sides)
    o_total = scatter_4(out_keep, o_came, o_sides, o_other, block_len)
    o_theirs = send(o_total[block_len:].astype(BF16), "far", 1)
    e_other, o_theirs, by_far, sums = meet(e_other, o_theirs, by_far, sums)
    sums = exchange(sums, EVERY)
    d_normed1 = scatter_4(e_keep, e_came, e_sides, e_other, block_len)
    d_input = d_middle + norm_backward(d_normed1, normed1, scale1)
    output = (middle + o_total[:block_len] + o_theirs.astype(F32)).astype(BF16)
    count = n_ctx // 2
    odd = position % 2
    by_far = [jnp.where(far == f, own_rows, by_far[f]) for f in range(n_far)]
    gate, up = [jnp.stack([v[:, at : at + wide] for v in by_far]) for at in (0, wide)]
    pieces = []
    for flip in range(2):
        pairs = [(c, ((c % 2) ^ flip) * count + c // 2) for c in range(n_ctx)]
        pieces.append(lax.ppermute(jnp.where(odd == flip, gate, up), CTX, pairs))
    down_grad = jnp.concatenate(
        [value[:, 2 * wide : 2 * wide + share].T.astype(F32) for value in by_far]
    )
    upper = position >= count
    columns = [jnp.where(upper, pieces[1], pieces[0]), jnp.where(upper, pieces[0], pieces[1])]
    own_gain = lax.dynamic_slice_in_dim(gain2, (far * n_near + near) * quarter, quarter)
    gateup_grad = (
        jnp.concatenate([columns[i][f][:, :share] for i in range(2) for f in range(n_far)], axis=1).astype(F32)
        * own_gain[:, None]
    )
    attn_grad, sums = meet(attn_grad, sums)
    sums = jnp.sum(sums, axis=0)
    own_gain = lax.dynamic_slice_in_dim(gain1, (far * n_near + near) * quarter, quarter)
    qkv_grad = attn_grad[:, : q_cols + kv_cols] * own_gain[:, None]
    out_grad = attn_grad[:, q_cols + kv_cols :].T
    return (
        output.reshape(1, block_len, width),
        d_input.reshape(1, block_len, width),
        sums[0],
        qkv_grad[:, :q_cols],
        qkv_grad[:, q_cols:],
        out_grad,
        sums[1],
        sums[2],
        gateup_grad,
        down_grad,
    )


def solution(mesh):
    n_ctx, n_seq = mesh.shape["ctx"], mesh.shape["seq"]
    side = math.isqrt(n_ctx // 2)
    fine = Mesh(
        mesh.devices.reshape(n_ctx // 2 // side, side, 2, n_seq // 2, 2), EVERY
    )
    whole = P(EVERY)
    return jax.shard_map(
        per_device,
        mesh=fine,
        in_specs=(
            P(SEQ, CTX, None),
            P(SEQ, CTX, None),
            whole,
            whole,
            whole,
            whole,
            whole,
            whole,
            whole,
            whole,
        ),
        out_specs=(
            P(SEQ, CTX, None),
            P(SEQ, CTX, None),
            whole,
            P(SEQ, CTX),
            P(SEQ, CTX),
            P(CTX, SEQ),
            whole,
            whole,
            P(SEQ, CTX),
            P(CTX, SEQ),
        ),
        check_vma=False,
    )
```

time: 945 us -> 872 us (0.923)
  waiting for transfers between devices: 454 us -> 380 us
  other arithmetic: 63.8 us -> 117 us
  local copies, waits for them, and re-layouts: 172 us -> 121 us
  Pallas kernels: 0 us -> 43.6 us
  starting transfers between devices: 109 us -> 76.8 us
  matrix products: 120 us -> 107 us
    ppermute x74 -> x40, waiting for transfers between devices: 335 us -> 138 us  [the longest x23 89.8 us: send(): lax.ppermute(value, axis, [(i, (i + step) % count) for i in range(count)])]
    all_gather x1 -> x4, waiting for transfers between devices: 0.01 us -> 80.2 us  [the longest x1 67.2 us: per_device(): by_far = lax.all_gather(give, 'far', axis=0)]
    all_to_all x10 -> x7, waiting for transfers between devices: 118 us -> 162 us  [exchange(): return lax.all_to_all(value, axes, split_axis=0, concat_axis=0, tiled=True)]
    pallas_call x0 -> x5, Pallas kernels: none -> 43.6 us  [the longest x2 36.2 us: feed_forward(): pl.pallas_call(functools.partial(middle_kernel, share, wide), out_shape=(...]
    dynamic_update_slice x54 -> x18, local copies, waits for them, and re-layouts: 54.5 us -> 17.5 us  [the longest x9 10.4 us: in_place(): return lax.dynamic_update_slice(both, other[:, None], (0, 1 - at) + rest)]
    concatenate x0 -> x17, other arithmetic: none -> 32.5 us  [the longest x2 13.6 us: gather_all(): return jnp.concatenate([pair[:rows], halves[0], pair[rows:], halves[1]])]
    reshape x8, local copies, waits for them, and re-layouts: 35.2 us -> 10.3 us  [the longest x2 8.6 us: per_device(): with_gain(w_gateup, gain_ffn).reshape(rows, 2, n_group, share)]
    ppermute x74 -> x40, starting transfers between devices: 66.4 us -> 43.9 us  [the longest x14 17.8 us: send_cross(): return lax.ppermute(value, CTX, pairs)]
  transfers between devices with their start and end apart: 87 -> 53, of which waited for: 31 -> 17; matrix products, arithmetic and copies ran while one was open for 35% -> 36% of each run, Pallas kernels for 0% -> 5%
where the time goes in v2:
time: 872 us; the launch traced here: 861 us
  waiting for transfers between devices  380 us (44%)
  local copies, waits for them, and re-layouts  121 us (14%)
  other arithmetic  117 us (13%)
  matrix products  107 us (12%)
  starting transfers between devices  76.8 us (9%)
  Pallas kernels  43.6 us (5%)
  between operations  15.8 us (2%)
    all_to_all x7, waiting for transfers between devices, exchange(): return lax.all_to_all(value, axes, split_axis=0, concat_axis=0, tiled=True)  162 us
    ppermute x23, waiting for transfers between devices, send(): lax.ppermute(value, axis, [(i, (i + step) % count) for i in range(count)])  89.8 us
    all_gather x1, waiting for transfers between devices, per_device(): by_far = lax.all_gather(give, 'far', axis=0)  67.2 us
    ppermute x14, waiting for transfers between devices, send_cross(): return lax.ppermute(value, CTX, pairs)  48.5 us
    dot_general x5, matrix products, dot_first(): lax.dot_general(left, right, (((0,), (0,)), ((), ())), preferred_element_...  41.4 us
    pallas_call x2, Pallas kernels, feed_forward(): pl.pallas_call(functools.partial(middle_kernel, share, wide), out_shape=(...  36.2 us
    all_to_all x7, starting transfers between devices, exchange(): return lax.all_to_all(value, axes, split_axis=0, concat_axis=0, tiled=True)  32.4 us
    dot_general x4, matrix products, dot(): return jnp.dot(left, right, preferred_element_type=F32)  28.6 us
  transfers between devices with their start and end apart: 53, of which 17 were waited for; matrix products, arithmetic and copies ran while one was open for 36% of the time, Pallas kernels for 5%

profile of v2, /device:TPU:0, one launch (start us, length us, event | category | flops | bytes accessed | tf_op | source)
XLA Modules:
  0.0 860.8 jit_solution(15793497541995991088)
XLA Ops:
  19.7 6.2 all-to-all-start
  37.8 15.3 %collective-permute-done.1 = bf16[1,96,2560]{2,1,0:T(8,128)(2,1)} collective-permute-done((bf16[1,96,2560]{2,1,0:T(8,128)(2,1)}, bf16[1,96,2560]{2,1,0:T(8,128)(2,1)}, u32[]{:S(2)}, u32[]{:S(2)}) %collective-permute-start.1) | collective-permute-done | bytes 491552 | tf_op jit(solution)/shard_map/ppermute | solution.py:42
  53.1 46.6 %all-to-all-done = bf16[32,80,384]{2,1,0:T(8,128)(2,1)} async-done(((bf16[32,80,384]{2,1,0:T(8,128)(2,1)}), bf16[32,80,384]{2,1,0:T(8,128)(2,1)}, u32[]{:S(2)}, u32[]{:S(2)}) %all-to-all-start) | async-done | bytes 1966112 | tf_op jit(solution)/shard_map/all_to_all | solution.py:182
  107.8 7.0 all-to-all-start.1
  125.2 21.9 %all-to-all-done.1 = bf16[16,80,480]{2,1,0:T(8,128)(2,1)S(1)} async-done(((bf16[16,80,480]{2,1,0:T(8,128)(2,1)}), bf16[16,80,480]{2,1,0:T(8,128)(2,1)S(1)}, u32[]{:S(2)}, u32[]{:S(2)}) %all-to-all-start.1) | async-done | bytes 1228832 | tf_op jit(solution)/shard_map/all_to_all | solution.py:182
  154.5 36.5 %all-to-all-done.2 = bf16[8,128,840]{1,2,0:T(8,128)(2,1)S(1)} async-done(((bf16[8,128,840]{1,2,0:T(8,128)(2,1)}), bf16[8,128,840]{1,2,0:T(8,128)(2,1)S(1)}, u32[]{:S(2)}, u32[]{:S(2)}) %all-to-all-start.2) | async-done | bytes 1720352 | tf_op jit(solution)/shard_map/all_to_all | solution.py:182
  197.8 13.0 %all-gather.8.cloned.1.call-done = bf16[2560,2560]{1,0:T(8,128)(2,1)} async-done(((bf16[320,2560]{1,0:T(8,128)(2,1)}), bf16[2560,2560]{1,0:T(8,128)(2,1)}) %all-gather.8.cloned.1.call-update) | async-done | bytes 13107216 | tf_op jit(solution)/shard_map/all_gather | solution.py:346
  214.7 7.4 multiply_reduce_fusion.1
  237.5 23.1 %all-to-all-done.3 = bf16[16,80,480]{2,1,0:T(8,128)(2,1)S(1)} async-done(((bf16[16,80,480]{2,1,0:T(8,128)(2,1)}), bf16[16,80,480]{2,1,0:T(8,128)(2,1)S(1)}, u32[]{:S(2)}, u32[]{:S(2)}) %all-to-all-start.3) | async-done | bytes 1228832 | tf_op jit(solution)/shard_map/all_to_all | solution.py:182
  260.6 28.1 %collective-permute-done.7 = bf16[128,2560]{1,0:T(8,128)(2,1)} collective-permute-done((bf16[128,2560]{1,0:T(8,128)(2,1)S(1)}, bf16[128,2560]{1,0:T(8,128)(2,1)}, u32[]{:S(2)}, u32[]{:S(2)}) %collective-permute-start.7) | collective-permute-done | bytes 655392 | tf_op jit(solution)/shard_map/ppermute | solution.py:42
  299.4 9.7 %convolution_convert_fusion.6 = bf16[2048,480]{0,1:T(8,128)(2,1)} fusion(bf16[2048,2560]{1,0:T(8,128)(2,1)} %all-gather.10.cloned.1.call-done, bf16[480,2560]{1,0:T(8,128)(2,1)} %bitcast.46), kind=kOutput, calls=%fused_computation.37 | convolution fusion | flops 5034147840 | bytes 14909440 | tf_op jit(solution)/shard_map/dot_general | solution.py:33
  319.1 27.1 %collective-permute-done.13 = bf16[16,80,480]{2,1,0:T(8,128)(2,1)} collective-permute-done((bf16[16,80,480]{2,1,0:T(8,128)(2,1)}, bf16[16,80,480]{2,1,0:T(8,128)(2,1)}, u32[]{:S(2)}, u32[]{:S(2)}) %collective-permute-start.13) | collective-permute-done | bytes 1228832 | tf_op jit(solution)/shard_map/ppermute | solution.py:42
  350.9 7.1 collective-permute-done.14
  361.5 8.6 pad_maximum_fusion.1.hidden_ref
  370.1 18.1 %feed_forward.2 = (bf16[1024,512]{1,0:T(8,128)(2,1)S(1)}, bf16[1024,1024]{1,0:T(8,128)(2,1)S(1)}, bf16[512,2560]{1,0:T(8,128)(2,1)}, bf16[512,2560]{1,0:T(8,128)(2,1)}) custom-call(s32[8]{0:T(128)S(1)} %get-tuple-element.291.order_ref, bf16[1024,2560]{1,0:T(8,128)(2,1)} %pad_maximum_fusion.1.hidden_ref, bf16[16,128,480]{2,1,0:T(8,128)(2,1)S(1)} %bitcast.400, ...), custom_call_target="tpu_custom_call" | custom-call | flops 10066329600 | bytes 15400960 | tf_op jit(solution)/shard_map/feed_forward/pallas_call | solution.py:230
  389.4 9.7 %fusion.86 = f32[2560,1024]{1,0:T(8,128)} fusion(bf16[1024,1024]{1,0:T(8,128)(2,1)S(1)} %get-tuple-element.136, bf16[384,2560]{1,0:T(8,128)(2,1)} %collective-permute-done.11, bf16[128,2560]{1,0:T(8,128)(2,1)S(1)} %copy-done.25, bf16[384,2560]{1,0:T(8,128)(2,1)S(1)} %copy-done.13, bf16[128,2560]{1,0:T(8,128)(2,1)S(1)} %copy-done.12), kind=kOutput, calls=%fused_computation.247 | convolution fusion | flops 5389680640 | bytes 17825792 | tf_op jit(solution)/shard_map/dot_general | solution.py:37
  408.4 18.2 %feed_forward.3 = (bf16[1024,512]{1,0:T(8,128)(2,1)S(1)}, bf16[1024,1024]{1,0:T(8,128)(2,1)S(1)}, bf16[512,2560]{1,0:T(8,128)(2,1)}, bf16[512,2560]{1,0:T(8,128)(2,1)}) custom-call(s32[8]{0:T(128)S(1)} %get-tuple-element.292.order_ref, bf16[1024,2560]{1,0:T(8,128)(2,1)} %pad_maximum_fusion.2.hidden_ref, bf16[16,128,480]{2,1,0:T(8,128)(2,1)S(1)} %bitcast.402, ...), custom_call_target="tpu_custom_call" | custom-call | flops 10066329600 | bytes 15400960 | tf_op jit(solution)/shard_map/feed_forward/pallas_call | solution.py:230
  432.1 10.5 %fusion.85 = f32[2560,1024]{1,0:T(8,128)} fusion(bf16[1024,1024]{1,0:T(8,128)(2,1)} %copy-done.2, bf16[384,2560]{1,0:T(8,128)(2,1)} %copy-done.37, bf16[128,2560]{1,0:T(8,128)(2,1)} %get-tuple-element.281, bf16[384,2560]{1,0:T(8,128)(2,1)} %copy-done.14, bf16[128,2560]{1,0:T(8,128)(2,1)S(1)} %copy-done.26), kind=kOutput, calls=%fused_computation.246 | convolution fusion | flops 5389680640 | bytes 17825792 | tf_op jit(solution)/shard_map/dot_general | solution.py:37
  455.9 11.2 %add_convert_fusion = bf16[2560,1024]{1,0:T(8,128)(2,1)} fusion(f32[2560,1024]{1,0:T(8,128)} %fusion.86, f32[2560,1024]{1,0:T(8,128)} %fusion.85), kind=kLoop, calls=%fused_computation | loop fusion | flops 5242880 | bytes 26214400 | tf_op jit(solution)/shard_map/convert_element_type | solution.py:427
  471.9 11.1 %convolution_convert_fusion.4 = bf16[2560,512]{1,0:T(8,128)(2,1)} fusion(bf16[2048,2560]{1,0:T(8,128)(2,1)} %all-gather.10.cloned.1.call-done, bf16[2048,512]{1,0:T(8,128)(2,1)S(1)} %bitcast.448), kind=kOutput, calls=%fused_computation.27 | convolution fusion | flops 5370019840 | bytes 15204352 | tf_op jit(solution)/shard_map/dot_general | solution.py:37
  494.4 5.9 pad_maximum_fusion
  504.2 7.8 convolution_convert_fusion.1
  512.1 7.5 convolution_convert_fusion
  519.6 16.0 %collective-permute-done.24 = bf16[128,2560]{1,0:T(8,128)(2,1)S(1)} collective-permute-done((bf16[128,2560]{1,0:T(8,128)(2,1)S(1)}, bf16[128,2560]{1,0:T(8,128)(2,1)S(1)}, u32[]{:S(2)}, u32[]{:S(2)}) %collective-permute-start.24) | collective-permute-done | bytes 655392 | tf_op jit(solution)/shard_map/ppermute | solution.py:42
  544.4 9.9 %convolution_convert_fusion.5 = bf16[128,2560]{1,0:T(8,128)(2,1)} fusion(bf16[128,2560]{1,0:T(8,128)(2,1)S(1)} %convert_element_type.398, bf16[2560,2560]{1,0:T(8,128)(2,1)} %all-gather.8.cloned.1.call-done), kind=kOutput, calls=%fused_computation.34 | convolution fusion | flops 1678049280 | bytes 14417920 | tf_op jit(solution)/shard_map/dot_general | solution.py:33
  591.2 24.8 %collective-permute-done.29 = bf16[128,2560]{1,0:T(8,128)(2,1)S(1)} collective-permute-done((bf16[128,2560]{1,0:T(8,128)(2,1)S(1)}, bf16[128,2560]{1,0:T(8,128)(2,1)S(1)}, u32[]{:S(2)}, u32[]{:S(2)}) %collective-permute-start.29) | collective-permute-done | bytes 655392 | tf_op jit(solution)/shard_map/ppermute | solution.py:62
  656.6 6.1 multiply_reduce_fusion
  675.7 10.9 %collective-permute-done.35 = bf16[256,2560]{1,0:T(8,128)(2,1)} collective-permute-done((bf16[256,2560]{1,0:T(8,128)(2,1)S(1)}, bf16[256,2560]{1,0:T(8,128)(2,1)}, u32[]{:S(2)}, u32[]{:S(2)}) %collective-permute-start.35) | collective-permute-done | bytes 1310752 | tf_op jit(solution)/shard_map/ppermute | solution.py:62
  686.6 6.1 copy.142
  700.9 67.2 %all-gather.12.cloned.1.call-done = bf16[1280,1536]{1,0:T(8,128)(2,1)} async-done(((bf16[640,1536]{1,0:T(8,128)(2,1)}), bf16[1280,1536]{1,0:T(8,128)(2,1)}) %all-gather.12.cloned.1.call-update) | async-done | bytes 3932176 | tf_op jit(solution)/shard_map/all_gather | solution.py:488
  774.5 12.1 %collective-permute-start.39 = (bf16[2,640,512]{2,1,0:T(8,128)(2,1)}, bf16[2,640,512]{2,1,0:T(8,128)(2,1)}, u32[]{:S(2)}, u32[]{:S(2)}) collective-permute-start(bf16[2,640,512]{2,1,0:T(8,128)(2,1)} %get-tuple-element.264), channel_id=1, source_target_pairs={{0,0},{4,16},{8,4},{12,20},{16,8},{20,24},{24,12},{28,28},{1,1},{5... | collective-permute-start | bytes 3932168 | tf_op jit(solution)/shard_map/ppermute | solution.py:524
  802.7 33.7 %all-to-all-done.6 = f32[32,1,240]{2,1,0:T(1,128)S(1)} async-done(((f32[32,1,240]{2,1,0:T(1,128)}), f32[32,1,240]{2,1,0:T(1,128)S(1)}, u32[]{:S(2)}, u32[]{:S(2)}) %all-to-all-start.6) | async-done | bytes 30752 | tf_op jit(solution)/shard_map/all_to_all | solution.py:182
  (405 shorter events, 300.8 us)
Async XLA Ops:
  7.2 92.5 %all-gather.6.cloned.1.call-start = ((), (), s32[]{:S(2)}) async-start(), calls=%async_computation.9 | async-start | bytes 5898240 | tf_op jit(solution)/shard_map/all_gather | solution.py:323
  14.7 38.4 %collective-permute-start.1 = (bf16[1,96,2560]{2,1,0:T(8,128)(2,1)}, bf16[1,96,2560]{2,1,0:T(8,128)(2,1)}, u32[]{:S(2)}, u32[]{:S(2)}) collective-permute-start(bf16[1,96,2560]{2,1,0:T(8,128)(2,1)} %maximum_bitcast_fusion.4), channel_id=1, source_target_pairs={{0,2},{2,0},{1,3},{3,1},{4,6},{6,4},{5,7},{7,5},{8,10},{10,8},{9,1... | collective-permute-start | bytes 1474568 | tf_op jit(solution)/shard_map/ppermute | solution.py:42
  17.3 35.9 %collective-permute-start.2 = (bf16[1,96,2560]{2,1,0:T(8,128)(2,1)}, bf16[1,96,2560]{2,1,0:T(8,128)(2,1)}, u32[]{:S(2)}, u32[]{:S(2)}) collective-permute-start(bf16[1,96,2560]{2,1,0:T(8,128)(2,1)} %maximum_bitcast_fusion.4), channel_id=1, source_target_pairs={{0,3},{1,2},{2,1},{3,0},{4,7},{5,6},{6,5},{7,4},{8,11},{9,10},{10,... | collective-permute-start | bytes 1474568 | tf_op jit(solution)/shard_map/ppermute | solution.py:322
  19.7 80.0 %all-to-all-start = ((bf16[32,80,384]{2,1,0:T(8,128)(2,1)}), bf16[32,80,384]{2,1,0:T(8,128)(2,1)}, u32[]{:S(2)}, u32[]{:S(2)}) async-start(bf16[32,80,384]{2,1,0:T(8,128)(2,1)} %bitcast.3), calls=%async_computation | async-start | bytes 3932160 | tf_op jit(solution)/shard_map/all_to_all | solution.py:182
  25.9 185.0 %all-gather.8.cloned.1.call-start = ((), (), s32[]{:S(2)}) async-start(), calls=%async_computation.10 | async-start | bytes 14745600 | tf_op jit(solution)/shard_map/all_gather | solution.py:346
  107.8 39.4 %all-to-all-start.1 = ((bf16[16,80,480]{2,1,0:T(8,128)(2,1)}), bf16[16,80,480]{2,1,0:T(8,128)(2,1)S(1)}, u32[]{:S(2)}, u32[]{:S(2)}) async-start(bf16[16,80,480]{2,1,0:T(8,128)(2,1)} %get-tuple-element.269), calls=%async_computation.1 | async-start | bytes 2621440 | tf_op jit(solution)/shard_map/all_to_all | solution.py:182
  148.2 42.8 %all-to-all-start.2 = ((bf16[8,128,840]{1,2,0:T(8,128)(2,1)}), bf16[8,128,840]{1,2,0:T(8,128)(2,1)S(1)}, u32[]{:S(2)}, u32[]{:S(2)}) async-start(bf16[8,128,840]{1,2,0:T(8,128)(2,1)} %pad_maximum_fusion.6), calls=%async_computation.2 | async-start | bytes 3440640 | tf_op jit(solution)/shard_map/all_to_all | solution.py:182
  151.8 147.6 %all-gather.10.cloned.1.call-start = ((), (), s32[]{:S(2)}) async-start(), calls=%async_computation.11 | async-start | bytes 11796480 | tf_op jit(solution)/shard_map/all_gather | solution.py:383
  152.3 44.3 %collective-permute-start.3 = (bf16[128,2560]{1,0:T(8,128)(2,1)}, bf16[128,2560]{1,0:T(8,128)(2,1)}, u32[]{:S(2)}, u32[]{:S(2)}) collective-permute-start(bf16[128,2560]{1,0:T(8,128)(2,1)} %bitcast.10), channel_id=1, source_target_pairs={{0,2},{2,0},{1,3},{3,1},{4,6},{6,4},{5,7},{7,5},{8,10},{10,8},{9,1... | collective-permute-start | bytes 1966088 | tf_op jit(solution)/shard_map/ppermute | solution.py:42
  152.3 45.5 %collective-permute-start.4 = (bf16[16,80,480]{2,1,0:T(8,128)(2,1)}, bf16[16,80,480]{2,1,0:T(8,128)(2,1)}, u32[]{:S(2)}, u32[]{:S(2)}) collective-permute-start(bf16[16,80,480]{2,1,0:T(8,128)(2,1)} %copy-done.16), channel_id=1, source_target_pairs={{0,1},{1,0},{2,3},{3,2},{4,5},{5,4},{6,7},{7,6},{8,9},{9,8},{10,11... | collective-permute-start | bytes 3686408 | tf_op jit(solution)/shard_map/ppermute | solution.py:42
  223.6 37.0 %all-to-all-start.3 = ((bf16[16,80,480]{2,1,0:T(8,128)(2,1)}), bf16[16,80,480]{2,1,0:T(8,128)(2,1)S(1)}, u32[]{:S(2)}, u32[]{:S(2)}) async-start(bf16[16,80,480]{2,1,0:T(8,128)(2,1)} %get-tuple-element.124), calls=%async_computation.3 | async-start | bytes 2621440 | tf_op jit(solution)/shard_map/all_to_all | solution.py:182
  229.0 59.7 %collective-permute-start.6 = (bf16[256,2560]{1,0:T(8,128)(2,1)}, bf16[256,2560]{1,0:T(8,128)(2,1)}, u32[]{:S(2)}, u32[]{:S(2)}) collective-permute-start(bf16[256,2560]{1,0:T(8,128)(2,1)} %pad_maximum_fusion.8), channel_id=1, source_target_pairs={{0,8},{4,20},{8,0},{12,28},{16,24},{20,4},{24,16},{28,12},{1,9},{5... | collective-permute-start | bytes 3932168 | tf_op jit(solution)/shard_map/ppermute | solution.py:62
  230.9 57.9 %collective-permute-start.10 = (bf16[240,2560]{1,0:T(8,128)(2,1)}, bf16[240,2560]{1,0:T(8,128)(2,1)}, u32[]{:S(2)}, u32[]{:S(2)}) collective-permute-start(bf16[240,2560]{1,0:T(8,128)(2,1)} %param.19), channel_id=1, source_target_pairs={{0,1},{1,0},{2,3},{3,2},{4,5},{5,4},{6,7},{7,6},{8,9},{9,8},{10,11... | collective-permute-start | bytes 3686408 | tf_op jit(solution)/shard_map/ppermute | solution.py:42
  231.1 57.6 %collective-permute-start.7 = (bf16[128,2560]{1,0:T(8,128)(2,1)S(1)}, bf16[128,2560]{1,0:T(8,128)(2,1)}, u32[]{:S(2)}, u32[]{:S(2)}) collective-permute-start(bf16[128,2560]{1,0:T(8,128)(2,1)S(1)} %multiply_convert_fusion.1), channel_id=1, source_target_pairs={{0,2},{2,0},{1,3},{3,1},{4,6},{6,4},{5,7},{7,5},{8,10},{10,8},{9,1... | collective-permute-start | bytes 1966088 | tf_op jit(solution)/shard_map/ppermute | solution.py:42
  314.4 31.7 %collective-permute-start.11 = (bf16[384,2560]{1,0:T(8,128)(2,1)}, bf16[384,2560]{1,0:T(8,128)(2,1)}, u32[]{:S(2)}, u32[]{:S(2)}) collective-permute-start(bf16[384,2560]{1,0:T(8,128)(2,1)} %constant_dynamic-update-slice_fusion), channel_id=1, source_target_pairs={{0,4},{4,0},{1,5},{5,1},{2,6},{6,2},{3,7},{7,3},{8,12},{12,8},{9,1... | collective-permute-start | bytes 5898248 | tf_op jit(solution)/shard_map/ppermute | solution.py:42
  314.4 31.7 %collective-permute-start.12 = (bf16[256,2560]{1,0:T(8,128)(2,1)}, bf16[256,2560]{1,0:T(8,128)(2,1)}, u32[]{:S(2)}, u32[]{:S(2)}) collective-permute-start(bf16[256,2560]{1,0:T(8,128)(2,1)} %pad_maximum_fusion.9), channel_id=1, source_target_pairs={{0,8},{4,20},{8,0},{12,28},{16,24},{20,4},{24,16},{28,12},{1,9},{5... | collective-permute-start | bytes 3932168 | tf_op jit(solution)/shard_map/ppermute | solution.py:62
  315.1 31.0 %collective-permute-start.13 = (bf16[16,80,480]{2,1,0:T(8,128)(2,1)}, bf16[16,80,480]{2,1,0:T(8,128)(2,1)}, u32[]{:S(2)}, u32[]{:S(2)}) collective-permute-start(bf16[16,80,480]{2,1,0:T(8,128)(2,1)} %copy-done.18), channel_id=1, source_target_pairs={{0,1},{1,0},{2,3},{3,2},{4,5},{5,4},{6,7},{7,6},{8,9},{9,8},{10,11... | collective-permute-start | bytes 3686408 | tf_op jit(solution)/shard_map/ppermute | solution.py:42
  358.0 30.1 %collective-permute-start.15 = (bf16[384,2560]{1,0:T(8,128)(2,1)S(1)}, bf16[384,2560]{1,0:T(8,128)(2,1)S(1)}, u32[]{:S(2)}, u32[]{:S(2)}) collective-permute-start(bf16[384,2560]{1,0:T(8,128)(2,1)S(1)} %constant_dynamic-update-slice_fusion.2), channel_id=1, source_target_pairs={{0,4},{4,0},{1,5},{5,1},{2,6},{6,2},{3,7},{7,3},{8,12},{12,8},{9,1... | collective-permute-start | bytes 5898248 | tf_op jit(solution)/shard_map/ppermute | solution.py:42
  388.1 39.7 %collective-permute-start.16 = (bf16[512,2560]{1,0:T(8,128)(2,1)}, bf16[512,2560]{1,0:T(8,128)(2,1)}, u32[]{:S(2)}, u32[]{:S(2)}) collective-permute-start(bf16[512,2560]{1,0:T(8,128)(2,1)} %get-tuple-element.146), channel_id=1, source_target_pairs={{0,4},{4,0},{1,5},{5,1},{2,6},{6,2},{3,7},{7,3},{8,12},{12,8},{9,1... | collective-permute-start | bytes 7864328 | tf_op jit(solution)/shard_map/ppermute | solution.py:42
  403.3 212.7 %reduce-scatter.5.cloned.1.call-start = ((), (), s32[]{:S(2)}) async-start(), calls=%async_computation.12 | async-start | bytes 11796480 | tf_op jit(solution)/shard_map/reduce_scatter | solution.py:443
  454.2 36.5 %collective-permute-start.21 = (bf16[256,2560]{1,0:T(8,128)(2,1)}, bf16[256,2560]{1,0:T(8,128)(2,1)}, u32[]{:S(2)}, u32[]{:S(2)}) collective-permute-start(bf16[256,2560]{1,0:T(8,128)(2,1)} %pad_maximum_fusion.12), channel_id=1, source_target_pairs={{0,8},{4,20},{8,0},{12,28},{16,24},{20,4},{24,16},{28,12},{1,9},{5... | collective-permute-start | bytes 3932168 | tf_op jit(solution)/shard_map/ppermute | solution.py:62
  504.2 31.5 %collective-permute-start.24 = (bf16[128,2560]{1,0:T(8,128)(2,1)S(1)}, bf16[128,2560]{1,0:T(8,128)(2,1)S(1)}, u32[]{:S(2)}, u32[]{:S(2)}) collective-permute-start(bf16[128,2560]{1,0:T(8,128)(2,1)S(1)} %fusion.35), channel_id=1, source_target_pairs={{0,2},{2,0},{1,3},{3,1},{4,6},{6,4},{5,7},{7,5},{8,10},{10,8},{9,1... | collective-permute-start | bytes 1966088 | tf_op jit(solution)/shard_map/ppermute | solution.py:42
  575.7 40.2 %all-to-all-start.5 = ((bf16[8,128,832]{1,2,0:T(8,128)(2,1)}), bf16[8,128,832]{1,2,0:T(8,128)(2,1)}, u32[]{:S(2)}, u32[]{:S(2)}) async-start(bf16[8,128,832]{1,2,0:T(8,128)(2,1)} %pad_maximum_fusion.7), calls=%async_computation.5 | async-start | bytes 3407872 | tf_op jit(solution)/shard_map/all_to_all | solution.py:182
  580.1 188.0 %all-gather.12.cloned.1.call-start = ((), (), s32[]{:S(2)}) async-start(), calls=%async_computation.13 | async-start | bytes 5898240 | tf_op jit(solution)/shard_map/all_gather | solution.py:488
  581.3 34.7 %collective-permute-start.29 = (bf16[128,2560]{1,0:T(8,128)(2,1)S(1)}, bf16[128,2560]{1,0:T(8,128)(2,1)S(1)}, u32[]{:S(2)}, u32[]{:S(2)}) collective-permute-start(bf16[128,2560]{1,0:T(8,128)(2,1)S(1)} %slice.385), channel_id=1, source_target_pairs={{0,16},{4,12},{8,24},{12,4},{16,0},{20,28},{24,8},{28,20},{1,17},{... | collective-permute-start | bytes 1966088 | tf_op jit(solution)/shard_map/ppermute | solution.py:62
  589.7 59.7 %collective-permute-start.32 = (bf16[512,2560]{1,0:T(8,128)(2,1)}, bf16[512,2560]{1,0:T(8,128)(2,1)}, u32[]{:S(2)}, u32[]{:S(2)}) collective-permute-start(bf16[512,2560]{1,0:T(8,128)(2,1)} %pad_maximum_fusion.4), channel_id=1, source_target_pairs={{0,8},{4,20},{8,0},{12,28},{16,24},{20,4},{24,16},{28,12},{1,9},{5... | collective-permute-start | bytes 7864328 | tf_op jit(solution)/shard_map/ppermute | solution.py:62
  646.1 202.3 %reduce-scatter.7.cloned.1.call-start = ((), (), s32[]{:S(2)}) async-start(), calls=%async_computation.14 | async-start | bytes 4915200
  698.1 70.0 %collective-permute-start.37 = (bf16[128,2560]{1,0:T(8,128)(2,1)}, bf16[128,2560]{1,0:T(8,128)(2,1)}, u32[]{:S(2)}, u32[]{:S(2)}) collective-permute-start(bf16[128,2560]{1,0:T(8,128)(2,1)} %slice.634), channel_id=1, source_target_pairs={{0,2},{2,0},{1,3},{3,1},{4,6},{6,4},{5,7},{7,5},{8,10},{10,8},{9,1... | collective-permute-start | bytes 1966088 | tf_op jit(solution)/shard_map/ppermute | solution.py:42
  700.9 67.2 %collective-permute-start.36 = (bf16[128,2560]{1,0:T(8,128)(2,1)}, bf16[128,2560]{1,0:T(8,128)(2,1)S(1)}, u32[]{:S(2)}, u32[]{:S(2)}) collective-permute-start(bf16[128,2560]{1,0:T(8,128)(2,1)} %slice.413), channel_id=1, source_target_pairs={{0,4},{4,0},{1,5},{5,1},{2,6},{6,2},{3,7},{7,3},{8,12},{12,8},{9,1... | collective-permute-start | bytes 1966088 | tf_op jit(solution)/shard_map/ppermute | solution.py:42
  774.5 63.2 %collective-permute-start.39 = (bf16[2,640,512]{2,1,0:T(8,128)(2,1)}, bf16[2,640,512]{2,1,0:T(8,128)(2,1)}, u32[]{:S(2)}, u32[]{:S(2)}) collective-permute-start(bf16[2,640,512]{2,1,0:T(8,128)(2,1)} %get-tuple-element.264), channel_id=1, source_target_pairs={{0,0},{4,16},{8,4},{12,20},{16,8},{20,24},{24,12},{28,28},{1,1},{5... | collective-permute-start | bytes 3932168 | tf_op jit(solution)/shard_map/ppermute | solution.py:524
  786.6 51.2 %collective-permute-start.38 = (bf16[2,640,512]{2,1,0:T(8,128)(2,1)}, bf16[2,640,512]{2,1,0:T(8,128)(2,1)}, u32[]{:S(2)}, u32[]{:S(2)}) collective-permute-start(bf16[2,640,512]{2,1,0:T(8,128)(2,1)} %get-tuple-element.265), channel_id=1, source_target_pairs={{0,16},{4,0},{8,20},{12,4},{16,24},{20,8},{24,28},{28,12},{1,17},{... | collective-permute-start | bytes 3932168 | tf_op jit(solution)/shard_map/ppermute | solution.py:524
  792.6 43.7 %all-to-all-start.6 = ((f32[32,1,240]{2,1,0:T(1,128)}), f32[32,1,240]{2,1,0:T(1,128)S(1)}, u32[]{:S(2)}, u32[]{:S(2)}) async-start(f32[32,1,240]{2,1,0:T(1,128)} %reshape.561), calls=%async_computation.7 | async-start | bytes 65536 | tf_op jit(solution)/shard_map/all_to_all | solution.py:182
  (78 other events, 963.4 us)
Sparse Core Ops, SparseCore 0:
  10.9 54.8 all-gather.5
  106.2 104.5 all-gather.7
  213.4 81.9 all-gather.9
  500.5 106.6 reduce-scatter.4
  646.2 121.8 all-gather.11
  770.4 72.1 reduce-scatter.6

commit v3 on v2

--- a/solution.py
+++ b/solution.py
@@ -318,13 +318,14 @@
     vectors = jnp.pad(vectors, ((0, 13), (0, width - rows)))
     out_send = jnp.concatenate([w_out, vectors])[None]
     out_near = send(out_send, "near", 1)
+    down_other = send(w_down, "near", 1)
     out_far = send(out_send, "far", 1)
     out_both = lax.ppermute(out_send, SEQ, [(i, (i + n_near) % n_seq ^ 1) for i in range(n_seq)])
     hidden1 = lax.all_gather(normed1.astype(BF16), CTX, axis=0, tiled=True)
     w_qkv = exchange(qkv_send.reshape((n_all,) + qkv_send.shape[2:]), EVERY)
     gateup_send = with_gain(w_gateup, gain_ffn).reshape(rows, 2, n_group, share).transpose(1, 2, 0, 3)
 
-    hidden1, w_qkv, gateup_send, out_near, out_far, out_both, d_start = meet(
+    hidden1, w_qkv, gateup_send, out_near, out_far, out_both, d_start, down_other = meet(
         hidden1,
         w_qkv.reshape(width, q_cols + kv_cols),
         gateup_send,
@@ -332,6 +333,7 @@
         out_far,
         out_both,
         d_final,
+        down_other,
     )
     gate_half = exchange(gateup_send[0], GROUP)
     f_theirs = send(d_start, "far", 1)
@@ -344,7 +346,6 @@
     out_rows = along_seq(lambda value: value[:, :rows]).reshape(n_seq * rows, width)
     vectors = along_seq(lambda value: value[:, rows : rows + 3, :rows]).reshape(-1)
     full_out = lax.all_gather(out_rows, CTX, axis=0, tiled=True)
-    down_other = send(w_down, "near", 1)
 
     qkv = dot(hidden1, w_qkv)
     qkv = jnp.concatenate([qkv[:, :q_cols] * q_scale, qkv[:, q_cols:]], axis=1).astype(BF16)
@@ -359,7 +360,8 @@
     came = exchange(q_send, CTX)
     gate_other = send(gate_half, "near", 1)
     came, up_send = meet(came, gateup_send[1])
-    up_half = exchange(up_send, GROUP)
+    cut = -(-rows * 3 // 5 // 16) * 16
+    up_first = exchange(up_send[:, :cut], GROUP)
     vectors = came[:, :, q_cols + 2 * HD :].reshape(n_ctx, -1)[:, : n_seq * 3 * rows]
     vectors = vectors.reshape(n_ctx * n_seq, 3, rows).transpose(1, 0, 2).reshape(3, width).astype(F32)
     gain1, bias, gain2 = vectors[0], vectors[1], vectors[2]
@@ -379,32 +381,40 @@
     mixed = jnp.einsum("hqk,kd->qhd", probs_low, value, preferred_element_type=F32).astype(BF16)
     mixed = mixed.reshape(block_len, NH * HD)
 
-    mixed, f_theirs, full_out, gate_other = meet(mixed, f_theirs, full_out, gate_other)
+    mixed, f_theirs, full_out, gate_other, up_first, up_send = meet(
+        mixed, f_theirs, full_out, gate_other, up_first, up_send
+    )
+    up_second = exchange(up_send[:, cut:], GROUP)
+    near_first = send(up_first, "near", 1)
     final_rows = lax.all_gather(jnp.concatenate([d_start, f_theirs]), CTX, axis=0, tiled=True)
     middle = residual + dot(mixed, full_out) + bias
 
     scale2 = norm_scale(middle)
     normed2 = middle * scale2
     hidden2 = normed2.astype(BF16)
+    hidden2, up_second = meet(hidden2, up_second)
     m_pair = gather_0(hidden2)
     theirs = send(hidden2, "far", 1)
+    near_second = send(up_second, "near", 1)
     m_sides = gather_1(m_pair)
-    m_sides, theirs, up_half = meet(m_sides, theirs, up_half)
-    up_other = send(up_half, "near", 1)
+    w_dn = in_place(w_down[None], down_other[None], near).reshape(share, width)
+    devices = order_ctx(False)
+    w_gate = in_place(gate_half, gate_other, near).reshape(width, share)
+    m_sides, theirs, near_first, w_dn, w_gate = meet(m_sides, theirs, near_first, w_dn, w_gate)
     m_corners = gather_2(m_sides)
     t_pair = gather_0(theirs)
-    w_dn = in_place(w_down[None], down_other[None], near).reshape(share, width)
-    devices = order_ctx(False)
+    m_corners, t_pair, near_second = meet(m_corners, t_pair, near_second)
     d_inner = dot_last(final_rows, w_dn).astype(BF16).reshape(2 * n_ctx, block_len, share)
-    m_corners, t_pair, d_inner = meet(m_corners, t_pair, d_inner)
     m_halves = gather_3(m_pair, m_sides, m_corners)
     t_sides = gather_1(t_pair)
-    m_halves, t_sides, up_other = meet(m_halves, t_sides, up_other)
+    up_half = jnp.concatenate([up_first, up_second], axis=1)
+    up_other = jnp.concatenate([near_first, near_second], axis=1)
+    w_up = in_place(up_half, up_other, near).reshape(width, share)
+    m_halves, t_sides, w_up, d_inner = meet(m_halves, t_sides, w_up, d_inner)
     t_corners = gather_2(t_sides)
     hidden_m = gather_all(m_pair, m_halves)
-    w_gate = in_place(gate_half, gate_other, near).reshape(width, share)
+    t_corners, hidden_m = meet(t_corners, hidden_m)
     t_halves = gather_3(t_pair, t_sides, t_corners)
-    w_up = in_place(up_half, up_other, near).reshape(width, share)
 
     wide = -(-share // 128) * 128
     half = length // 2
@@ -416,36 +426,41 @@
     m_came = send(m_give, "core", 1)
     hidden_t = gather_all(t_pair, t_halves)
     inner_t, d_gu_t, t_keep, t_give = feed_forward(hidden_t, d_inner, 2 * devices + 1, w_gate, w_up, wide)
-    t_give, m_keep, m_came, mixed_cols = meet(t_give, m_keep, m_came, mixed_cols)
+    t_give, m_keep, m_came, mixed_cols, inner_m = meet(t_give, m_keep, m_came, mixed_cols, inner_m)
     t_came = send(t_give, "core", 1)
     m_back = scatter_1(m_keep, m_came, block_len)
-
-    gu_grad = dot_first(hidden_m, d_gu_m)
-    gu_grad, t_keep, t_came, m_back, m_keep, m_came = meet(gu_grad, t_keep, t_came, m_back, m_keep, m_came)
-    t_back = scatter_1(t_keep, t_came, block_len)
-    m_sides = scatter_2(m_keep, m_came, m_back, block_len)
-    gu_grad = (gu_grad + dot_first(hidden_t, d_gu_t)).astype(BF16)
-    gu_grad, t_back, t_keep, t_came = meet(gu_grad, t_back, t_keep, t_came)
-    t_sides = scatter_2(t_keep, t_came, t_back, block_len)
     mixed_cols = pick_blocks(mixed_cols, devices).reshape(length, q_cols)
     places = order_ctx(True)
     inner_rows = jnp.concatenate([inner_m, inner_t]).reshape(2 * n_ctx, block_len, wide)
     inner_rows = pick_blocks(inner_rows, jnp.stack([places, places + n_ctx], axis=1).reshape(-1))
-    down_grad = dot_first(final_rows, inner_rows.reshape(2 * length, wide)).astype(BF16)
-    down_grad, t_sides, m_sides, mixed_cols = meet(down_grad, t_sides, m_sides, mixed_cols)
+    mixed_cols, inner_rows, t_keep, t_came, m_back, m_keep, m_came, inner_m, inner_t = meet(
+        mixed_cols, inner_rows, t_keep, t_came, m_back, m_keep, m_came, inner_m, inner_t
+    )
+    t_back = scatter_1(t_keep, t_came, block_len)
+    m_sides = scatter_2(m_keep, m_came, m_back, block_len)
+    out_give = dot(jnp.concatenate([inner_m[half:, :share], inner_t[half:, :share]]), w_dn).astype(BF16)
+    out_keep = dot(jnp.concatenate([inner_m[:half, :share], inner_t[:half, :share]]), w_dn).astype(BF16)
+    out_give, out_keep, t_back, t_keep, t_came, d_gu_m, d_gu_t = meet(
+        out_give, out_keep, t_back, t_keep, t_came, d_gu_m, d_gu_t
+    )
+    t_sides = scatter_2(t_keep, t_came, t_back, block_len)
+
+    gu_grad = dot_first(jnp.concatenate([hidden_m, hidden_t]), jnp.concatenate([d_gu_m, d_gu_t]))
+    gu_grad, t_sides, m_sides, t_keep, t_came, inner_rows = meet(
+        gu_grad.astype(BF16), t_sides, m_sides, t_keep, t_came, inner_rows
+    )
     t_other = scatter_3(t_sides)
     m_other = scatter_3(m_sides)
+    theirs = scatter_4(t_keep, t_came, t_sides, t_other, block_len).astype(BF16)
+    theirs, inner_rows = meet(theirs, inner_rows)
+    theirs = send(theirs, "far", 1)
+    down_grad = dot_first(final_rows, inner_rows.reshape(2 * length, wide)).astype(BF16)
     ffn_grad = [value.reshape(n_far, n_near, quarter, -1) for value in (gu_grad, down_grad)]
     ffn_grad = jnp.stack(
         [jnp.concatenate([value[:, n] for value in ffn_grad], axis=2) for n in range(n_near)]
     )
-    ffn_grad, t_other, t_keep, t_came, t_sides = meet(ffn_grad, t_other, t_keep, t_came, t_sides)
+    m_other, theirs = meet(m_other, theirs)
     ffn_grad = lax.psum_scatter(ffn_grad, "near", scatter_dimension=0, tiled=True)
-    theirs = scatter_4(t_keep, t_came, t_sides, t_other, block_len).astype(BF16)
-    theirs = send(theirs, "far", 1)
-    out_give = dot(jnp.concatenate([inner_m[half:, :share], inner_t[half:, :share]]), w_dn).astype(BF16)
-    out_keep = dot(jnp.concatenate([inner_m[:half, :share], inner_t[:half, :share]]), w_dn).astype(BF16)
-    m_other, theirs, out_keep, out_give = meet(m_other, theirs, out_keep, out_give)
     d_hidden2 = scatter_4(m_keep, m_came, m_sides, m_other, block_len) + theirs.astype(F32)
 
     d_middle = d_final.astype(F32) + norm_backward(d_hidden2, normed2, scale2)
@@ -481,11 +496,7 @@
     l_corners = gather_2(l_sides)
     o_sides = scatter_2(out_keep, o_came, o_back, block_len)
     came, l_corners, ffn_grad = meet(came, l_corners, ffn_grad)
-    ffn_grad = ffn_grad[0]
-    own_rows = lax.dynamic_index_in_dim(ffn_grad, far, 0, False)
-    give = lax.dynamic_index_in_dim(ffn_grad, (far + 1) % n_far, 0, False)
-    came, give = meet(came, give)
-    by_far = lax.all_gather(give, "far", axis=0)
+    ffn_grad = exchange(ffn_grad[0], ("far",))
     l_halves = gather_3(l_pair, l_sides, l_corners)
     d_keyval = jnp.sum(came[:, :, q_cols:].astype(F32), axis=0).astype(BF16)
     d_keyval = d_keyval.reshape(block_len, n_ctx, kv_cols).transpose(1, 0, 2)
@@ -504,27 +515,23 @@
     e_back, o_other, out_keep, o_came = meet(e_back, o_other, out_keep, o_came)
     e_sides = scatter_2(e_keep, e_came, e_back, block_len)
     sums = jnp.stack([d_gain1, d_bias, d_gain2]).reshape(3, n_all, rows).transpose(1, 0, 2)
-    e_sides, attn_grad, sums = meet(e_sides, attn_grad, sums)
-    attn_grad = lax.psum_scatter(attn_grad, SEQ, scatter_dimension=0, tiled=True).astype(F32)
+    e_sides, attn_grad, sums, ffn_grad = meet(e_sides, attn_grad, sums, ffn_grad)
+    attn_grad = lax.psum_scatter(attn_grad, SEQ, scatter_dimension=0, tiled=True)
     e_other = scatter_3(e_sides)
     o_total = scatter_4(out_keep, o_came, o_sides, o_other, block_len)
     o_theirs = send(o_total[block_len:].astype(BF16), "far", 1)
-    e_other, o_theirs, by_far, sums = meet(e_other, o_theirs, by_far, sums)
-    sums = exchange(sums, EVERY)
     d_normed1 = scatter_4(e_keep, e_came, e_sides, e_other, block_len)
     d_input = d_middle + norm_backward(d_normed1, normed1, scale1)
     output = (middle + o_total[:block_len] + o_theirs.astype(F32)).astype(BF16)
     count = n_ctx // 2
     odd = position % 2
-    by_far = [jnp.where(far == f, own_rows, by_far[f]) for f in range(n_far)]
-    gate, up = [jnp.stack([v[:, at : at + wide] for v in by_far]) for at in (0, wide)]
+    gate, up = ffn_grad[:, :, :wide], ffn_grad[:, :, wide : 2 * wide]
     pieces = []
     for flip in range(2):
         pairs = [(c, ((c % 2) ^ flip) * count + c // 2) for c in range(n_ctx)]
         pieces.append(lax.ppermute(jnp.where(odd == flip, gate, up), CTX, pairs))
-    down_grad = jnp.concatenate(
-        [value[:, 2 * wide : 2 * wide + share].T.astype(F32) for value in by_far]
-    )
+    down_grad = ffn_grad[:, :, 2 * wide : 2 * wide + share].transpose(0, 2, 1)
+    down_grad = down_grad.reshape(n_far * share, quarter).astype(F32)
     upper = position >= count
     columns = [jnp.where(upper, pieces[1], pieces[0]), jnp.where(upper, pieces[0], pieces[1])]
     own_gain = lax.dynamic_slice_in_dim(gain2, (far * n_near + near) * quarter, quarter)
@@ -532,8 +539,11 @@
         jnp.concatenate([columns[i][f][:, :share] for i in range(2) for f in range(n_far)], axis=1).astype(F32)
         * own_gain[:, None]
     )
-    attn_grad, sums = meet(attn_grad, sums)
+    sums, d_input, down_grad = meet(sums, d_input, down_grad)
+    sums = exchange(sums, EVERY)
+    sums, attn_grad, output, gateup_grad = meet(sums, attn_grad, output, gateup_grad)
     sums = jnp.sum(sums, axis=0)
+    attn_grad = attn_grad.astype(F32)
     own_gain = lax.dynamic_slice_in_dim(gain1, (far * n_near + near) * quarter, quarter)
     qkv_grad = attn_grad[:, : q_cols + kv_cols] * own_gain[:, None]
     out_grad = attn_grad[:, q_cols + kv_cols :].T

time: 872 us -> 837 us (0.960)
  other arithmetic: 117 us -> 98.3 us
  waiting for transfers between devices: 380 us -> 365 us
  matrix products: 107 us -> 93.9 us
  starting transfers between devices: 76.8 us -> 87.9 us
    ppermute x23 -> x24, waiting for transfers between devices: 89.8 us -> 181 us  [send(): lax.ppermute(value, axis, [(i, (i + step) % count) for i in range(count)])]
    all_gather x1 -> x0, waiting for transfers between devices: 67.2 us -> none  [per_device(): by_far = lax.all_gather(give, 'far', axis=0)]
    all_to_all x7 -> x9, waiting for transfers between devices: 162 us -> 135 us  [exchange(): return lax.all_to_all(value, axes, split_axis=0, concat_axis=0, tiled=True)]
    all_gather x1, waiting for transfers between devices: 13 us -> 1.61 us  [per_device(): full_out = lax.all_gather(out_rows, CTX, axis=0, tiled=True)]
    dot_general x5 -> x4, matrix products: 41.4 us -> 31.2 us  [dot_first(): lax.dot_general(left, right, (((0,), (0,)), ((), ())), preferred_element_...]
    all_to_all x7 -> x9, starting transfers between devices: 32.4 us -> 41.4 us  [exchange(): return lax.all_to_all(value, axes, split_axis=0, concat_axis=0, tiled=True)]
    unnamed x123 -> x132, local copies, waits for them, and re-layouts: 27.7 us -> 30.4 us
  transfers between devices with their start and end apart: 53 -> 55, of which waited for: 17 -> 24; matrix products, arithmetic and copies ran while one was open for 36% -> 32% of each run, Pallas kernels for 5% -> 5%
where the time goes in v3:
time: 837 us; the launch traced here: 825 us
  waiting for transfers between devices  365 us (44%)
  local copies, waits for them, and re-layouts  120 us (14%)
  other arithmetic  98.3 us (12%)
  matrix products  93.9 us (11%)
  starting transfers between devices  87.9 us (11%)
  Pallas kernels  43.8 us (5%)
  between operations  15.5 us (2%)
    ppermute x24, waiting for transfers between devices, send(): lax.ppermute(value, axis, [(i, (i + step) % count) for i in range(count)])  181 us
    all_to_all x9, waiting for transfers between devices, exchange(): return lax.all_to_all(value, axes, split_axis=0, concat_axis=0, tiled=True)  135 us
    ppermute x14, waiting for transfers between devices, send_cross(): return lax.ppermute(value, CTX, pairs)  47.9 us
    all_to_all x9, starting transfers between devices, exchange(): return lax.all_to_all(value, axes, split_axis=0, concat_axis=0, tiled=True)  41.4 us
    pallas_call x2, Pallas kernels, feed_forward(): pl.pallas_call(functools.partial(middle_kernel, share, wide), out_shape=(...  36.5 us
    dot_general x4, matrix products, dot_first(): lax.dot_general(left, right, (((0,), (0,)), ((), ())), preferred_element_...  31.2 us
    unnamed x132, local copies, waits for them, and re-layouts  30.4 us
    dot_general x4, matrix products, dot_last(): lax.dot_general(left, right, (((1,), (1,)), ((), ())), preferred_element_...  27.9 us
  transfers between devices with their start and end apart: 55, of which 24 were waited for; matrix products, arithmetic and copies ran while one was open for 32% of the time, Pallas kernels for 5%

profile of v3, /device:TPU:0, one launch (start us, length us, event | category | flops | bytes accessed | tf_op | source)
XLA Modules:
  0.0 825.0 jit_solution(18287107072451694971)
XLA Ops:
  19.7 6.2 all-to-all-start
  29.9 5.4 reshape.484
  39.6 13.5 %collective-permute-done.1 = bf16[1,96,2560]{2,1,0:T(8,128)(2,1)} collective-permute-done((bf16[1,96,2560]{2,1,0:T(8,128)(2,1)}, bf16[1,96,2560]{2,1,0:T(8,128)(2,1)}, u32[]{:S(2)}, u32[]{:S(2)}) %collective-permute-start.1) | collective-permute-done | bytes 491552 | tf_op jit(solution)/shard_map/ppermute | solution.py:42
  53.1 52.1 %collective-permute-done.3 = bf16[240,2560]{1,0:T(8,128)(2,1)} collective-permute-done((bf16[240,2560]{1,0:T(8,128)(2,1)}, bf16[240,2560]{1,0:T(8,128)(2,1)}, u32[]{:S(2)}, u32[]{:S(2)}) %collective-permute-start.3) | collective-permute-done | bytes 1228832 | tf_op jit(solution)/shard_map/ppermute | solution.py:42
  113.3 6.3 all-to-all-start.1
  122.6 5.8 fusion.96
  130.0 22.0 %all-to-all-done.1 = bf16[16,80,480]{2,1,0:T(8,128)(2,1)S(1)} async-done(((bf16[16,80,480]{2,1,0:T(8,128)(2,1)}), bf16[16,80,480]{2,1,0:T(8,128)(2,1)S(1)}, u32[]{:S(2)}, u32[]{:S(2)}) %all-to-all-start.1) | async-done | bytes 1228832 | tf_op jit(solution)/shard_map/all_to_all | solution.py:182
  158.9 36.9 %all-to-all-done.2 = bf16[8,128,840]{1,2,0:T(8,128)(2,1)S(1)} async-done(((bf16[8,128,840]{1,2,0:T(8,128)(2,1)}), bf16[8,128,840]{1,2,0:T(8,128)(2,1)S(1)}, u32[]{:S(2)}, u32[]{:S(2)}) %all-to-all-start.2) | async-done | bytes 1720352 | tf_op jit(solution)/shard_map/all_to_all | solution.py:182
  210.3 12.2 %all-to-all-done.3 = bf16[16,48,480]{2,1,0:T(8,128)(2,1)S(1)} async-done(((bf16[16,48,480]{2,1,0:T(8,128)(2,1)}), bf16[16,48,480]{2,1,0:T(8,128)(2,1)S(1)}, u32[]{:S(2)}, u32[]{:S(2)}) %all-to-all-start.3) | async-done | bytes 737312 | tf_op jit(solution)/shard_map/all_to_all | solution.py:182
  234.0 7.0 multiply_reduce_fusion.1
  242.2 6.0 all-to-all-done.4
  258.5 25.3 %collective-permute-done.9 = bf16[16,48,480]{2,1,0:T(8,128)(2,1)S(1)} collective-permute-done((bf16[16,48,480]{2,1,0:T(8,128)(2,1)S(1)}, bf16[16,48,480]{2,1,0:T(8,128)(2,1)S(1)}, u32[]{:S(2)}, u32[]{:S(2)}) %collective-permute-start.9) | collective-permute-done | bytes 737312 | tf_op jit(solution)/shard_map/ppermute | solution.py:42
  289.6 12.3 %collective-permute-done.12 = bf16[16,32,480]{2,1,0:T(8,128)(2,1)S(1)} collective-permute-done((bf16[16,32,480]{2,1,0:T(8,128)(2,1)}, bf16[16,32,480]{2,1,0:T(8,128)(2,1)S(1)}, u32[]{:S(2)}, u32[]{:S(2)}) %collective-permute-start.12) | collective-permute-done | bytes 491552 | tf_op jit(solution)/shard_map/ppermute | solution.py:42
  313.1 9.8 %convolution_convert_fusion.7 = bf16[2048,480]{0,1:T(8,128)(2,1)} fusion(bf16[2048,2560]{1,0:T(8,128)(2,1)} %all-gather.8.cloned.1.call-done, bf16[480,2560]{1,0:T(8,128)(2,1)} %bitcast.430), kind=kOutput, calls=%fused_computation.40 | convolution fusion | flops 5034147840 | bytes 14909440 | tf_op jit(solution)/shard_map/dot_general | solution.py:33
  333.2 5.2 pad_maximum_fusion.1.hidden_ref
  341.1 18.4 %feed_forward.2 = (bf16[1024,512]{1,0:T(8,128)(2,1)S(1)}, bf16[1024,1024]{1,0:T(8,128)(2,1)S(1)}, bf16[512,2560]{1,0:T(8,128)(2,1)}, bf16[512,2560]{1,0:T(8,128)(2,1)}) custom-call(s32[8]{0:T(128)S(1)} %get-tuple-element.285.order_ref, bf16[1024,2560]{1,0:T(8,128)(2,1)} %pad_maximum_fusion.1.hidden_ref, bf16[16,128,480]{2,1,0:T(8,128)(2,1)S(1)} %bitcast.385, ...), custom_call_target="tpu_custom_call" | custom-call | flops 10066329600 | bytes 15400960 | tf_op jit(solution)/shard_map/feed_forward/pallas_call | solution.py:230
  367.5 5.3 pad_maximum_fusion.2.hidden_ref
  372.8 18.1 %feed_forward.3 = (bf16[1024,512]{1,0:T(8,128)(2,1)S(1)}, bf16[1024,1024]{1,0:T(8,128)(2,1)S(1)}, bf16[512,2560]{1,0:T(8,128)(2,1)}, bf16[512,2560]{1,0:T(8,128)(2,1)}) custom-call(s32[8]{0:T(128)S(1)} %get-tuple-element.284.order_ref, bf16[1024,2560]{1,0:T(8,128)(2,1)} %pad_maximum_fusion.2.hidden_ref, bf16[16,128,480]{2,1,0:T(8,128)(2,1)S(1)} %bitcast.387, ...), custom_call_target="tpu_custom_call" | custom-call | flops 10066329600 | bytes 15400960 | tf_op jit(solution)/shard_map/feed_forward/pallas_call | solution.py:230
  420.9 5.4 convolution_convert_fusion.1
  426.3 5.3 convolution_convert_fusion
  437.1 12.3 %convolution_convert_fusion.2 = bf16[2560,1024]{1,0:T(8,128)(2,1)S(1)} fusion(bf16[2048,2560]{1,0:T(8,128)(2,1)S(1)} %bitcast.417, bf16[1024,1024]{1,0:T(8,128)(2,1)S(1)} %copy-done.5, bf16[1024,1024]{1,0:T(8,128)(2,1)S(1)} %copy-done.3), kind=kOutput, calls=%fused_computation.3 | convolution fusion | flops 10748428288 | bytes 19922944 | tf_op jit(solution)/shard_map/dot_general | solution.py:37
  458.3 8.8 %convolution_convert_fusion.5 = bf16[2560,512]{1,0:T(8,128)(2,1)S(1)} fusion(bf16[2048,2560]{1,0:T(8,128)(2,1)} %all-gather.8.cloned.1.call-done, bf16[2048,512]{1,0:T(8,128)(2,1)S(1)} %bitcast.437), kind=kOutput, calls=%fused_computation.27 | convolution fusion | flops 5370019840 | bytes 15204352 | tf_op jit(solution)/shard_map/dot_general | solution.py:37
  475.1 30.1 %collective-permute-done.25 = bf16[128,2560]{1,0:T(8,128)(2,1)S(1)} collective-permute-done((bf16[128,2560]{1,0:T(8,128)(2,1)S(1)}, bf16[128,2560]{1,0:T(8,128)(2,1)S(1)}, u32[]{:S(2)}, u32[]{:S(2)}) %collective-permute-start.25) | collective-permute-done | bytes 655392 | tf_op jit(solution)/shard_map/ppermute | solution.py:42
  515.3 10.3 %convolution_convert_fusion.6 = bf16[128,2560]{1,0:T(8,128)(2,1)} fusion(bf16[128,2560]{1,0:T(8,128)(2,1)S(1)} %convert_element_type.398, bf16[2560,2560]{1,0:T(8,128)(2,1)} %all-gather.6.cloned.1.call-done), kind=kOutput, calls=%fused_computation.37 | convolution fusion | flops 1678049280 | bytes 14417920 | tf_op jit(solution)/shard_map/dot_general | solution.py:33
  541.5 5.7 collective-permute-done.29
  562.9 24.8 %collective-permute-done.30 = bf16[128,2560]{1,0:T(8,128)(2,1)} collective-permute-done((bf16[128,2560]{1,0:T(8,128)(2,1)S(1)}, bf16[128,2560]{1,0:T(8,128)(2,1)}, u32[]{:S(2)}, u32[]{:S(2)}) %collective-permute-start.30) | collective-permute-done | bytes 655392 | tf_op jit(solution)/shard_map/ppermute | solution.py:62
  615.9 5.5 all-to-all-start.7
  631.4 6.1 multiply_reduce_fusion
  651.5 57.5 %all-to-all-done.7 = bf16[2,640,1536]{2,1,0:T(8,128)(2,1)} async-done(((bf16[2,640,1536]{2,1,0:T(8,128)(2,1)}), bf16[2,640,1536]{2,1,0:T(8,128)(2,1)}, u32[]{:S(2)}, u32[]{:S(2)}) %all-to-all-start.7) | async-done | bytes 3932192 | tf_op jit(solution)/shard_map/all_to_all | solution.py:182
  709.1 6.2 copy.144
  734.3 11.3 %collective-permute-start.40 = (bf16[2,640,512]{2,1,0:T(8,128)(2,1)}, bf16[2,640,512]{2,1,0:T(8,128)(2,1)}, u32[]{:S(2)}, u32[]{:S(2)}) collective-permute-start(bf16[2,640,512]{2,1,0:T(8,128)(2,1)} %get-tuple-element.256), channel_id=1, source_target_pairs={{0,0},{4,16},{8,4},{12,20},{16,8},{20,24},{24,12},{28,28},{1,1},{5... | collective-permute-start | bytes 3932168 | tf_op jit(solution)/shard_map/ppermute | solution.py:532
  755.2 43.2 %collective-permute-done.38 = bf16[128,2560]{1,0:T(8,128)(2,1)} collective-permute-done((bf16[128,2560]{1,0:T(8,128)(2,1)}, bf16[128,2560]{1,0:T(8,128)(2,1)}, u32[]{:S(2)}, u32[]{:S(2)}) %collective-permute-start.38) | collective-permute-done | bytes 655392 | tf_op jit(solution)/shard_map/ppermute | solution.py:42
  (420 shorter events, 309.4 us)
Async XLA Ops:
  7.2 98.0 %all-gather.4.cloned.1.call-start = ((), (), s32[]{:S(2)}) async-start(), calls=%async_computation.11 | async-start | bytes 5898240 | tf_op jit(solution)/shard_map/all_gather | solution.py:324
  11.7 27.9 %collective-permute-start = (bf16[1,96,2560]{2,1,0:T(8,128)(2,1)}, bf16[1,96,2560]{2,1,0:T(8,128)(2,1)}, u32[]{:S(2)}, u32[]{:S(2)}) collective-permute-start(bf16[1,96,2560]{2,1,0:T(8,128)(2,1)} %maximum_bitcast_fusion.6), channel_id=1, source_target_pairs={{0,1},{1,0},{2,3},{3,2},{4,5},{5,4},{6,7},{7,6},{8,9},{9,8},{10,11... | collective-permute-start | bytes 1474568 | tf_op jit(solution)/shard_map/ppermute | solution.py:42
  14.7 38.4 %collective-permute-start.1 = (bf16[1,96,2560]{2,1,0:T(8,128)(2,1)}, bf16[1,96,2560]{2,1,0:T(8,128)(2,1)}, u32[]{:S(2)}, u32[]{:S(2)}) collective-permute-start(bf16[1,96,2560]{2,1,0:T(8,128)(2,1)} %maximum_bitcast_fusion.6), channel_id=1, source_target_pairs={{0,2},{2,0},{1,3},{3,1},{4,6},{6,4},{5,7},{7,5},{8,10},{10,8},{9,1... | collective-permute-start | bytes 1474568 | tf_op jit(solution)/shard_map/ppermute | solution.py:42
  17.3 35.9 %collective-permute-start.2 = (bf16[1,96,2560]{2,1,0:T(8,128)(2,1)}, bf16[1,96,2560]{2,1,0:T(8,128)(2,1)}, u32[]{:S(2)}, u32[]{:S(2)}) collective-permute-start(bf16[1,96,2560]{2,1,0:T(8,128)(2,1)} %maximum_bitcast_fusion.6), channel_id=1, source_target_pairs={{0,3},{1,2},{2,1},{3,0},{4,7},{5,6},{6,5},{7,4},{8,11},{9,10},{10,... | collective-permute-start | bytes 1474568 | tf_op jit(solution)/shard_map/ppermute | solution.py:323
  19.7 85.5 %all-to-all-start = ((bf16[32,80,384]{2,1,0:T(8,128)(2,1)}), bf16[32,80,384]{2,1,0:T(8,128)(2,1)}, u32[]{:S(2)}, u32[]{:S(2)}) async-start(bf16[32,80,384]{2,1,0:T(8,128)(2,1)} %bitcast.11), calls=%async_computation | async-start | bytes 3932160 | tf_op jit(solution)/shard_map/all_to_all | solution.py:182
  25.9 198.2 %all-gather.6.cloned.1.call-start = ((), (), s32[]{:S(2)}) async-start(), calls=%async_computation.12 | async-start | bytes 14745600 | tf_op jit(solution)/shard_map/all_gather | solution.py:348
  25.9 79.3 %collective-permute-start.3 = (bf16[240,2560]{1,0:T(8,128)(2,1)}, bf16[240,2560]{1,0:T(8,128)(2,1)}, u32[]{:S(2)}, u32[]{:S(2)}) collective-permute-start(bf16[240,2560]{1,0:T(8,128)(2,1)} %param.19), channel_id=1, source_target_pairs={{0,1},{1,0},{2,3},{3,2},{4,5},{5,4},{6,7},{7,6},{8,9},{9,8},{10,11... | collective-permute-start | bytes 3686408 | tf_op jit(solution)/shard_map/ppermute | solution.py:42
  113.3 38.7 %all-to-all-start.1 = ((bf16[16,80,480]{2,1,0:T(8,128)(2,1)}), bf16[16,80,480]{2,1,0:T(8,128)(2,1)S(1)}, u32[]{:S(2)}, u32[]{:S(2)}) async-start(bf16[16,80,480]{2,1,0:T(8,128)(2,1)} %get-tuple-element.265), calls=%async_computation.1 | async-start | bytes 2621440 | tf_op jit(solution)/shard_map/all_to_all | solution.py:182
  153.1 42.8 %all-to-all-start.2 = ((bf16[8,128,840]{1,2,0:T(8,128)(2,1)}), bf16[8,128,840]{1,2,0:T(8,128)(2,1)S(1)}, u32[]{:S(2)}, u32[]{:S(2)}) async-start(bf16[8,128,840]{1,2,0:T(8,128)(2,1)} %pad_maximum_fusion.6), calls=%async_computation.2 | async-start | bytes 3440640 | tf_op jit(solution)/shard_map/all_to_all | solution.py:182
  156.8 53.5 %collective-permute-start.4 = (bf16[128,2560]{1,0:T(8,128)(2,1)}, bf16[128,2560]{1,0:T(8,128)(2,1)S(1)}, u32[]{:S(2)}, u32[]{:S(2)}) collective-permute-start(bf16[128,2560]{1,0:T(8,128)(2,1)} %bitcast.18), channel_id=1, source_target_pairs={{0,2},{2,0},{1,3},{3,1},{4,6},{6,4},{5,7},{7,5},{8,10},{10,8},{9,1... | collective-permute-start | bytes 1966088 | tf_op jit(solution)/shard_map/ppermute | solution.py:42
  156.9 53.4 %collective-permute-start.5 = (bf16[16,80,480]{2,1,0:T(8,128)(2,1)}, bf16[16,80,480]{2,1,0:T(8,128)(2,1)}, u32[]{:S(2)}, u32[]{:S(2)}) collective-permute-start(bf16[16,80,480]{2,1,0:T(8,128)(2,1)} %copy-done.17), channel_id=1, source_target_pairs={{0,1},{1,0},{2,3},{3,2},{4,5},{5,4},{6,7},{7,6},{8,9},{9,8},{10,11... | collective-permute-start | bytes 3686408 | tf_op jit(solution)/shard_map/ppermute | solution.py:42
  203.3 109.8 %all-gather.8.cloned.1.call-start = ((), (), s32[]{:S(2)}) async-start(), calls=%async_computation.13 | async-start | bytes 11796480 | tf_op jit(solution)/shard_map/all_gather | solution.py:389
  249.8 34.0 %collective-permute-start.9 = (bf16[16,48,480]{2,1,0:T(8,128)(2,1)S(1)}, bf16[16,48,480]{2,1,0:T(8,128)(2,1)S(1)}, u32[]{:S(2)}, u32[]{:S(2)}) collective-permute-start(bf16[16,48,480]{2,1,0:T(8,128)(2,1)S(1)} %all-to-all-done.3), channel_id=1, source_target_pairs={{0,1},{1,0},{2,3},{3,2},{4,5},{5,4},{6,7},{7,6},{8,9},{9,8},{10,11... | collective-permute-start | bytes 2211848 | tf_op jit(solution)/shard_map/ppermute | solution.py:42
  249.9 33.9 %collective-permute-start.8 = (bf16[128,2560]{1,0:T(8,128)(2,1)S(1)}, bf16[128,2560]{1,0:T(8,128)(2,1)S(1)}, u32[]{:S(2)}, u32[]{:S(2)}) collective-permute-start(bf16[128,2560]{1,0:T(8,128)(2,1)S(1)} %multiply_convert_fusion.1), channel_id=1, source_target_pairs={{0,2},{2,0},{1,3},{3,1},{4,6},{6,4},{5,7},{7,5},{8,10},{10,8},{9,1... | collective-permute-start | bytes 1966088 | tf_op jit(solution)/shard_map/ppermute | solution.py:42
  252.6 34.7 %collective-permute-start.7 = (bf16[256,2560]{1,0:T(8,128)(2,1)S(1)}, bf16[256,2560]{1,0:T(8,128)(2,1)S(1)}, u32[]{:S(2)}, u32[]{:S(2)}) collective-permute-start(bf16[256,2560]{1,0:T(8,128)(2,1)S(1)} %pad_maximum_fusion.8), channel_id=1, source_target_pairs={{0,8},{4,20},{8,0},{12,28},{16,24},{20,4},{24,16},{28,12},{1,9},{5... | collective-permute-start | bytes 3932168 | tf_op jit(solution)/shard_map/ppermute | solution.py:62
  359.5 32.7 %collective-permute-start.17 = (bf16[512,2560]{1,0:T(8,128)(2,1)}, bf16[512,2560]{1,0:T(8,128)(2,1)}, u32[]{:S(2)}, u32[]{:S(2)}) collective-permute-start(bf16[512,2560]{1,0:T(8,128)(2,1)} %get-tuple-element.168), channel_id=1, source_target_pairs={{0,4},{4,0},{1,5},{5,1},{2,6},{6,2},{3,7},{7,3},{8,12},{12,8},{9,1... | collective-permute-start | bytes 7864328 | tf_op jit(solution)/shard_map/ppermute | solution.py:42
  363.7 28.5 %all-to-all-start.5 = ((bf16[8,128,320]{1,2,0:T(8,128)(2,1)}), bf16[8,128,320]{1,2,0:T(8,128)(2,1)S(1)}, u32[]{:S(2)}, u32[]{:S(2)}) async-start(bf16[8,128,320]{1,2,0:T(8,128)(2,1)} %bitcast.58), calls=%async_computation.5 | async-start | bytes 1310720 | tf_op jit(solution)/shard_map/all_to_all | solution.py:182
  367.3 220.4 %reduce-scatter.5.cloned.1.call-start = ((), (), s32[]{:S(2)}) async-start(), calls=%async_computation.14 | async-start | bytes 11796480 | tf_op jit(solution)/shard_map/reduce_scatter | solution.py:463
  419.1 30.2 %collective-permute-start.22 = (bf16[256,2560]{1,0:T(8,128)(2,1)}, bf16[256,2560]{1,0:T(8,128)(2,1)}, u32[]{:S(2)}, u32[]{:S(2)}) collective-permute-start(bf16[256,2560]{1,0:T(8,128)(2,1)} %pad_maximum_fusion.12), channel_id=1, source_target_pairs={{0,8},{4,20},{8,0},{12,28},{16,24},{20,4},{24,16},{28,12},{1,9},{5... | collective-permute-start | bytes 3932168 | tf_op jit(solution)/shard_map/ppermute | solution.py:62
  473.2 32.0 %collective-permute-start.25 = (bf16[128,2560]{1,0:T(8,128)(2,1)S(1)}, bf16[128,2560]{1,0:T(8,128)(2,1)S(1)}, u32[]{:S(2)}, u32[]{:S(2)}) collective-permute-start(bf16[128,2560]{1,0:T(8,128)(2,1)S(1)} %fusion.39), channel_id=1, source_target_pairs={{0,2},{2,0},{1,3},{3,1},{4,6},{6,4},{5,7},{7,5},{8,10},{10,8},{9,1... | collective-permute-start | bytes 1966088 | tf_op jit(solution)/shard_map/ppermute | solution.py:42
  513.7 27.7 %collective-permute-start.28 = (bf16[256,2560]{1,0:T(8,128)(2,1)}, bf16[256,2560]{1,0:T(8,128)(2,1)}, u32[]{:S(2)}, u32[]{:S(2)}) collective-permute-start(bf16[256,2560]{1,0:T(8,128)(2,1)} %pad_maximum_fusion.13), channel_id=1, source_target_pairs={{0,8},{4,20},{8,0},{12,28},{16,24},{20,4},{24,16},{28,12},{1,9},{5... | collective-permute-start | bytes 3932168 | tf_op jit(solution)/shard_map/ppermute | solution.py:62
  547.1 40.5 %all-to-all-start.6 = ((bf16[8,128,832]{1,2,0:T(8,128)(2,1)}), bf16[8,128,832]{1,2,0:T(8,128)(2,1)}, u32[]{:S(2)}, u32[]{:S(2)}) async-start(bf16[8,128,832]{1,2,0:T(8,128)(2,1)} %pad_maximum_fusion.7), calls=%async_computation.6 | async-start | bytes 3407872 | tf_op jit(solution)/shard_map/all_to_all | solution.py:182
  552.8 34.9 %collective-permute-start.30 = (bf16[128,2560]{1,0:T(8,128)(2,1)S(1)}, bf16[128,2560]{1,0:T(8,128)(2,1)}, u32[]{:S(2)}, u32[]{:S(2)}) collective-permute-start(bf16[128,2560]{1,0:T(8,128)(2,1)S(1)} %slice.374), channel_id=1, source_target_pairs={{0,16},{4,12},{8,24},{12,4},{16,0},{20,28},{24,8},{28,20},{1,17},{... | collective-permute-start | bytes 1966088 | tf_op jit(solution)/shard_map/ppermute | solution.py:62
  561.4 63.1 %collective-permute-start.33 = (bf16[512,2560]{1,0:T(8,128)(2,1)}, bf16[512,2560]{1,0:T(8,128)(2,1)}, u32[]{:S(2)}, u32[]{:S(2)}) collective-permute-start(bf16[512,2560]{1,0:T(8,128)(2,1)} %pad_maximum_fusion.4), channel_id=1, source_target_pairs={{0,8},{4,20},{8,0},{12,28},{16,24},{20,4},{24,16},{28,12},{1,9},{5... | collective-permute-start | bytes 7864328 | tf_op jit(solution)/shard_map/ppermute | solution.py:62
  615.9 93.2 %all-to-all-start.7 = ((bf16[2,640,1536]{2,1,0:T(8,128)(2,1)}), bf16[2,640,1536]{2,1,0:T(8,128)(2,1)}, u32[]{:S(2)}, u32[]{:S(2)}) async-start(bf16[2,640,1536]{2,1,0:T(8,128)(2,1)} %bitcast.410), calls=%async_computation.8 | async-start | bytes 7864320 | tf_op jit(solution)/shard_map/all_to_all | solution.py:182
  621.4 191.6 %reduce-scatter.7.cloned.1.call-start = ((), (), s32[]{:S(2)}) async-start(), calls=%async_computation.15 | async-start | bytes 4915200
  644.3 64.7 %collective-permute-start.36 = (bf16[256,2560]{1,0:T(8,128)(2,1)}, bf16[256,2560]{1,0:T(8,128)(2,1)}, u32[]{:S(2)}, u32[]{:S(2)}) collective-permute-start(bf16[256,2560]{1,0:T(8,128)(2,1)} %pad_maximum_fusion.14), channel_id=1, source_target_pairs={{0,8},{4,20},{8,0},{12,28},{16,24},{20,4},{24,16},{28,12},{1,9},{5... | collective-permute-start | bytes 3932168 | tf_op jit(solution)/shard_map/ppermute | solution.py:62
  719.6 26.0 %collective-permute-start.37 = (bf16[128,2560]{1,0:T(8,128)(2,1)}, bf16[128,2560]{1,0:T(8,128)(2,1)S(1)}, u32[]{:S(2)}, u32[]{:S(2)}) collective-permute-start(bf16[128,2560]{1,0:T(8,128)(2,1)} %slice.404), channel_id=1, source_target_pairs={{0,4},{4,0},{1,5},{5,1},{2,6},{6,2},{3,7},{7,3},{8,12},{12,8},{9,1... | collective-permute-start | bytes 1966088 | tf_op jit(solution)/shard_map/ppermute | solution.py:42
  724.3 74.1 %collective-permute-start.38 = (bf16[128,2560]{1,0:T(8,128)(2,1)}, bf16[128,2560]{1,0:T(8,128)(2,1)}, u32[]{:S(2)}, u32[]{:S(2)}) collective-permute-start(bf16[128,2560]{1,0:T(8,128)(2,1)} %slice.615), channel_id=1, source_target_pairs={{0,2},{2,0},{1,3},{3,1},{4,6},{6,4},{5,7},{7,5},{8,10},{10,8},{9,1... | collective-permute-start | bytes 1966088 | tf_op jit(solution)/shard_map/ppermute | solution.py:42
  734.3 68.0 %collective-permute-start.40 = (bf16[2,640,512]{2,1,0:T(8,128)(2,1)}, bf16[2,640,512]{2,1,0:T(8,128)(2,1)}, u32[]{:S(2)}, u32[]{:S(2)}) collective-permute-start(bf16[2,640,512]{2,1,0:T(8,128)(2,1)} %get-tuple-element.256), channel_id=1, source_target_pairs={{0,0},{4,16},{8,4},{12,20},{16,8},{20,24},{24,12},{28,28},{1,1},{5... | collective-permute-start | bytes 3932168 | tf_op jit(solution)/shard_map/ppermute | solution.py:532
  745.6 56.7 %collective-permute-start.39 = (bf16[2,640,512]{2,1,0:T(8,128)(2,1)}, bf16[2,640,512]{2,1,0:T(8,128)(2,1)}, u32[]{:S(2)}, u32[]{:S(2)}) collective-permute-start(bf16[2,640,512]{2,1,0:T(8,128)(2,1)} %get-tuple-element.257), channel_id=1, source_target_pairs={{0,16},{4,0},{8,20},{12,4},{16,24},{20,8},{24,28},{28,12},{1,17},{... | collective-permute-start | bytes 3932168 | tf_op jit(solution)/shard_map/ppermute | solution.py:532
  751.2 49.7 %all-to-all-start.8 = ((f32[32,1,240]{2,1,0:T(1,128)}), f32[32,1,240]{2,1,0:T(1,128)S(1)}, u32[]{:S(2)}, u32[]{:S(2)}) async-start(f32[32,1,240]{2,1,0:T(1,128)} %reshape.560), calls=%async_computation.9 | async-start | bytes 65536 | tf_op jit(solution)/shard_map/all_to_all | solution.py:182
  (85 other events, 818.0 us)
Sparse Core Ops, SparseCore 0:
  10.9 54.8 all-gather.3
  111.7 112.3 all-gather.5
  226.5 77.0 all-gather.7
  471.8 108.3 reduce-scatter.4
  715.4 92.7 reduce-scatter.6

commit v4 on v3

--- a/solution.py
+++ b/solution.py
@@ -260,6 +260,84 @@
         ),
         name="feed_forward",
     )(order, hidden, d_inner, d_inner, w_gate, w_up)
+
+
+def gradient_kernel(both, hidden_ref, more_ref, final_ref, d_gu_ref, d_more_ref, inner_ref, grad_ref):
+    grad_ref[0, 0, :, :both] = (
+        dot_first(hidden_ref[...], d_gu_ref[...]) + dot_first(more_ref[...], d_more_ref[...])
+    ).astype(BF16)
+    grad_ref[0, 0, :, both:] = dot_first(final_ref[...], inner_ref[...]).astype(BF16)
+
+
+def weight_gradients(hidden, d_gu, final, inner, n_far, n_near):
+    length, width = hidden[0].shape
+    quarter = width // (n_far * n_near)
+    both, wide = d_gu[0].shape[1], inner.shape[1]
+    rows = quarter if 16 * length * quarter <= 2**24 else 128
+    steps = quarter // rows
+
+    def columns(n, f, k):
+        return (0, (f * n_near + n) * steps + k)
+
+    def whole(value):
+        return pl.BlockSpec(value.shape, lambda n, f, k: (0, 0), pipeline_mode=pl.Buffered(1))
+
+    return pl.pallas_call(
+        functools.partial(gradient_kernel, both),
+        out_shape=jax.ShapeDtypeStruct((n_near, n_far, quarter, both + wide), BF16),
+        grid=(n_near, n_far, steps),
+        in_specs=[
+            pl.BlockSpec((length, rows), columns),
+            pl.BlockSpec((length, rows), columns),
+            pl.BlockSpec((final.shape[0], rows), columns),
+            whole(d_gu[0]),
+            whole(d_gu[1]),
+            whole(inner),
+        ],
+        out_specs=pl.BlockSpec((1, 1, rows, both + wide), lambda n, f, k: (n, f, k, 0)),
+        compiler_params=pltpu.CompilerParams(vmem_limit_bytes=48 * 2**20),
+        cost_estimate=pl.CostEstimate(
+            flops=4 * length * width * (both + wide),
+            bytes_accessed=8 * length * width + 2 * width * (both + wide),
+            transcendentals=0,
+        ),
+        name="weight_gradients",
+    )(*hidden, final, *d_gu, inner)
+
+
+def two_gradients_kernel(left_ref, d_left_ref, right_ref, d_right_ref, grad_ref):
+    split = d_left_ref.shape[1]
+    grad_ref[:, :split] = dot_first(left_ref[...], d_left_ref[...]).astype(BF16)
+    grad_ref[:, split:] = dot_first(right_ref[...], d_right_ref[...]).astype(BF16)
+
+
+def two_gradients(left, d_left, right, d_right):
+    length, width = left.shape
+    rows = 256 if length <= 1024 else 128
+    total = d_left.shape[1] + d_right.shape[1]
+
+    def whole(value):
+        return pl.BlockSpec(value.shape, lambda n: (0, 0), pipeline_mode=pl.Buffered(1))
+
+    return pl.pallas_call(
+        two_gradients_kernel,
+        out_shape=jax.ShapeDtypeStruct((width, total), BF16),
+        grid=(width // rows,),
+        in_specs=[
+            pl.BlockSpec((length, rows), lambda n: (0, n)),
+            whole(d_left),
+            pl.BlockSpec((length, rows), lambda n: (0, n)),
+            whole(d_right),
+        ],
+        out_specs=pl.BlockSpec((rows, total), lambda n: (n, 0)),
+        compiler_params=pltpu.CompilerParams(vmem_limit_bytes=32 * 2**20),
+        cost_estimate=pl.CostEstimate(
+            flops=2 * length * width * total,
+            bytes_accessed=4 * length * width + 2 * width * total,
+            transcendentals=0,
+        ),
+        name="two_gradients",
+    )(left, d_left, right, d_right)
 
 
 def norm_scale(value):
@@ -445,20 +523,19 @@
     )
     t_sides = scatter_2(t_keep, t_came, t_back, block_len)
 
-    gu_grad = dot_first(jnp.concatenate([hidden_m, hidden_t]), jnp.concatenate([d_gu_m, d_gu_t]))
-    gu_grad, t_sides, m_sides, t_keep, t_came, inner_rows = meet(
-        gu_grad.astype(BF16), t_sides, m_sides, t_keep, t_came, inner_rows
-    )
+    ffn_grad = weight_gradients(
+        (hidden_m, hidden_t),
+        (d_gu_m, d_gu_t),
+        final_rows,
+        inner_rows.reshape(2 * length, wide),
+        n_far,
+        n_near,
+    )
+    ffn_grad, t_sides, m_sides, t_keep, t_came = meet(ffn_grad, t_sides, m_sides, t_keep, t_came)
     t_other = scatter_3(t_sides)
     m_other = scatter_3(m_sides)
     theirs = scatter_4(t_keep, t_came, t_sides, t_other, block_len).astype(BF16)
-    theirs, inner_rows = meet(theirs, inner_rows)
     theirs = send(theirs, "far", 1)
-    down_grad = dot_first(final_rows, inner_rows.reshape(2 * length, wide)).astype(BF16)
-    ffn_grad = [value.reshape(n_far, n_near, quarter, -1) for value in (gu_grad, down_grad)]
-    ffn_grad = jnp.stack(
-        [jnp.concatenate([value[:, n] for value in ffn_grad], axis=2) for n in range(n_near)]
-    )
     m_other, theirs = meet(m_other, theirs)
     ffn_grad = lax.psum_scatter(ffn_grad, "near", scatter_dimension=0, tiled=True)
     d_hidden2 = scatter_4(m_keep, m_came, m_sides, m_other, block_len) + theirs.astype(F32)
@@ -508,10 +585,9 @@
     e_keep, e_came, l_halves, o_sides, d_qkv = meet(e_keep, e_came, l_halves, o_sides, d_qkv)
     e_back = scatter_1(e_keep, e_came, block_len)
     o_other = scatter_3(o_sides)
-    out_grad = dot_first(gather_all(l_pair, l_halves), mixed_cols)
-    qkv_grad = dot_first(hidden1, d_qkv)
-    d_gain1 = jnp.sum(qkv_grad * w_qkv.astype(F32), axis=1) / gain1
-    attn_grad = jnp.concatenate([qkv_grad.astype(BF16), out_grad.astype(BF16)], axis=1)
+    attn_grad = two_gradients(hidden1, d_qkv, gather_all(l_pair, l_halves), mixed_cols)
+    d_gain1 = attn_grad[:, : q_cols + kv_cols].astype(F32) * w_qkv.astype(F32)
+    d_gain1 = jnp.sum(d_gain1, axis=1) / gain1
     e_back, o_other, out_keep, o_came = meet(e_back, o_other, out_keep, o_came)
     e_sides = scatter_2(e_keep, e_came, e_back, block_len)
     sums = jnp.stack([d_gain1, d_bias, d_gain2]).reshape(3, n_all, rows).transpose(1, 0, 2)

time: 837 us -> 803 us (0.959)
  matrix products: 93.9 us -> 61.1 us
  Pallas kernels: 43.8 us -> 74.1 us
  local copies, waits for them, and re-layouts: 120 us -> 97.5 us
    dot_general x4 -> x0, matrix products: 31.2 us -> none  [dot_first(): lax.dot_general(left, right, (((0,), (0,)), ((), ())), preferred_element_...]
    pallas_call x0 -> x2, Pallas kernels: none -> 30.5 us  [the longest x1 22.2 us: weight_gradients(): pl.pallas_call(functools.partial(gradient_kernel, both), out_shape=jax.Sh...]
    unnamed x132 -> x113, local copies, waits for them, and re-layouts: 30.4 us -> 24.7 us
  transfers between devices with their start and end apart: 55 -> 55, of which waited for: 24 -> 23; matrix products, arithmetic and copies ran while one was open for 32% -> 28% of each run, Pallas kernels for 5% -> 9%
where the time goes in v4:
time: 803 us; the launch traced here: 791 us
  waiting for transfers between devices  359 us (45%)
  local copies, waits for them, and re-layouts  97.5 us (12%)
  other arithmetic  95.9 us (12%)
  starting transfers between devices  88.6 us (11%)
  Pallas kernels  74.1 us (9%)
  matrix products  61.1 us (8%)
  between operations  15.4 us (2%)
    ppermute x24, waiting for transfers between devices, send(): lax.ppermute(value, axis, [(i, (i + step) % count) for i in range(count)])  179 us
    all_to_all x9, waiting for transfers between devices, exchange(): return lax.all_to_all(value, axes, split_axis=0, concat_axis=0, tiled=True)  128 us
    ppermute x14, waiting for transfers between devices, send_cross(): return lax.ppermute(value, CTX, pairs)  49.3 us
    all_to_all x9, starting transfers between devices, exchange(): return lax.all_to_all(value, axes, split_axis=0, concat_axis=0, tiled=True)  42.2 us
    pallas_call x2, Pallas kernels, feed_forward(): pl.pallas_call(functools.partial(middle_kernel, share, wide), out_shape=(...  36.2 us
    dot_general x4, matrix products, dot_last(): lax.dot_general(left, right, (((1,), (1,)), ((), ())), preferred_element_...  27.3 us
    unnamed x113, local copies, waits for them, and re-layouts  24.7 us
    dot_general x4, matrix products, dot(): return jnp.dot(left, right, preferred_element_type=F32)  23.4 us
  transfers between devices with their start and end apart: 55, of which 23 were waited for; matrix products, arithmetic and copies ran while one was open for 28% of the time, Pallas kernels for 9%

profile of v4, /device:TPU:0, one launch (start us, length us, event | category | flops | bytes accessed | tf_op | source)
XLA Modules:
  0.0 791.4 jit_solution(11845950771434463399)
XLA Ops:
  19.7 6.2 all-to-all-start
  29.9 5.4 reshape.478
  39.6 13.5 %collective-permute-done.1 = bf16[1,96,2560]{2,1,0:T(8,128)(2,1)} collective-permute-done((bf16[1,96,2560]{2,1,0:T(8,128)(2,1)}, bf16[1,96,2560]{2,1,0:T(8,128)(2,1)}, u32[]{:S(2)}, u32[]{:S(2)}) %collective-permute-start.1) | collective-permute-done | bytes 491552 | tf_op jit(solution)/shard_map/ppermute | solution.py:42
  53.1 52.1 %collective-permute-done.3 = bf16[240,2560]{1,0:T(8,128)(2,1)} collective-permute-done((bf16[240,2560]{1,0:T(8,128)(2,1)}, bf16[240,2560]{1,0:T(8,128)(2,1)}, u32[]{:S(2)}, u32[]{:S(2)}) %collective-permute-start.3) | collective-permute-done | bytes 1228832 | tf_op jit(solution)/shard_map/ppermute | solution.py:42
  113.3 6.3 all-to-all-start.1
  122.6 5.8 fusion.80
  130.0 21.9 %all-to-all-done.1 = bf16[16,80,480]{2,1,0:T(8,128)(2,1)S(1)} async-done(((bf16[16,80,480]{2,1,0:T(8,128)(2,1)}), bf16[16,80,480]{2,1,0:T(8,128)(2,1)S(1)}, u32[]{:S(2)}, u32[]{:S(2)}) %all-to-all-start.1) | async-done | bytes 1228832 | tf_op jit(solution)/shard_map/all_to_all | solution.py:182
  159.0 37.0 %all-to-all-done.2 = bf16[8,128,840]{1,2,0:T(8,128)(2,1)S(1)} async-done(((bf16[8,128,840]{1,2,0:T(8,128)(2,1)}), bf16[8,128,840]{1,2,0:T(8,128)(2,1)S(1)}, u32[]{:S(2)}, u32[]{:S(2)}) %all-to-all-start.2) | async-done | bytes 1720352 | tf_op jit(solution)/shard_map/all_to_all | solution.py:182
  209.5 12.5 %all-to-all-done.3 = bf16[16,48,480]{2,1,0:T(8,128)(2,1)} async-done(((bf16[16,48,480]{2,1,0:T(8,128)(2,1)}), bf16[16,48,480]{2,1,0:T(8,128)(2,1)}, u32[]{:S(2)}, u32[]{:S(2)}) %all-to-all-start.3) | async-done | bytes 737312 | tf_op jit(solution)/shard_map/all_to_all | solution.py:182
  234.0 7.0 multiply_reduce_fusion.1
  242.2 6.7 all-to-all-done.4
  259.2 25.5 %collective-permute-done.9 = bf16[16,48,480]{2,1,0:T(8,128)(2,1)S(1)} collective-permute-done((bf16[16,48,480]{2,1,0:T(8,128)(2,1)}, bf16[16,48,480]{2,1,0:T(8,128)(2,1)S(1)}, u32[]{:S(2)}, u32[]{:S(2)}) %collective-permute-start.9) | collective-permute-done | bytes 737312 | tf_op jit(solution)/shard_map/ppermute | solution.py:42
  291.3 11.3 %collective-permute-done.12 = bf16[16,32,480]{2,1,0:T(8,128)(2,1)S(1)} collective-permute-done((bf16[16,32,480]{2,1,0:T(8,128)(2,1)}, bf16[16,32,480]{2,1,0:T(8,128)(2,1)S(1)}, u32[]{:S(2)}, u32[]{:S(2)}) %collective-permute-start.12) | collective-permute-done | bytes 491552 | tf_op jit(solution)/shard_map/ppermute | solution.py:42
  311.9 9.7 %convolution_convert_fusion.5 = bf16[2048,480]{0,1:T(8,128)(2,1)} fusion(bf16[2048,2560]{1,0:T(8,128)(2,1)} %all-gather.8.cloned.1.call-done.final_ref, bf16[480,2560]{1,0:T(8,128)(2,1)} %bitcast.404), kind=kOutput, calls=%fused_computation.23 | convolution fusion | flops 5034147840 | bytes 14909440 | tf_op jit(solution)/shard_map/dot_general | solution.py:33
  331.8 5.2 pad_maximum_fusion.hidden_ref
  339.4 18.2 %feed_forward.2 = (bf16[1024,512]{1,0:T(8,128)(2,1)S(1)}, bf16[1024,1024]{1,0:T(8,128)(2,1)S(1)}, bf16[512,2560]{1,0:T(8,128)(2,1)}, bf16[512,2560]{1,0:T(8,128)(2,1)}) custom-call(s32[8]{0:T(128)S(1)} %get-tuple-element.302.order_ref, bf16[1024,2560]{1,0:T(8,128)(2,1)} %pad_maximum_fusion.hidden_ref, bf16[16,128,480]{2,1,0:T(8,128)(2,1)S(1)} %bitcast.361, ...), custom_call_target="tpu_custom_call" | custom-call | flops 10066329600 | bytes 15400960 | tf_op jit(solution)/shard_map/feed_forward/pallas_call | solution.py:230
  364.6 5.3 pad_maximum_fusion.1.hidden_ref.more_ref
  370.0 18.1 %feed_forward.3 = (bf16[1024,512]{1,0:T(8,128)(2,1)S(1)}, bf16[1024,1024]{1,0:T(8,128)(2,1)S(1)}, bf16[512,2560]{1,0:T(8,128)(2,1)}, bf16[512,2560]{1,0:T(8,128)(2,1)}) custom-call(s32[8]{0:T(128)S(1)} %get-tuple-element.301.order_ref, bf16[1024,2560]{1,0:T(8,128)(2,1)} %pad_maximum_fusion.1.hidden_ref.more_ref, bf16[16,128,480]{2,1,0:T(8,128)(2,1)S(1)} %bitcast.363, ...), custom_call_target="tpu_custom_call" | custom-call | flops 10066329600 | bytes 15400960 | tf_op jit(solution)/shard_map/feed_forward/pallas_call | solution.py:230
  412.1 5.4 convolution_convert_fusion.1
  417.6 5.3 convolution_convert_fusion
  427.2 22.2 %weight_gradients.1 = bf16[2,2,640,1536]{3,2,1,0:T(8,128)(2,1)} custom-call(bf16[1024,2560]{1,0:T(8,128)(2,1)} %pad_maximum_fusion.hidden_ref, bf16[1024,2560]{1,0:T(8,128)(2,1)} %pad_maximum_fusion.1.hidden_ref.more_ref, bf16[2048,2560]{1,0:T(8,128)(2,1)} %all-gather.8.cloned.1.call-done.final_ref, bf16[1024,1024]{1,0:T(8,128)(2,1)S(1)} %copy-done.6, ...), custom_call_target="tpu_custom_call" | custom-call | flops 16106127360 | bytes 28835840 | tf_op jit(solution)/shard_map/weight_gradients/pallas_call | solution.py:285
  454.8 30.3 %collective-permute-done.25 = bf16[128,2560]{1,0:T(8,128)(2,1)S(1)} collective-permute-done((bf16[128,2560]{1,0:T(8,128)(2,1)S(1)}, bf16[128,2560]{1,0:T(8,128)(2,1)S(1)}, u32[]{:S(2)}, u32[]{:S(2)}) %collective-permute-start.25) | collective-permute-done | bytes 655392 | tf_op jit(solution)/shard_map/ppermute | solution.py:42
  494.4 9.9 %convolution_convert_fusion.4 = bf16[128,2560]{1,0:T(8,128)(2,1)} fusion(bf16[128,2560]{1,0:T(8,128)(2,1)S(1)} %convert_element_type.388, bf16[2560,2560]{1,0:T(8,128)(2,1)} %all-gather.6.cloned.1.call-done), kind=kOutput, calls=%fused_computation.21 | convolution fusion | flops 1678049280 | bytes 14417920 | tf_op jit(solution)/shard_map/dot_general | solution.py:33
  519.2 6.5 collective-permute-done.29
  525.6 4.7 all-to-all-start.6
  541.7 24.7 %collective-permute-done.30 = bf16[128,2560]{1,0:T(8,128)(2,1)} collective-permute-done((bf16[128,2560]{1,0:T(8,128)(2,1)S(1)}, bf16[128,2560]{1,0:T(8,128)(2,1)}, u32[]{:S(2)}, u32[]{:S(2)}) %collective-permute-start.30) | collective-permute-done | bytes 655392 | tf_op jit(solution)/shard_map/ppermute | solution.py:62
  588.0 5.5 all-to-all-start.7
  603.0 8.4 %collective-permute-done.34 = bf16[128,2560]{1,0:T(8,128)(2,1)S(1)} collective-permute-done((bf16[128,2560]{1,0:T(8,128)(2,1)S(1)}, bf16[128,2560]{1,0:T(8,128)(2,1)S(1)}, u32[]{:S(2)}, u32[]{:S(2)}) %collective-permute-start.34) | collective-permute-done | bytes 655392 | tf_op jit(solution)/shard_map/ppermute | solution.py:62
  618.7 8.3 %two_gradients.1 = bf16[2560,704]{1,0:T(8,128)(2,1)S(1)} custom-call(bf16[1024,2560]{1,0:T(8,128)(2,1)S(1)} %bitcast.359, bf16[1024,384]{1,0:T(8,128)(2,1)S(1)} %bitcast.357, bf16[1024,2560]{1,0:T(8,128)(2,1)S(1)} %pad_maximum_fusion.2.right_ref, bf16[1024,320]{1,0:T(8,128)(2,1)S(1)} %bitcast.360), custom_call_target="tpu_custom_call" | custom-call | flops 3690987520 | bytes 14090240 | tf_op jit(solution)/shard_map/two_gradients/pallas_call | solution.py:322
  631.9 49.5 %all-to-all-done.7 = bf16[2,640,1536]{2,1,0:T(8,128)(2,1)} async-done(((bf16[2,640,1536]{2,1,0:T(8,128)(2,1)}), bf16[2,640,1536]{2,1,0:T(8,128)(2,1)}, u32[]{:S(2)}, u32[]{:S(2)}) %all-to-all-start.7) | async-done | bytes 3932192 | tf_op jit(solution)/shard_map/all_to_all | solution.py:182
  700.2 11.2 %collective-permute-start.40 = (bf16[2,640,512]{2,1,0:T(8,128)(2,1)}, bf16[2,640,512]{2,1,0:T(8,128)(2,1)}, u32[]{:S(2)}, u32[]{:S(2)}) collective-permute-start(bf16[2,640,512]{2,1,0:T(8,128)(2,1)} %get-tuple-element.278), channel_id=1, source_target_pairs={{0,0},{4,16},{8,4},{12,20},{16,8},{20,24},{24,12},{28,28},{1,1},{5... | collective-permute-start | bytes 3932168 | tf_op jit(solution)/shard_map/ppermute | solution.py:608
  720.9 43.6 %collective-permute-done.38 = bf16[128,2560]{1,0:T(8,128)(2,1)} collective-permute-done((bf16[128,2560]{1,0:T(8,128)(2,1)}, bf16[128,2560]{1,0:T(8,128)(2,1)}, u32[]{:S(2)}, u32[]{:S(2)}) %collective-permute-start.38) | collective-permute-done | bytes 655392 | tf_op jit(solution)/shard_map/ppermute | solution.py:42
  (390 shorter events, 272.7 us)
Async XLA Ops:
  7.2 98.0 %all-gather.4.cloned.1.call-start = ((), (), s32[]{:S(2)}) async-start(), calls=%async_computation.11 | async-start | bytes 5898240 | tf_op jit(solution)/shard_map/all_gather | solution.py:402
  11.7 27.9 %collective-permute-start = (bf16[1,96,2560]{2,1,0:T(8,128)(2,1)}, bf16[1,96,2560]{2,1,0:T(8,128)(2,1)}, u32[]{:S(2)}, u32[]{:S(2)}) collective-permute-start(bf16[1,96,2560]{2,1,0:T(8,128)(2,1)} %maximum_bitcast_fusion.4), channel_id=1, source_target_pairs={{0,1},{1,0},{2,3},{3,2},{4,5},{5,4},{6,7},{7,6},{8,9},{9,8},{10,11... | collective-permute-start | bytes 1474568 | tf_op jit(solution)/shard_map/ppermute | solution.py:42
  14.7 38.4 %collective-permute-start.1 = (bf16[1,96,2560]{2,1,0:T(8,128)(2,1)}, bf16[1,96,2560]{2,1,0:T(8,128)(2,1)}, u32[]{:S(2)}, u32[]{:S(2)}) collective-permute-start(bf16[1,96,2560]{2,1,0:T(8,128)(2,1)} %maximum_bitcast_fusion.4), channel_id=1, source_target_pairs={{0,2},{2,0},{1,3},{3,1},{4,6},{6,4},{5,7},{7,5},{8,10},{10,8},{9,1... | collective-permute-start | bytes 1474568 | tf_op jit(solution)/shard_map/ppermute | solution.py:42
  17.3 35.9 %collective-permute-start.2 = (bf16[1,96,2560]{2,1,0:T(8,128)(2,1)}, bf16[1,96,2560]{2,1,0:T(8,128)(2,1)}, u32[]{:S(2)}, u32[]{:S(2)}) collective-permute-start(bf16[1,96,2560]{2,1,0:T(8,128)(2,1)} %maximum_bitcast_fusion.4), channel_id=1, source_target_pairs={{0,3},{1,2},{2,1},{3,0},{4,7},{5,6},{6,5},{7,4},{8,11},{9,10},{10,... | collective-permute-start | bytes 1474568 | tf_op jit(solution)/shard_map/ppermute | solution.py:401
  19.7 85.5 %all-to-all-start = ((bf16[32,80,384]{2,1,0:T(8,128)(2,1)}), bf16[32,80,384]{2,1,0:T(8,128)(2,1)}, u32[]{:S(2)}, u32[]{:S(2)}) async-start(bf16[32,80,384]{2,1,0:T(8,128)(2,1)} %bitcast.11), calls=%async_computation | async-start | bytes 3932160 | tf_op jit(solution)/shard_map/all_to_all | solution.py:182
  25.9 198.3 %all-gather.6.cloned.1.call-start = ((), (), s32[]{:S(2)}) async-start(), calls=%async_computation.12 | async-start | bytes 14745600 | tf_op jit(solution)/shard_map/all_gather | solution.py:426
  25.9 79.3 %collective-permute-start.3 = (bf16[240,2560]{1,0:T(8,128)(2,1)}, bf16[240,2560]{1,0:T(8,128)(2,1)}, u32[]{:S(2)}, u32[]{:S(2)}) collective-permute-start(bf16[240,2560]{1,0:T(8,128)(2,1)} %param.19), channel_id=1, source_target_pairs={{0,1},{1,0},{2,3},{3,2},{4,5},{5,4},{6,7},{7,6},{8,9},{9,8},{10,11... | collective-permute-start | bytes 3686408 | tf_op jit(solution)/shard_map/ppermute | solution.py:42
  113.3 38.7 %all-to-all-start.1 = ((bf16[16,80,480]{2,1,0:T(8,128)(2,1)}), bf16[16,80,480]{2,1,0:T(8,128)(2,1)S(1)}, u32[]{:S(2)}, u32[]{:S(2)}) async-start(bf16[16,80,480]{2,1,0:T(8,128)(2,1)} %get-tuple-element.283), calls=%async_computation.1 | async-start | bytes 2621440 | tf_op jit(solution)/shard_map/all_to_all | solution.py:182
  153.1 42.9 %all-to-all-start.2 = ((bf16[8,128,840]{1,2,0:T(8,128)(2,1)}), bf16[8,128,840]{1,2,0:T(8,128)(2,1)S(1)}, u32[]{:S(2)}, u32[]{:S(2)}) async-start(bf16[8,128,840]{1,2,0:T(8,128)(2,1)} %pad_maximum_fusion.5), calls=%async_computation.2 | async-start | bytes 3440640 | tf_op jit(solution)/shard_map/all_to_all | solution.py:182
  156.9 52.5 %collective-permute-start.4 = (bf16[128,2560]{1,0:T(8,128)(2,1)}, bf16[128,2560]{1,0:T(8,128)(2,1)S(1)}, u32[]{:S(2)}, u32[]{:S(2)}) collective-permute-start(bf16[128,2560]{1,0:T(8,128)(2,1)} %bitcast.18), channel_id=1, source_target_pairs={{0,2},{2,0},{1,3},{3,1},{4,6},{6,4},{5,7},{7,5},{8,10},{10,8},{9,1... | collective-permute-start | bytes 1966088 | tf_op jit(solution)/shard_map/ppermute | solution.py:42
  157.0 52.5 %collective-permute-start.5 = (bf16[16,80,480]{2,1,0:T(8,128)(2,1)}, bf16[16,80,480]{2,1,0:T(8,128)(2,1)}, u32[]{:S(2)}, u32[]{:S(2)}) collective-permute-start(bf16[16,80,480]{2,1,0:T(8,128)(2,1)} %copy-done.16), channel_id=1, source_target_pairs={{0,1},{1,0},{2,3},{3,2},{4,5},{5,4},{6,7},{7,6},{8,9},{9,8},{10,11... | collective-permute-start | bytes 3686408 | tf_op jit(solution)/shard_map/ppermute | solution.py:42
  203.4 107.0 %all-gather.8.cloned.1.call-start = ((), (), s32[]{:S(2)}) async-start(), calls=%async_computation.13 | async-start | bytes 11796480 | tf_op jit(solution)/shard_map/all_gather | solution.py:467
  250.5 34.2 %collective-permute-start.9 = (bf16[16,48,480]{2,1,0:T(8,128)(2,1)}, bf16[16,48,480]{2,1,0:T(8,128)(2,1)S(1)}, u32[]{:S(2)}, u32[]{:S(2)}) collective-permute-start(bf16[16,48,480]{2,1,0:T(8,128)(2,1)} %all-to-all-done.3), channel_id=1, source_target_pairs={{0,1},{1,0},{2,3},{3,2},{4,5},{5,4},{6,7},{7,6},{8,9},{9,8},{10,11... | collective-permute-start | bytes 2211848 | tf_op jit(solution)/shard_map/ppermute | solution.py:42
  250.6 34.1 %collective-permute-start.8 = (bf16[128,2560]{1,0:T(8,128)(2,1)S(1)}, bf16[128,2560]{1,0:T(8,128)(2,1)S(1)}, u32[]{:S(2)}, u32[]{:S(2)}) collective-permute-start(bf16[128,2560]{1,0:T(8,128)(2,1)S(1)} %multiply_convert_fusion.1), channel_id=1, source_target_pairs={{0,2},{2,0},{1,3},{3,1},{4,6},{6,4},{5,7},{7,5},{8,10},{10,8},{9,1... | collective-permute-start | bytes 1966088 | tf_op jit(solution)/shard_map/ppermute | solution.py:42
  253.4 34.7 %collective-permute-start.7 = (bf16[256,2560]{1,0:T(8,128)(2,1)S(1)}, bf16[256,2560]{1,0:T(8,128)(2,1)S(1)}, u32[]{:S(2)}, u32[]{:S(2)}) collective-permute-start(bf16[256,2560]{1,0:T(8,128)(2,1)S(1)} %pad_maximum_fusion.7), channel_id=1, source_target_pairs={{0,8},{4,20},{8,0},{12,28},{16,24},{20,4},{24,16},{28,12},{1,9},{5... | collective-permute-start | bytes 3932168 | tf_op jit(solution)/shard_map/ppermute | solution.py:62
  359.0 30.4 %collective-permute-start.17 = (bf16[512,2560]{1,0:T(8,128)(2,1)}, bf16[512,2560]{1,0:T(8,128)(2,1)}, u32[]{:S(2)}, u32[]{:S(2)}) collective-permute-start(bf16[512,2560]{1,0:T(8,128)(2,1)} %get-tuple-element.165), channel_id=1, source_target_pairs={{0,4},{4,0},{1,5},{5,1},{2,6},{6,2},{3,7},{7,3},{8,12},{12,8},{9,1... | collective-permute-start | bytes 7864328 | tf_op jit(solution)/shard_map/ppermute | solution.py:42
  360.8 28.5 %all-to-all-start.5 = ((bf16[8,128,320]{1,2,0:T(8,128)(2,1)}), bf16[8,128,320]{1,2,0:T(8,128)(2,1)S(1)}, u32[]{:S(2)}, u32[]{:S(2)}) async-start(bf16[8,128,320]{1,2,0:T(8,128)(2,1)} %bitcast.386), calls=%async_computation.5 | async-start | bytes 1310720 | tf_op jit(solution)/shard_map/all_to_all | solution.py:182
  364.4 202.0 %reduce-scatter.3.cloned.1.call-start = ((), (), s32[]{:S(2)}) async-start(), calls=%async_computation.14 | async-start | bytes 11796480 | tf_op jit(solution)/shard_map/reduce_scatter | solution.py:540
  410.5 39.0 %collective-permute-start.22 = (bf16[256,2560]{1,0:T(8,128)(2,1)}, bf16[256,2560]{1,0:T(8,128)(2,1)}, u32[]{:S(2)}, u32[]{:S(2)}) collective-permute-start(bf16[256,2560]{1,0:T(8,128)(2,1)} %pad_maximum_fusion.11), channel_id=1, source_target_pairs={{0,8},{4,20},{8,0},{12,28},{16,24},{20,4},{24,16},{28,12},{1,9},{5... | collective-permute-start | bytes 3932168 | tf_op jit(solution)/shard_map/ppermute | solution.py:62
  453.3 31.8 %collective-permute-start.25 = (bf16[128,2560]{1,0:T(8,128)(2,1)S(1)}, bf16[128,2560]{1,0:T(8,128)(2,1)S(1)}, u32[]{:S(2)}, u32[]{:S(2)}) collective-permute-start(bf16[128,2560]{1,0:T(8,128)(2,1)S(1)} %fusion.25), channel_id=1, source_target_pairs={{0,2},{2,0},{1,3},{3,1},{4,6},{6,4},{5,7},{7,5},{8,10},{10,8},{9,1... | collective-permute-start | bytes 1966088 | tf_op jit(solution)/shard_map/ppermute | solution.py:42
  493.7 25.5 %collective-permute-start.28 = (bf16[256,2560]{1,0:T(8,128)(2,1)}, bf16[256,2560]{1,0:T(8,128)(2,1)}, u32[]{:S(2)}, u32[]{:S(2)}) collective-permute-start(bf16[256,2560]{1,0:T(8,128)(2,1)} %pad_maximum_fusion.12), channel_id=1, source_target_pairs={{0,8},{4,20},{8,0},{12,28},{16,24},{20,4},{24,16},{28,12},{1,9},{5... | collective-permute-start | bytes 3932168 | tf_op jit(solution)/shard_map/ppermute | solution.py:62
  525.6 40.8 %all-to-all-start.6 = ((bf16[8,128,832]{1,2,0:T(8,128)(2,1)}), bf16[8,128,832]{1,2,0:T(8,128)(2,1)}, u32[]{:S(2)}, u32[]{:S(2)}) async-start(bf16[8,128,832]{1,2,0:T(8,128)(2,1)} %pad_maximum_fusion.6), calls=%async_computation.6 | async-start | bytes 3407872 | tf_op jit(solution)/shard_map/all_to_all | solution.py:182
  531.5 34.9 %collective-permute-start.30 = (bf16[128,2560]{1,0:T(8,128)(2,1)S(1)}, bf16[128,2560]{1,0:T(8,128)(2,1)}, u32[]{:S(2)}, u32[]{:S(2)}) collective-permute-start(bf16[128,2560]{1,0:T(8,128)(2,1)S(1)} %slice.365), channel_id=1, source_target_pairs={{0,16},{4,12},{8,24},{12,4},{16,0},{20,28},{24,8},{28,20},{1,17},{... | collective-permute-start | bytes 1966088 | tf_op jit(solution)/shard_map/ppermute | solution.py:62
  540.2 56.4 %collective-permute-start.33 = (bf16[512,2560]{1,0:T(8,128)(2,1)}, bf16[512,2560]{1,0:T(8,128)(2,1)}, u32[]{:S(2)}, u32[]{:S(2)}) collective-permute-start(bf16[512,2560]{1,0:T(8,128)(2,1)} %pad_maximum_fusion.3), channel_id=1, source_target_pairs={{0,8},{4,20},{8,0},{12,28},{16,24},{20,4},{24,16},{28,12},{1,9},{5... | collective-permute-start | bytes 7864328 | tf_op jit(solution)/shard_map/ppermute | solution.py:62
  588.0 93.4 %all-to-all-start.7 = ((bf16[2,640,1536]{2,1,0:T(8,128)(2,1)}), bf16[2,640,1536]{2,1,0:T(8,128)(2,1)}, u32[]{:S(2)}, u32[]{:S(2)}) async-start(bf16[2,640,1536]{2,1,0:T(8,128)(2,1)} %bitcast.384), calls=%async_computation.8 | async-start | bytes 7864320 | tf_op jit(solution)/shard_map/all_to_all | solution.py:182
  593.5 185.6 %reduce-scatter.5.cloned.1.call-start = ((), (), s32[]{:S(2)}) async-start(), calls=%async_computation.15 | async-start | bytes 4915200 | tf_op jit(solution)/shard_map/reduce_scatter | solution.py:595
  614.4 67.0 %collective-permute-start.36 = (bf16[256,2560]{1,0:T(8,128)(2,1)}, bf16[256,2560]{1,0:T(8,128)(2,1)}, u32[]{:S(2)}, u32[]{:S(2)}) collective-permute-start(bf16[256,2560]{1,0:T(8,128)(2,1)} %pad_maximum_fusion.13), channel_id=1, source_target_pairs={{0,8},{4,20},{8,0},{12,28},{16,24},{20,4},{24,16},{28,12},{1,9},{5... | collective-permute-start | bytes 3932168 | tf_op jit(solution)/shard_map/ppermute | solution.py:62
  685.9 25.6 %collective-permute-start.37 = (bf16[128,2560]{1,0:T(8,128)(2,1)}, bf16[128,2560]{1,0:T(8,128)(2,1)S(1)}, u32[]{:S(2)}, u32[]{:S(2)}) collective-permute-start(bf16[128,2560]{1,0:T(8,128)(2,1)} %slice.392), channel_id=1, source_target_pairs={{0,4},{4,0},{1,5},{5,1},{2,6},{6,2},{3,7},{7,3},{8,12},{12,8},{9,1... | collective-permute-start | bytes 1966088 | tf_op jit(solution)/shard_map/ppermute | solution.py:42
  690.2 74.3 %collective-permute-start.38 = (bf16[128,2560]{1,0:T(8,128)(2,1)}, bf16[128,2560]{1,0:T(8,128)(2,1)}, u32[]{:S(2)}, u32[]{:S(2)}) collective-permute-start(bf16[128,2560]{1,0:T(8,128)(2,1)} %slice.595), channel_id=1, source_target_pairs={{0,2},{2,0},{1,3},{3,1},{4,6},{6,4},{5,7},{7,5},{8,10},{10,8},{9,1... | collective-permute-start | bytes 1966088 | tf_op jit(solution)/shard_map/ppermute | solution.py:42
  700.2 68.2 %collective-permute-start.40 = (bf16[2,640,512]{2,1,0:T(8,128)(2,1)}, bf16[2,640,512]{2,1,0:T(8,128)(2,1)}, u32[]{:S(2)}, u32[]{:S(2)}) collective-permute-start(bf16[2,640,512]{2,1,0:T(8,128)(2,1)} %get-tuple-element.278), channel_id=1, source_target_pairs={{0,0},{4,16},{8,4},{12,20},{16,8},{20,24},{24,12},{28,28},{1,1},{5... | collective-permute-start | bytes 3932168 | tf_op jit(solution)/shard_map/ppermute | solution.py:608
  711.4 57.0 %collective-permute-start.39 = (bf16[2,640,512]{2,1,0:T(8,128)(2,1)}, bf16[2,640,512]{2,1,0:T(8,128)(2,1)}, u32[]{:S(2)}, u32[]{:S(2)}) collective-permute-start(bf16[2,640,512]{2,1,0:T(8,128)(2,1)} %get-tuple-element.279), channel_id=1, source_target_pairs={{0,16},{4,0},{8,20},{12,4},{16,24},{20,8},{24,28},{28,12},{1,17},{... | collective-permute-start | bytes 3932168 | tf_op jit(solution)/shard_map/ppermute | solution.py:608
  717.0 50.0 %all-to-all-start.8 = ((f32[32,1,240]{2,1,0:T(1,128)}), f32[32,1,240]{2,1,0:T(1,128)S(1)}, u32[]{:S(2)}, u32[]{:S(2)}) async-start(f32[32,1,240]{2,1,0:T(1,128)} %reshape.550), calls=%async_computation.9 | async-start | bytes 65536 | tf_op jit(solution)/shard_map/all_to_all | solution.py:182
  (76 other events, 660.9 us)
Sparse Core Ops, SparseCore 0:
  10.9 54.8 all-gather.3
  111.7 112.4 all-gather.5
  226.6 77.7 all-gather.7
  449.6 106.8 reduce-scatter.2
  681.5 92.7 reduce-scatter.4

commit v5 on v4

--- a/solution.py
+++ b/solution.py
@@ -393,7 +393,7 @@
     scale1 = norm_scale(residual)
     normed1 = residual * scale1
     vectors = jnp.stack([gain_attn, b_out, gain_ffn])
-    vectors = jnp.pad(vectors, ((0, 13), (0, width - rows)))
+    vectors = jnp.pad(vectors, ((0, 5), (0, width - rows)))
     out_send = jnp.concatenate([w_out, vectors])[None]
     out_near = send(out_send, "near", 1)
     down_other = send(w_down, "near", 1)
@@ -507,12 +507,11 @@
     t_give, m_keep, m_came, mixed_cols, inner_m = meet(t_give, m_keep, m_came, mixed_cols, inner_m)
     t_came = send(t_give, "core", 1)
     m_back = scatter_1(m_keep, m_came, block_len)
-    mixed_cols = pick_blocks(mixed_cols, devices).reshape(length, q_cols)
     places = order_ctx(True)
     inner_rows = jnp.concatenate([inner_m, inner_t]).reshape(2 * n_ctx, block_len, wide)
     inner_rows = pick_blocks(inner_rows, jnp.stack([places, places + n_ctx], axis=1).reshape(-1))
-    mixed_cols, inner_rows, t_keep, t_came, m_back, m_keep, m_came, inner_m, inner_t = meet(
-        mixed_cols, inner_rows, t_keep, t_came, m_back, m_keep, m_came, inner_m, inner_t
+    inner_rows, t_keep, t_came, m_back, m_keep, m_came, inner_m, inner_t = meet(
+        inner_rows, t_keep, t_came, m_back, m_keep, m_came, inner_m, inner_t
     )
     t_back = scatter_1(t_keep, t_came, block_len)
     m_sides = scatter_2(m_keep, m_came, m_back, block_len)
@@ -568,11 +567,14 @@
     d_keyval = d_keyval.reshape(n_ctx, block_len, n_ctx, kv_cols).transpose(2, 1, 0, 3)
     d_keyval = d_keyval.reshape(n_ctx, block_len, 2 * HD)
     d_send = jnp.concatenate([d_query, d_keyval], axis=2)
-    d_send, l_sides, o_back, out_keep, o_came = meet(d_send, l_sides, o_back, out_keep, o_came)
+    d_send, l_sides, o_back, out_keep, o_came, mixed_cols = meet(
+        d_send, l_sides, o_back, out_keep, o_came, mixed_cols
+    )
     came = exchange(d_send, CTX)
     l_corners = gather_2(l_sides)
     o_sides = scatter_2(out_keep, o_came, o_back, block_len)
-    came, l_corners, ffn_grad = meet(came, l_corners, ffn_grad)
+    mixed_cols = pick_blocks(mixed_cols, devices).reshape(length, q_cols)
+    came, l_corners, ffn_grad, mixed_cols = meet(came, l_corners, ffn_grad, mixed_cols)
     ffn_grad = exchange(ffn_grad[0], ("far",))
     l_halves = gather_3(l_pair, l_sides, l_corners)
     d_keyval = jnp.sum(came[:, :, q_cols:].astype(F32), axis=0).astype(BF16)

time: 803 us -> 800 us (level)
  waiting for transfers between devices: 359 us -> 346 us
    unnamed x113 -> x117, local copies, waits for them, and re-layouts: 24.7 us -> 24.7 us
  transfers between devices with their start and end apart: 55 -> 55, of which waited for: 23 -> 24; matrix products, arithmetic and copies ran while one was open for 28% -> 29% of each run, Pallas kernels for 9% -> 9%
where the time goes in v5:
time: 800 us; the launch traced here: 787 us
  waiting for transfers between devices  346 us (43%)
  other arithmetic  100 us (12%)
  local copies, waits for them, and re-layouts  98.1 us (12%)
  starting transfers between devices  92.1 us (12%)
  Pallas kernels  74.1 us (9%)
  matrix products  61.1 us (8%)
  between operations  15.4 us (2%)
    ppermute x24, waiting for transfers between devices, send(): lax.ppermute(value, axis, [(i, (i + step) % count) for i in range(count)])  173 us
    all_to_all x9, waiting for transfers between devices, exchange(): return lax.all_to_all(value, axes, split_axis=0, concat_axis=0, tiled=True)  128 us
    all_to_all x9, starting transfers between devices, exchange(): return lax.all_to_all(value, axes, split_axis=0, concat_axis=0, tiled=True)  43 us
    ppermute x14, waiting for transfers between devices, send_cross(): return lax.ppermute(value, CTX, pairs)  42.1 us
    pallas_call x2, Pallas kernels, feed_forward(): pl.pallas_call(functools.partial(middle_kernel, share, wide), out_shape=(...  36.2 us
    dot_general x4, matrix products, dot_last(): lax.dot_general(left, right, (((1,), (1,)), ((), ())), preferred_element_...  27.3 us
    unnamed x117, local copies, waits for them, and re-layouts  24.7 us
    dot_general x4, matrix products, dot(): return jnp.dot(left, right, preferred_element_type=F32)  23.5 us
  transfers between devices with their start and end apart: 55, of which 24 were waited for; matrix products, arithmetic and copies ran while one was open for 29% of the time, Pallas kernels for 9%

profile of v5, /device:TPU:0, one launch (start us, length us, event | category | flops | bytes accessed | tf_op | source)
XLA Modules:
  0.0 786.8 jit_solution(11102920348100668846)
XLA Ops:
  19.7 6.2 all-to-all-start
  29.9 5.4 reshape.478
  39.6 10.9 %collective-permute-done.1 = bf16[1,88,2560]{2,1,0:T(8,128)(2,1)} collective-permute-done((bf16[1,88,2560]{2,1,0:T(8,128)(2,1)}, bf16[1,88,2560]{2,1,0:T(8,128)(2,1)}, u32[]{:S(2)}, u32[]{:S(2)}) %collective-permute-start.1) | collective-permute-done | bytes 450592 | tf_op jit(solution)/shard_map/ppermute | solution.py:42
  50.5 52.1 %collective-permute-done.3 = bf16[240,2560]{1,0:T(8,128)(2,1)} collective-permute-done((bf16[240,2560]{1,0:T(8,128)(2,1)}, bf16[240,2560]{1,0:T(8,128)(2,1)}, u32[]{:S(2)}, u32[]{:S(2)}) %collective-permute-start.3) | collective-permute-done | bytes 1228832 | tf_op jit(solution)/shard_map/ppermute | solution.py:42
  110.7 6.2 all-to-all-start.1
  119.9 5.8 fusion.80
  127.4 22.0 %all-to-all-done.1 = bf16[16,80,480]{2,1,0:T(8,128)(2,1)S(1)} async-done(((bf16[16,80,480]{2,1,0:T(8,128)(2,1)}), bf16[16,80,480]{2,1,0:T(8,128)(2,1)S(1)}, u32[]{:S(2)}, u32[]{:S(2)}) %all-to-all-start.1) | async-done | bytes 1228832 | tf_op jit(solution)/shard_map/all_to_all | solution.py:182
  156.4 37.1 %all-to-all-done.2 = bf16[8,128,840]{1,2,0:T(8,128)(2,1)S(1)} async-done(((bf16[8,128,840]{1,2,0:T(8,128)(2,1)}), bf16[8,128,840]{1,2,0:T(8,128)(2,1)S(1)}, u32[]{:S(2)}, u32[]{:S(2)}) %all-to-all-start.2) | async-done | bytes 1720352 | tf_op jit(solution)/shard_map/all_to_all | solution.py:182
  206.8 12.6 %all-to-all-done.3 = bf16[16,48,480]{2,1,0:T(8,128)(2,1)} async-done(((bf16[16,48,480]{2,1,0:T(8,128)(2,1)}), bf16[16,48,480]{2,1,0:T(8,128)(2,1)}, u32[]{:S(2)}, u32[]{:S(2)}) %all-to-all-start.3) | async-done | bytes 737312 | tf_op jit(solution)/shard_map/all_to_all | solution.py:182
  231.4 7.0 multiply_reduce_fusion.1
  239.6 6.7 all-to-all-done.4
  256.6 25.5 %collective-permute-done.9 = bf16[16,48,480]{2,1,0:T(8,128)(2,1)S(1)} collective-permute-done((bf16[16,48,480]{2,1,0:T(8,128)(2,1)}, bf16[16,48,480]{2,1,0:T(8,128)(2,1)S(1)}, u32[]{:S(2)}, u32[]{:S(2)}) %collective-permute-start.9) | collective-permute-done | bytes 737312 | tf_op jit(solution)/shard_map/ppermute | solution.py:42
  288.6 11.3 %collective-permute-done.12 = bf16[16,32,480]{2,1,0:T(8,128)(2,1)S(1)} collective-permute-done((bf16[16,32,480]{2,1,0:T(8,128)(2,1)}, bf16[16,32,480]{2,1,0:T(8,128)(2,1)S(1)}, u32[]{:S(2)}, u32[]{:S(2)}) %collective-permute-start.12) | collective-permute-done | bytes 491552 | tf_op jit(solution)/shard_map/ppermute | solution.py:42
  309.2 9.7 %convolution_convert_fusion.5 = bf16[2048,480]{0,1:T(8,128)(2,1)} fusion(bf16[2048,2560]{1,0:T(8,128)(2,1)} %all-gather.8.cloned.1.call-done.final_ref, bf16[480,2560]{1,0:T(8,128)(2,1)} %bitcast.404), kind=kOutput, calls=%fused_computation.23 | convolution fusion | flops 5034147840 | bytes 14909440 | tf_op jit(solution)/shard_map/dot_general | solution.py:33
  329.1 5.2 pad_maximum_fusion.hidden_ref
  336.8 18.1 %feed_forward.2 = (bf16[1024,512]{1,0:T(8,128)(2,1)S(1)}, bf16[1024,1024]{1,0:T(8,128)(2,1)S(1)}, bf16[512,2560]{1,0:T(8,128)(2,1)}, bf16[512,2560]{1,0:T(8,128)(2,1)}) custom-call(s32[8]{0:T(128)S(1)} %get-tuple-element.304.order_ref, bf16[1024,2560]{1,0:T(8,128)(2,1)} %pad_maximum_fusion.hidden_ref, bf16[16,128,480]{2,1,0:T(8,128)(2,1)S(1)} %bitcast.361, ...), custom_call_target="tpu_custom_call" | custom-call | flops 10066329600 | bytes 15400960 | tf_op jit(solution)/shard_map/feed_forward/pallas_call | solution.py:230
  362.0 5.4 pad_maximum_fusion.1.hidden_ref.more_ref
  367.4 18.1 %feed_forward.3 = (bf16[1024,512]{1,0:T(8,128)(2,1)S(1)}, bf16[1024,1024]{1,0:T(8,128)(2,1)S(1)}, bf16[512,2560]{1,0:T(8,128)(2,1)}, bf16[512,2560]{1,0:T(8,128)(2,1)}) custom-call(s32[8]{0:T(128)S(1)} %get-tuple-element.303.order_ref, bf16[1024,2560]{1,0:T(8,128)(2,1)} %pad_maximum_fusion.1.hidden_ref.more_ref, bf16[16,128,480]{2,1,0:T(8,128)(2,1)S(1)} %bitcast.363, ...), custom_call_target="tpu_custom_call" | custom-call | flops 10066329600 | bytes 15400960 | tf_op jit(solution)/shard_map/feed_forward/pallas_call | solution.py:230
  409.6 5.4 convolution_convert_fusion.1
  415.0 5.3 convolution_convert_fusion
  424.7 22.2 %weight_gradients.1 = bf16[2,2,640,1536]{3,2,1,0:T(8,128)(2,1)} custom-call(bf16[1024,2560]{1,0:T(8,128)(2,1)} %pad_maximum_fusion.hidden_ref, bf16[1024,2560]{1,0:T(8,128)(2,1)} %pad_maximum_fusion.1.hidden_ref.more_ref, bf16[2048,2560]{1,0:T(8,128)(2,1)} %all-gather.8.cloned.1.call-done.final_ref, bf16[1024,1024]{1,0:T(8,128)(2,1)S(1)} %copy-done.6, ...), custom_call_target="tpu_custom_call" | custom-call | flops 16106127360 | bytes 28835840 | tf_op jit(solution)/shard_map/weight_gradients/pallas_call | solution.py:285
  452.3 30.3 %collective-permute-done.25 = bf16[128,2560]{1,0:T(8,128)(2,1)S(1)} collective-permute-done((bf16[128,2560]{1,0:T(8,128)(2,1)S(1)}, bf16[128,2560]{1,0:T(8,128)(2,1)S(1)}, u32[]{:S(2)}, u32[]{:S(2)}) %collective-permute-start.25) | collective-permute-done | bytes 655392 | tf_op jit(solution)/shard_map/ppermute | solution.py:42
  491.9 9.9 %convolution_convert_fusion.4 = bf16[128,2560]{1,0:T(8,128)(2,1)} fusion(bf16[128,2560]{1,0:T(8,128)(2,1)S(1)} %convert_element_type.388, bf16[2560,2560]{1,0:T(8,128)(2,1)} %all-gather.6.cloned.1.call-done), kind=kOutput, calls=%fused_computation.21 | convolution fusion | flops 1678049280 | bytes 14417920 | tf_op jit(solution)/shard_map/dot_general | solution.py:33
  516.6 6.5 collective-permute-done.29
  547.2 15.0 %collective-permute-done.30 = bf16[128,2560]{1,0:T(8,128)(2,1)} collective-permute-done((bf16[128,2560]{1,0:T(8,128)(2,1)}, bf16[128,2560]{1,0:T(8,128)(2,1)}, u32[]{:S(2)}, u32[]{:S(2)}) %collective-permute-start.30) | collective-permute-done | bytes 655392 | tf_op jit(solution)/shard_map/ppermute | solution.py:62
  584.2 5.5 all-to-all-start.7
  600.4 7.6 collective-permute-done.34
  616.1 8.3 %two_gradients.1 = bf16[2560,704]{1,0:T(8,128)(2,1)S(1)} custom-call(bf16[1024,2560]{1,0:T(8,128)(2,1)S(1)} %bitcast.359, bf16[1024,384]{1,0:T(8,128)(2,1)S(1)} %bitcast.357, bf16[1024,2560]{1,0:T(8,128)(2,1)S(1)} %pad_maximum_fusion.2.right_ref, bf16[1024,320]{1,0:T(8,128)(2,1)S(1)} %bitcast.360), custom_call_target="tpu_custom_call" | custom-call | flops 3690987520 | bytes 14090240 | tf_op jit(solution)/shard_map/two_gradients/pallas_call | solution.py:322
  629.3 48.7 %all-to-all-done.7 = bf16[2,640,1536]{2,1,0:T(8,128)(2,1)} async-done(((bf16[2,640,1536]{2,1,0:T(8,128)(2,1)}), bf16[2,640,1536]{2,1,0:T(8,128)(2,1)}, u32[]{:S(2)}, u32[]{:S(2)}) %all-to-all-start.7) | async-done | bytes 3932192 | tf_op jit(solution)/shard_map/all_to_all | solution.py:182
  696.8 11.2 %collective-permute-start.40 = (bf16[2,640,512]{2,1,0:T(8,128)(2,1)}, bf16[2,640,512]{2,1,0:T(8,128)(2,1)}, u32[]{:S(2)}, u32[]{:S(2)}) collective-permute-start(bf16[2,640,512]{2,1,0:T(8,128)(2,1)} %get-tuple-element.280), channel_id=1, source_target_pairs={{0,0},{4,16},{8,4},{12,20},{16,8},{20,24},{24,12},{28,28},{1,1},{5... | collective-permute-start | bytes 3932168 | tf_op jit(solution)/shard_map/ppermute | solution.py:610
  713.8 4.8 all-to-all-start.8
  718.6 40.0 %collective-permute-done.38 = bf16[128,2560]{1,0:T(8,128)(2,1)} collective-permute-done((bf16[128,2560]{1,0:T(8,128)(2,1)}, bf16[128,2560]{1,0:T(8,128)(2,1)}, u32[]{:S(2)}, u32[]{:S(2)}) %collective-permute-start.38) | collective-permute-done | bytes 655392 | tf_op jit(solution)/shard_map/ppermute | solution.py:42
  (394 shorter events, 285.6 us)
Async XLA Ops:
  7.2 95.4 %all-gather.4.cloned.1.call-start = ((), (), s32[]{:S(2)}) async-start(), calls=%async_computation.11 | async-start | bytes 5898240 | tf_op jit(solution)/shard_map/all_gather | solution.py:402
  11.7 27.9 %collective-permute-start = (bf16[1,88,2560]{2,1,0:T(8,128)(2,1)}, bf16[1,88,2560]{2,1,0:T(8,128)(2,1)}, u32[]{:S(2)}, u32[]{:S(2)}) collective-permute-start(bf16[1,88,2560]{2,1,0:T(8,128)(2,1)} %maximum_bitcast_fusion.4), channel_id=1, source_target_pairs={{0,1},{1,0},{2,3},{3,2},{4,5},{5,4},{6,7},{7,6},{8,9},{9,8},{10,11... | collective-permute-start | bytes 1351688 | tf_op jit(solution)/shard_map/ppermute | solution.py:42
  14.7 35.8 %collective-permute-start.1 = (bf16[1,88,2560]{2,1,0:T(8,128)(2,1)}, bf16[1,88,2560]{2,1,0:T(8,128)(2,1)}, u32[]{:S(2)}, u32[]{:S(2)}) collective-permute-start(bf16[1,88,2560]{2,1,0:T(8,128)(2,1)} %maximum_bitcast_fusion.4), channel_id=1, source_target_pairs={{0,2},{2,0},{1,3},{3,1},{4,6},{6,4},{5,7},{7,5},{8,10},{10,8},{9,1... | collective-permute-start | bytes 1351688 | tf_op jit(solution)/shard_map/ppermute | solution.py:42
  17.3 33.2 %collective-permute-start.2 = (bf16[1,88,2560]{2,1,0:T(8,128)(2,1)}, bf16[1,88,2560]{2,1,0:T(8,128)(2,1)}, u32[]{:S(2)}, u32[]{:S(2)}) collective-permute-start(bf16[1,88,2560]{2,1,0:T(8,128)(2,1)} %maximum_bitcast_fusion.4), channel_id=1, source_target_pairs={{0,3},{1,2},{2,1},{3,0},{4,7},{5,6},{6,5},{7,4},{8,11},{9,10},{10,... | collective-permute-start | bytes 1351688 | tf_op jit(solution)/shard_map/ppermute | solution.py:401
  19.7 83.0 %all-to-all-start = ((bf16[32,80,384]{2,1,0:T(8,128)(2,1)}), bf16[32,80,384]{2,1,0:T(8,128)(2,1)}, u32[]{:S(2)}, u32[]{:S(2)}) async-start(bf16[32,80,384]{2,1,0:T(8,128)(2,1)} %bitcast.11), calls=%async_computation | async-start | bytes 3932160 | tf_op jit(solution)/shard_map/all_to_all | solution.py:182
  25.9 195.7 %all-gather.6.cloned.1.call-start = ((), (), s32[]{:S(2)}) async-start(), calls=%async_computation.12 | async-start | bytes 14745600 | tf_op jit(solution)/shard_map/all_gather | solution.py:426
  25.9 76.7 %collective-permute-start.3 = (bf16[240,2560]{1,0:T(8,128)(2,1)}, bf16[240,2560]{1,0:T(8,128)(2,1)}, u32[]{:S(2)}, u32[]{:S(2)}) collective-permute-start(bf16[240,2560]{1,0:T(8,128)(2,1)} %param.19), channel_id=1, source_target_pairs={{0,1},{1,0},{2,3},{3,2},{4,5},{5,4},{6,7},{7,6},{8,9},{9,8},{10,11... | collective-permute-start | bytes 3686408 | tf_op jit(solution)/shard_map/ppermute | solution.py:42
  110.7 38.6 %all-to-all-start.1 = ((bf16[16,80,480]{2,1,0:T(8,128)(2,1)}), bf16[16,80,480]{2,1,0:T(8,128)(2,1)S(1)}, u32[]{:S(2)}, u32[]{:S(2)}) async-start(bf16[16,80,480]{2,1,0:T(8,128)(2,1)} %get-tuple-element.285), calls=%async_computation.1 | async-start | bytes 2621440 | tf_op jit(solution)/shard_map/all_to_all | solution.py:182
  150.5 43.0 %all-to-all-start.2 = ((bf16[8,128,840]{1,2,0:T(8,128)(2,1)}), bf16[8,128,840]{1,2,0:T(8,128)(2,1)S(1)}, u32[]{:S(2)}, u32[]{:S(2)}) async-start(bf16[8,128,840]{1,2,0:T(8,128)(2,1)} %pad_maximum_fusion.5), calls=%async_computation.2 | async-start | bytes 3440640 | tf_op jit(solution)/shard_map/all_to_all | solution.py:182
  154.3 52.5 %collective-permute-start.4 = (bf16[128,2560]{1,0:T(8,128)(2,1)}, bf16[128,2560]{1,0:T(8,128)(2,1)S(1)}, u32[]{:S(2)}, u32[]{:S(2)}) collective-permute-start(bf16[128,2560]{1,0:T(8,128)(2,1)} %bitcast.18), channel_id=1, source_target_pairs={{0,2},{2,0},{1,3},{3,1},{4,6},{6,4},{5,7},{7,5},{8,10},{10,8},{9,1... | collective-permute-start | bytes 1966088 | tf_op jit(solution)/shard_map/ppermute | solution.py:42
  154.3 52.5 %collective-permute-start.5 = (bf16[16,80,480]{2,1,0:T(8,128)(2,1)}, bf16[16,80,480]{2,1,0:T(8,128)(2,1)}, u32[]{:S(2)}, u32[]{:S(2)}) collective-permute-start(bf16[16,80,480]{2,1,0:T(8,128)(2,1)} %copy-done.16), channel_id=1, source_target_pairs={{0,1},{1,0},{2,3},{3,2},{4,5},{5,4},{6,7},{7,6},{8,9},{9,8},{10,11... | collective-permute-start | bytes 3686408 | tf_op jit(solution)/shard_map/ppermute | solution.py:42
  200.8 107.0 %all-gather.8.cloned.1.call-start = ((), (), s32[]{:S(2)}) async-start(), calls=%async_computation.13 | async-start | bytes 11796480 | tf_op jit(solution)/shard_map/all_gather | solution.py:467
  247.9 34.2 %collective-permute-start.9 = (bf16[16,48,480]{2,1,0:T(8,128)(2,1)}, bf16[16,48,480]{2,1,0:T(8,128)(2,1)S(1)}, u32[]{:S(2)}, u32[]{:S(2)}) collective-permute-start(bf16[16,48,480]{2,1,0:T(8,128)(2,1)} %all-to-all-done.3), channel_id=1, source_target_pairs={{0,1},{1,0},{2,3},{3,2},{4,5},{5,4},{6,7},{7,6},{8,9},{9,8},{10,11... | collective-permute-start | bytes 2211848 | tf_op jit(solution)/shard_map/ppermute | solution.py:42
  248.0 34.1 %collective-permute-start.8 = (bf16[128,2560]{1,0:T(8,128)(2,1)S(1)}, bf16[128,2560]{1,0:T(8,128)(2,1)S(1)}, u32[]{:S(2)}, u32[]{:S(2)}) collective-permute-start(bf16[128,2560]{1,0:T(8,128)(2,1)S(1)} %multiply_convert_fusion.1), channel_id=1, source_target_pairs={{0,2},{2,0},{1,3},{3,1},{4,6},{6,4},{5,7},{7,5},{8,10},{10,8},{9,1... | collective-permute-start | bytes 1966088 | tf_op jit(solution)/shard_map/ppermute | solution.py:42
  250.7 34.7 %collective-permute-start.7 = (bf16[256,2560]{1,0:T(8,128)(2,1)S(1)}, bf16[256,2560]{1,0:T(8,128)(2,1)S(1)}, u32[]{:S(2)}, u32[]{:S(2)}) collective-permute-start(bf16[256,2560]{1,0:T(8,128)(2,1)S(1)} %pad_maximum_fusion.7), channel_id=1, source_target_pairs={{0,8},{4,20},{8,0},{12,28},{16,24},{20,4},{24,16},{28,12},{1,9},{5... | collective-permute-start | bytes 3932168 | tf_op jit(solution)/shard_map/ppermute | solution.py:62
  356.3 30.4 %collective-permute-start.17 = (bf16[512,2560]{1,0:T(8,128)(2,1)}, bf16[512,2560]{1,0:T(8,128)(2,1)}, u32[]{:S(2)}, u32[]{:S(2)}) collective-permute-start(bf16[512,2560]{1,0:T(8,128)(2,1)} %get-tuple-element.166), channel_id=1, source_target_pairs={{0,4},{4,0},{1,5},{5,1},{2,6},{6,2},{3,7},{7,3},{8,12},{12,8},{9,1... | collective-permute-start | bytes 7864328 | tf_op jit(solution)/shard_map/ppermute | solution.py:42
  358.2 28.5 %all-to-all-start.5 = ((bf16[8,128,320]{1,2,0:T(8,128)(2,1)}), bf16[8,128,320]{1,2,0:T(8,128)(2,1)S(1)}, u32[]{:S(2)}, u32[]{:S(2)}) async-start(bf16[8,128,320]{1,2,0:T(8,128)(2,1)} %bitcast.386), calls=%async_computation.5 | async-start | bytes 1310720 | tf_op jit(solution)/shard_map/all_to_all | solution.py:182
  361.8 200.4 %reduce-scatter.3.cloned.1.call-start = ((), (), s32[]{:S(2)}) async-start(), calls=%async_computation.14 | async-start | bytes 11796480 | tf_op jit(solution)/shard_map/reduce_scatter | solution.py:539
  407.9 39.0 %collective-permute-start.22 = (bf16[256,2560]{1,0:T(8,128)(2,1)}, bf16[256,2560]{1,0:T(8,128)(2,1)}, u32[]{:S(2)}, u32[]{:S(2)}) collective-permute-start(bf16[256,2560]{1,0:T(8,128)(2,1)} %pad_maximum_fusion.11), channel_id=1, source_target_pairs={{0,8},{4,20},{8,0},{12,28},{16,24},{20,4},{24,16},{28,12},{1,9},{5... | collective-permute-start | bytes 3932168 | tf_op jit(solution)/shard_map/ppermute | solution.py:62
  450.7 31.8 %collective-permute-start.25 = (bf16[128,2560]{1,0:T(8,128)(2,1)S(1)}, bf16[128,2560]{1,0:T(8,128)(2,1)S(1)}, u32[]{:S(2)}, u32[]{:S(2)}) collective-permute-start(bf16[128,2560]{1,0:T(8,128)(2,1)S(1)} %fusion.25), channel_id=1, source_target_pairs={{0,2},{2,0},{1,3},{3,1},{4,6},{6,4},{5,7},{7,5},{8,10},{10,8},{9,1... | collective-permute-start | bytes 1966088 | tf_op jit(solution)/shard_map/ppermute | solution.py:42
  491.1 25.5 %collective-permute-start.28 = (bf16[256,2560]{1,0:T(8,128)(2,1)}, bf16[256,2560]{1,0:T(8,128)(2,1)}, u32[]{:S(2)}, u32[]{:S(2)}) collective-permute-start(bf16[256,2560]{1,0:T(8,128)(2,1)} %pad_maximum_fusion.12), channel_id=1, source_target_pairs={{0,8},{4,20},{8,0},{12,28},{16,24},{20,4},{24,16},{28,12},{1,9},{5... | collective-permute-start | bytes 3932168 | tf_op jit(solution)/shard_map/ppermute | solution.py:62
  523.1 39.1 %all-to-all-start.6 = ((bf16[8,128,832]{1,2,0:T(8,128)(2,1)}), bf16[8,128,832]{1,2,0:T(8,128)(2,1)}, u32[]{:S(2)}, u32[]{:S(2)}) async-start(bf16[8,128,832]{1,2,0:T(8,128)(2,1)} %pad_maximum_fusion.6), calls=%async_computation.6 | async-start | bytes 3407872 | tf_op jit(solution)/shard_map/all_to_all | solution.py:182
  529.8 32.4 %collective-permute-start.30 = (bf16[128,2560]{1,0:T(8,128)(2,1)}, bf16[128,2560]{1,0:T(8,128)(2,1)}, u32[]{:S(2)}, u32[]{:S(2)}) collective-permute-start(bf16[128,2560]{1,0:T(8,128)(2,1)} %slice.365), channel_id=1, source_target_pairs={{0,16},{4,12},{8,24},{12,4},{16,0},{20,28},{24,8},{28,20},{1,17},{... | collective-permute-start | bytes 1966088 | tf_op jit(solution)/shard_map/ppermute | solution.py:62
  545.7 47.1 %collective-permute-start.33 = (bf16[512,2560]{1,0:T(8,128)(2,1)}, bf16[512,2560]{1,0:T(8,128)(2,1)}, u32[]{:S(2)}, u32[]{:S(2)}) collective-permute-start(bf16[512,2560]{1,0:T(8,128)(2,1)} %pad_maximum_fusion.3), channel_id=1, source_target_pairs={{0,8},{4,20},{8,0},{12,28},{16,24},{20,4},{24,16},{28,12},{1,9},{5... | collective-permute-start | bytes 7864328 | tf_op jit(solution)/shard_map/ppermute | solution.py:62
  584.2 93.9 %all-to-all-start.7 = ((bf16[2,640,1536]{2,1,0:T(8,128)(2,1)}), bf16[2,640,1536]{2,1,0:T(8,128)(2,1)}, u32[]{:S(2)}, u32[]{:S(2)}) async-start(bf16[2,640,1536]{2,1,0:T(8,128)(2,1)} %bitcast.384), calls=%async_computation.8 | async-start | bytes 7864320 | tf_op jit(solution)/shard_map/all_to_all | solution.py:182
  589.7 184.9 %reduce-scatter.5.cloned.1.call-start = ((), (), s32[]{:S(2)}) async-start(), calls=%async_computation.15 | async-start | bytes 4915200 | tf_op jit(solution)/shard_map/reduce_scatter | solution.py:597
  611.0 67.1 %collective-permute-start.36 = (bf16[256,2560]{1,0:T(8,128)(2,1)}, bf16[256,2560]{1,0:T(8,128)(2,1)}, u32[]{:S(2)}, u32[]{:S(2)}) collective-permute-start(bf16[256,2560]{1,0:T(8,128)(2,1)} %pad_maximum_fusion.13), channel_id=1, source_target_pairs={{0,8},{4,20},{8,0},{12,28},{16,24},{20,4},{24,16},{28,12},{1,9},{5... | collective-permute-start | bytes 3932168 | tf_op jit(solution)/shard_map/ppermute | solution.py:62
  682.3 25.9 %collective-permute-start.37 = (bf16[128,2560]{1,0:T(8,128)(2,1)}, bf16[128,2560]{1,0:T(8,128)(2,1)S(1)}, u32[]{:S(2)}, u32[]{:S(2)}) collective-permute-start(bf16[128,2560]{1,0:T(8,128)(2,1)} %slice.392), channel_id=1, source_target_pairs={{0,4},{4,0},{1,5},{5,1},{2,6},{6,2},{3,7},{7,3},{8,12},{12,8},{9,1... | collective-permute-start | bytes 1966088 | tf_op jit(solution)/shard_map/ppermute | solution.py:42
  686.7 71.9 %collective-permute-start.38 = (bf16[128,2560]{1,0:T(8,128)(2,1)}, bf16[128,2560]{1,0:T(8,128)(2,1)}, u32[]{:S(2)}, u32[]{:S(2)}) collective-permute-start(bf16[128,2560]{1,0:T(8,128)(2,1)} %slice.595), channel_id=1, source_target_pairs={{0,2},{2,0},{1,3},{3,1},{4,6},{6,4},{5,7},{7,5},{8,10},{10,8},{9,1... | collective-permute-start | bytes 1966088 | tf_op jit(solution)/shard_map/ppermute | solution.py:42
  696.8 67.1 %collective-permute-start.40 = (bf16[2,640,512]{2,1,0:T(8,128)(2,1)}, bf16[2,640,512]{2,1,0:T(8,128)(2,1)}, u32[]{:S(2)}, u32[]{:S(2)}) collective-permute-start(bf16[2,640,512]{2,1,0:T(8,128)(2,1)} %get-tuple-element.280), channel_id=1, source_target_pairs={{0,0},{4,16},{8,4},{12,20},{16,8},{20,24},{24,12},{28,28},{1,1},{5... | collective-permute-start | bytes 3932168 | tf_op jit(solution)/shard_map/ppermute | solution.py:610
  708.0 55.8 %collective-permute-start.39 = (bf16[2,640,512]{2,1,0:T(8,128)(2,1)}, bf16[2,640,512]{2,1,0:T(8,128)(2,1)}, u32[]{:S(2)}, u32[]{:S(2)}) collective-permute-start(bf16[2,640,512]{2,1,0:T(8,128)(2,1)} %get-tuple-element.281), channel_id=1, source_target_pairs={{0,16},{4,0},{8,20},{12,4},{16,24},{20,8},{24,28},{28,12},{1,17},{... | collective-permute-start | bytes 3932168 | tf_op jit(solution)/shard_map/ppermute | solution.py:610
  713.8 48.7 %all-to-all-start.8 = ((f32[32,1,240]{2,1,0:T(1,128)}), f32[32,1,240]{2,1,0:T(1,128)S(1)}, u32[]{:S(2)}, u32[]{:S(2)}) async-start(f32[32,1,240]{2,1,0:T(1,128)} %reshape.550), calls=%async_computation.9 | async-start | bytes 65536 | tf_op jit(solution)/shard_map/all_to_all | solution.py:182
  (78 other events, 673.0 us)
Sparse Core Ops, SparseCore 0:
  10.9 55.2 all-gather.3
  109.1 112.3 all-gather.5
  223.9 77.7 all-gather.7
  447.0 106.8 reduce-scatter.2
  678.2 93.5 reduce-scatter.4

commit v6 on v5

--- a/solution.py
+++ b/solution.py
@@ -438,7 +438,7 @@
     came = exchange(q_send, CTX)
     gate_other = send(gate_half, "near", 1)
     came, up_send = meet(came, gateup_send[1])
-    cut = -(-rows * 3 // 5 // 16) * 16
+    cut = rows * 4 // 5 // 16 * 16
     up_first = exchange(up_send[:, :cut], GROUP)
     vectors = came[:, :, q_cols + 2 * HD :].reshape(n_ctx, -1)[:, : n_seq * 3 * rows]
     vectors = vectors.reshape(n_ctx * n_seq, 3, rows).transpose(1, 0, 2).reshape(3, width).astype(F32)

time: 800 us -> 830 us (1.038)
  blocking collectives: 0 us -> 42.1 us
  waiting for transfers between devices: 346 us -> 336 us
    all_to_all x9 -> x8, waiting for transfers between devices: 128 us -> 71.8 us  [exchange(): return lax.all_to_all(value, axes, split_axis=0, concat_axis=0, tiled=True)]
    ppermute x24, waiting for transfers between devices: 173 us -> 219 us  [send(): lax.ppermute(value, axis, [(i, (i + step) % count) for i in range(count)])]
    all_to_all x0 -> x1, blocking collectives: none -> 42.1 us  [exchange(): return lax.all_to_all(value, axes, split_axis=0, concat_axis=0, tiled=True)]
    all_to_all x9 -> x8, starting transfers between devices: 43 us -> 38.4 us  [exchange(): return lax.all_to_all(value, axes, split_axis=0, concat_axis=0, tiled=True)]
    unnamed x117 -> x129, local copies, waits for them, and re-layouts: 24.7 us -> 21.1 us
  transfers between devices with their start and end apart: 55 -> 54, of which waited for: 24 -> 20; matrix products, arithmetic and copies ran while one was open for 29% -> 28% of each run, Pallas kernels for 9% -> 9%
where the time goes in v6:
time: 830 us; the launch traced here: 819 us
  waiting for transfers between devices  336 us (40%)
  other arithmetic  99.6 us (12%)
  local copies, waits for them, and re-layouts  99.3 us (12%)
  starting transfers between devices  91.2 us (11%)
  Pallas kernels  74 us (9%)
  matrix products  61.9 us (7%)
  blocking collectives  42.1 us (5%)
  between operations  15.4 us (2%)
    ppermute x24, waiting for transfers between devices, send(): lax.ppermute(value, axis, [(i, (i + step) % count) for i in range(count)])  219 us
    all_to_all x8, waiting for transfers between devices, exchange(): return lax.all_to_all(value, axes, split_axis=0, concat_axis=0, tiled=True)  71.8 us
    ppermute x14, waiting for transfers between devices, send_cross(): return lax.ppermute(value, CTX, pairs)  45 us
    all_to_all x1, blocking collectives, exchange(): return lax.all_to_all(value, axes, split_axis=0, concat_axis=0, tiled=True)  42.1 us
    all_to_all x8, starting transfers between devices, exchange(): return lax.all_to_all(value, axes, split_axis=0, concat_axis=0, tiled=True)  38.4 us
    pallas_call x2, Pallas kernels, feed_forward(): pl.pallas_call(functools.partial(middle_kernel, share, wide), out_shape=(...  36.2 us
    dot_general x4, matrix products, dot_last(): lax.dot_general(left, right, (((1,), (1,)), ((), ())), preferred_element_...  28.5 us
    dot_general x4, matrix products, dot(): return jnp.dot(left, right, preferred_element_type=F32)  23.2 us
  transfers between devices with their start and end apart: 54, of which 20 were waited for; matrix products, arithmetic and copies ran while one was open for 28% of the time, Pallas kernels for 9%

profile of v6, /device:TPU:0, one launch (start us, length us, event | category | flops | bytes accessed | tf_op | source)
XLA Modules:
  0.0 819.3 jit_solution(14053950160445911282)
XLA Ops:
  19.7 6.2 all-to-all-start
  29.9 5.4 reshape.478
  39.6 10.9 %collective-permute-done.1 = bf16[1,88,2560]{2,1,0:T(8,128)(2,1)} collective-permute-done((bf16[1,88,2560]{2,1,0:T(8,128)(2,1)}, bf16[1,88,2560]{2,1,0:T(8,128)(2,1)}, u32[]{:S(2)}, u32[]{:S(2)}) %collective-permute-start.1) | collective-permute-done | bytes 450592 | tf_op jit(solution)/shard_map/ppermute | solution.py:42
  50.5 52.1 %collective-permute-done.3 = bf16[240,2560]{1,0:T(8,128)(2,1)} collective-permute-done((bf16[240,2560]{1,0:T(8,128)(2,1)}, bf16[240,2560]{1,0:T(8,128)(2,1)}, u32[]{:S(2)}, u32[]{:S(2)}) %collective-permute-start.3) | collective-permute-done | bytes 1228832 | tf_op jit(solution)/shard_map/ppermute | solution.py:42
  110.7 6.3 all-to-all-start.1
  120.0 5.8 fusion.80
  127.4 22.0 %all-to-all-done.1 = bf16[16,80,480]{2,1,0:T(8,128)(2,1)} async-done(((bf16[16,80,480]{2,1,0:T(8,128)(2,1)}), bf16[16,80,480]{2,1,0:T(8,128)(2,1)}, u32[]{:S(2)}, u32[]{:S(2)}) %all-to-all-start.1) | async-done | bytes 1228832 | tf_op jit(solution)/shard_map/all_to_all | solution.py:182
  149.5 42.1 %all_to_all.45 = bf16[8,128,840]{1,2,0:T(8,128)(2,1)S(1)} all-to-all(bf16[8,128,840]{1,2,0:T(8,128)(2,1)} %pad_maximum_fusion.5), channel_id=1, replica_groups=mesh['hi'=2,'lo'=2,'core'=2,'far'=2,'near'=2] {'hi','lo','core'}, dimensions={0} | all-to-all | bytes 3440640 | tf_op jit(solution)/shard_map/all_to_all | solution.py:182
  206.1 43.1 %collective-permute-done.4 = bf16[128,2560]{1,0:T(8,128)(2,1)S(1)} collective-permute-done((bf16[128,2560]{1,0:T(8,128)(2,1)S(1)}, bf16[128,2560]{1,0:T(8,128)(2,1)S(1)}, u32[]{:S(2)}, u32[]{:S(2)}) %collective-permute-start.4) | collective-permute-done | bytes 655392 | tf_op jit(solution)/shard_map/ppermute | solution.py:42
  250.1 5.7 collective-permute-done.5
  266.4 6.8 multiply_reduce_fusion.1
  286.8 29.7 %collective-permute-done.9 = bf16[16,64,480]{2,1,0:T(8,128)(2,1)S(1)} collective-permute-done((bf16[16,64,480]{2,1,0:T(8,128)(2,1)S(1)}, bf16[16,64,480]{2,1,0:T(8,128)(2,1)S(1)}, u32[]{:S(2)}, u32[]{:S(2)}) %collective-permute-start.9) | collective-permute-done | bytes 983072 | tf_op jit(solution)/shard_map/ppermute | solution.py:42
  325.5 8.3 %collective-permute-done.10 = bf16[128,2560]{1,0:T(8,128)(2,1)S(1)} collective-permute-done((bf16[128,2560]{1,0:T(8,128)(2,1)S(1)}, bf16[128,2560]{1,0:T(8,128)(2,1)S(1)}, u32[]{:S(2)}, u32[]{:S(2)}) %collective-permute-start.10) | collective-permute-done | bytes 655392 | tf_op jit(solution)/shard_map/ppermute | solution.py:62
  340.5 10.7 %convolution_convert_fusion.5 = bf16[2048,480]{0,1:T(8,128)(2,1)} fusion(bf16[2048,2560]{1,0:T(8,128)(2,1)} %all-gather.8.cloned.1.call-done.final_ref, bf16[480,2560]{1,0:T(8,128)(2,1)S(1)} %bitcast.404), kind=kOutput, calls=%fused_computation.23 | convolution fusion | flops 5034147840 | bytes 14909440 | tf_op jit(solution)/shard_map/dot_general | solution.py:33
  360.1 5.2 pad_maximum_fusion.hidden_ref
  368.5 18.1 %feed_forward.2 = (bf16[1024,512]{1,0:T(8,128)(2,1)S(1)}, bf16[1024,1024]{1,0:T(8,128)(2,1)S(1)}, bf16[512,2560]{1,0:T(8,128)(2,1)}, bf16[512,2560]{1,0:T(8,128)(2,1)}) custom-call(s32[8]{0:T(128)S(1)} %get-tuple-element.304.order_ref, bf16[1024,2560]{1,0:T(8,128)(2,1)} %pad_maximum_fusion.hidden_ref, bf16[16,128,480]{2,1,0:T(8,128)(2,1)S(1)} %bitcast.361, ...), custom_call_target="tpu_custom_call" | custom-call | flops 10066329600 | bytes 15400960 | tf_op jit(solution)/shard_map/feed_forward/pallas_call | solution.py:230
  393.6 5.3 pad_maximum_fusion.1.hidden_ref.more_ref
  398.9 18.1 %feed_forward.3 = (bf16[1024,512]{1,0:T(8,128)(2,1)S(1)}, bf16[1024,1024]{1,0:T(8,128)(2,1)S(1)}, bf16[512,2560]{1,0:T(8,128)(2,1)}, bf16[512,2560]{1,0:T(8,128)(2,1)}) custom-call(s32[8]{0:T(128)S(1)} %get-tuple-element.303.order_ref, bf16[1024,2560]{1,0:T(8,128)(2,1)} %pad_maximum_fusion.1.hidden_ref.more_ref, bf16[16,128,480]{2,1,0:T(8,128)(2,1)S(1)} %bitcast.363, ...), custom_call_target="tpu_custom_call" | custom-call | flops 10066329600 | bytes 15400960 | tf_op jit(solution)/shard_map/feed_forward/pallas_call | solution.py:230
  441.2 5.4 convolution_convert_fusion.1
  446.5 5.3 convolution_convert_fusion
  456.2 22.2 %weight_gradients.1 = bf16[2,2,640,1536]{3,2,1,0:T(8,128)(2,1)} custom-call(bf16[1024,2560]{1,0:T(8,128)(2,1)} %pad_maximum_fusion.hidden_ref, bf16[1024,2560]{1,0:T(8,128)(2,1)} %pad_maximum_fusion.1.hidden_ref.more_ref, bf16[2048,2560]{1,0:T(8,128)(2,1)} %all-gather.8.cloned.1.call-done.final_ref, bf16[1024,1024]{1,0:T(8,128)(2,1)S(1)} %copy-done.6, ...), custom_call_target="tpu_custom_call" | custom-call | flops 16106127360 | bytes 28835840 | tf_op jit(solution)/shard_map/weight_gradients/pallas_call | solution.py:285
  484.8 29.0 %collective-permute-done.25 = bf16[128,2560]{1,0:T(8,128)(2,1)S(1)} collective-permute-done((bf16[128,2560]{1,0:T(8,128)(2,1)S(1)}, bf16[128,2560]{1,0:T(8,128)(2,1)S(1)}, u32[]{:S(2)}, u32[]{:S(2)}) %collective-permute-start.25) | collective-permute-done | bytes 655392 | tf_op jit(solution)/shard_map/ppermute | solution.py:42
  522.2 10.1 %convolution_convert_fusion.4 = bf16[128,2560]{1,0:T(8,128)(2,1)} fusion(bf16[128,2560]{1,0:T(8,128)(2,1)S(1)} %convert_element_type.388, bf16[2560,2560]{1,0:T(8,128)(2,1)} %all-gather.6.cloned.1.call-done), kind=kOutput, calls=%fused_computation.21 | convolution fusion | flops 1678049280 | bytes 14417920 | tf_op jit(solution)/shard_map/dot_general | solution.py:33
  547.4 6.5 collective-permute-done.29
  553.8 4.7 all-to-all-start.6
  577.8 15.1 %collective-permute-done.30 = bf16[128,2560]{1,0:T(8,128)(2,1)} collective-permute-done((bf16[128,2560]{1,0:T(8,128)(2,1)}, bf16[128,2560]{1,0:T(8,128)(2,1)}, u32[]{:S(2)}, u32[]{:S(2)}) %collective-permute-start.30) | collective-permute-done | bytes 655392 | tf_op jit(solution)/shard_map/ppermute | solution.py:62
  615.0 5.5 all-to-all-start.7
  631.3 7.6 collective-permute-done.34
  647.0 8.3 %two_gradients.1 = bf16[2560,704]{1,0:T(8,128)(2,1)S(1)} custom-call(bf16[1024,2560]{1,0:T(8,128)(2,1)S(1)} %bitcast.359, bf16[1024,384]{1,0:T(8,128)(2,1)S(1)} %bitcast.357, bf16[1024,2560]{1,0:T(8,128)(2,1)S(1)} %pad_maximum_fusion.2.right_ref, bf16[1024,320]{1,0:T(8,128)(2,1)S(1)} %bitcast.360), custom_call_target="tpu_custom_call" | custom-call | flops 3690987520 | bytes 14090240 | tf_op jit(solution)/shard_map/two_gradients/pallas_call | solution.py:322
  660.2 48.9 %all-to-all-done.7 = bf16[2,640,1536]{2,1,0:T(8,128)(2,1)} async-done(((bf16[2,640,1536]{2,1,0:T(8,128)(2,1)}), bf16[2,640,1536]{2,1,0:T(8,128)(2,1)}, u32[]{:S(2)}, u32[]{:S(2)}) %all-to-all-start.7) | async-done | bytes 3932192 | tf_op jit(solution)/shard_map/all_to_all | solution.py:182
  727.8 11.2 %collective-permute-start.40 = (bf16[2,640,512]{2,1,0:T(8,128)(2,1)}, bf16[2,640,512]{2,1,0:T(8,128)(2,1)}, u32[]{:S(2)}, u32[]{:S(2)}) collective-permute-start(bf16[2,640,512]{2,1,0:T(8,128)(2,1)} %get-tuple-element.280), channel_id=1, source_target_pairs={{0,0},{4,16},{8,4},{12,20},{16,8},{20,24},{24,12},{28,28},{1,1},{5... | collective-permute-start | bytes 3932168 | tf_op jit(solution)/shard_map/ppermute | solution.py:610
  749.5 43.0 %collective-permute-done.38 = bf16[128,2560]{1,0:T(8,128)(2,1)} collective-permute-done((bf16[128,2560]{1,0:T(8,128)(2,1)}, bf16[128,2560]{1,0:T(8,128)(2,1)}, u32[]{:S(2)}, u32[]{:S(2)}) %collective-permute-start.38) | collective-permute-done | bytes 655392 | tf_op jit(solution)/shard_map/ppermute | solution.py:42
  (405 shorter events, 279.4 us)
Async XLA Ops:
  7.2 95.4 %all-gather.4.cloned.1.call-start = ((), (), s32[]{:S(2)}) async-start(), calls=%async_computation.11 | async-start | bytes 5898240 | tf_op jit(solution)/shard_map/all_gather | solution.py:402
  11.7 27.9 %collective-permute-start = (bf16[1,88,2560]{2,1,0:T(8,128)(2,1)}, bf16[1,88,2560]{2,1,0:T(8,128)(2,1)}, u32[]{:S(2)}, u32[]{:S(2)}) collective-permute-start(bf16[1,88,2560]{2,1,0:T(8,128)(2,1)} %maximum_bitcast_fusion.4), channel_id=1, source_target_pairs={{0,1},{1,0},{2,3},{3,2},{4,5},{5,4},{6,7},{7,6},{8,9},{9,8},{10,11... | collective-permute-start | bytes 1351688 | tf_op jit(solution)/shard_map/ppermute | solution.py:42
  14.7 35.8 %collective-permute-start.1 = (bf16[1,88,2560]{2,1,0:T(8,128)(2,1)}, bf16[1,88,2560]{2,1,0:T(8,128)(2,1)}, u32[]{:S(2)}, u32[]{:S(2)}) collective-permute-start(bf16[1,88,2560]{2,1,0:T(8,128)(2,1)} %maximum_bitcast_fusion.4), channel_id=1, source_target_pairs={{0,2},{2,0},{1,3},{3,1},{4,6},{6,4},{5,7},{7,5},{8,10},{10,8},{9,1... | collective-permute-start | bytes 1351688 | tf_op jit(solution)/shard_map/ppermute | solution.py:42
  17.3 33.2 %collective-permute-start.2 = (bf16[1,88,2560]{2,1,0:T(8,128)(2,1)}, bf16[1,88,2560]{2,1,0:T(8,128)(2,1)}, u32[]{:S(2)}, u32[]{:S(2)}) collective-permute-start(bf16[1,88,2560]{2,1,0:T(8,128)(2,1)} %maximum_bitcast_fusion.4), channel_id=1, source_target_pairs={{0,3},{1,2},{2,1},{3,0},{4,7},{5,6},{6,5},{7,4},{8,11},{9,10},{10,... | collective-permute-start | bytes 1351688 | tf_op jit(solution)/shard_map/ppermute | solution.py:401
  19.7 83.0 %all-to-all-start = ((bf16[32,80,384]{2,1,0:T(8,128)(2,1)}), bf16[32,80,384]{2,1,0:T(8,128)(2,1)}, u32[]{:S(2)}, u32[]{:S(2)}) async-start(bf16[32,80,384]{2,1,0:T(8,128)(2,1)} %bitcast.11), calls=%async_computation | async-start | bytes 3932160 | tf_op jit(solution)/shard_map/all_to_all | solution.py:182
  25.9 229.9 %all-gather.6.cloned.1.call-start = ((), (), s32[]{:S(2)}) async-start(), calls=%async_computation.12 | async-start | bytes 14745600 | tf_op jit(solution)/shard_map/all_gather | solution.py:426
  25.9 76.7 %collective-permute-start.3 = (bf16[240,2560]{1,0:T(8,128)(2,1)}, bf16[240,2560]{1,0:T(8,128)(2,1)}, u32[]{:S(2)}, u32[]{:S(2)}) collective-permute-start(bf16[240,2560]{1,0:T(8,128)(2,1)} %param.19), channel_id=1, source_target_pairs={{0,1},{1,0},{2,3},{3,2},{4,5},{5,4},{6,7},{7,6},{8,9},{9,8},{10,11... | collective-permute-start | bytes 3686408 | tf_op jit(solution)/shard_map/ppermute | solution.py:42
  110.7 38.7 %all-to-all-start.1 = ((bf16[16,80,480]{2,1,0:T(8,128)(2,1)}), bf16[16,80,480]{2,1,0:T(8,128)(2,1)}, u32[]{:S(2)}, u32[]{:S(2)}) async-start(bf16[16,80,480]{2,1,0:T(8,128)(2,1)} %get-tuple-element.285), calls=%async_computation.1 | async-start | bytes 2621440 | tf_op jit(solution)/shard_map/all_to_all | solution.py:182
  192.6 63.2 %all-to-all-start.3 = ((bf16[16,64,480]{2,1,0:T(8,128)(2,1)}), bf16[16,64,480]{2,1,0:T(8,128)(2,1)S(1)}, u32[]{:S(2)}, u32[]{:S(2)}) async-start(bf16[16,64,480]{2,1,0:T(8,128)(2,1)} %slice.330), calls=%async_computation.3 | async-start | bytes 2097152 | tf_op jit(solution)/shard_map/all_to_all | solution.py:182
  196.3 144.2 %all-gather.8.cloned.1.call-start = ((), (), s32[]{:S(2)}) async-start(), calls=%async_computation.13 | async-start | bytes 11796480 | tf_op jit(solution)/shard_map/all_gather | solution.py:467
  197.0 52.3 %collective-permute-start.4 = (bf16[128,2560]{1,0:T(8,128)(2,1)S(1)}, bf16[128,2560]{1,0:T(8,128)(2,1)S(1)}, u32[]{:S(2)}, u32[]{:S(2)}) collective-permute-start(bf16[128,2560]{1,0:T(8,128)(2,1)S(1)} %bitcast.401), channel_id=1, source_target_pairs={{0,2},{2,0},{1,3},{3,1},{4,6},{6,4},{5,7},{7,5},{8,10},{10,8},{9,1... | collective-permute-start | bytes 1966088 | tf_op jit(solution)/shard_map/ppermute | solution.py:42
  199.7 56.0 %collective-permute-start.5 = (bf16[16,80,480]{2,1,0:T(8,128)(2,1)}, bf16[16,80,480]{2,1,0:T(8,128)(2,1)}, u32[]{:S(2)}, u32[]{:S(2)}) collective-permute-start(bf16[16,80,480]{2,1,0:T(8,128)(2,1)} %all-to-all-done.1), channel_id=1, source_target_pairs={{0,1},{1,0},{2,3},{3,2},{4,5},{5,4},{6,7},{7,6},{8,9},{9,8},{10,11... | collective-permute-start | bytes 3686408 | tf_op jit(solution)/shard_map/ppermute | solution.py:42
  277.0 39.5 %collective-permute-start.9 = (bf16[16,64,480]{2,1,0:T(8,128)(2,1)S(1)}, bf16[16,64,480]{2,1,0:T(8,128)(2,1)S(1)}, u32[]{:S(2)}, u32[]{:S(2)}) collective-permute-start(bf16[16,64,480]{2,1,0:T(8,128)(2,1)S(1)} %all-to-all-done.3), channel_id=1, source_target_pairs={{0,1},{1,0},{2,3},{3,2},{4,5},{5,4},{6,7},{7,6},{8,9},{9,8},{10,11... | collective-permute-start | bytes 2949128 | tf_op jit(solution)/shard_map/ppermute | solution.py:42
  277.1 39.4 %collective-permute-start.8 = (bf16[128,2560]{1,0:T(8,128)(2,1)S(1)}, bf16[128,2560]{1,0:T(8,128)(2,1)S(1)}, u32[]{:S(2)}, u32[]{:S(2)}) collective-permute-start(bf16[128,2560]{1,0:T(8,128)(2,1)S(1)} %multiply_convert_fusion.1), channel_id=1, source_target_pairs={{0,2},{2,0},{1,3},{3,1},{4,6},{6,4},{5,7},{7,5},{8,10},{10,8},{9,1... | collective-permute-start | bytes 1966088 | tf_op jit(solution)/shard_map/ppermute | solution.py:42
  280.0 36.4 %collective-permute-start.7 = (bf16[256,2560]{1,0:T(8,128)(2,1)S(1)}, bf16[256,2560]{1,0:T(8,128)(2,1)S(1)}, u32[]{:S(2)}, u32[]{:S(2)}) collective-permute-start(bf16[256,2560]{1,0:T(8,128)(2,1)S(1)} %pad_maximum_fusion.7), channel_id=1, source_target_pairs={{0,8},{4,20},{8,0},{12,28},{16,24},{20,4},{24,16},{28,12},{1,9},{5... | collective-permute-start | bytes 3932168 | tf_op jit(solution)/shard_map/ppermute | solution.py:62
  387.9 30.4 %collective-permute-start.17 = (bf16[512,2560]{1,0:T(8,128)(2,1)}, bf16[512,2560]{1,0:T(8,128)(2,1)}, u32[]{:S(2)}, u32[]{:S(2)}) collective-permute-start(bf16[512,2560]{1,0:T(8,128)(2,1)} %get-tuple-element.166), channel_id=1, source_target_pairs={{0,4},{4,0},{1,5},{5,1},{2,6},{6,2},{3,7},{7,3},{8,12},{12,8},{9,1... | collective-permute-start | bytes 7864328 | tf_op jit(solution)/shard_map/ppermute | solution.py:42
  389.8 28.5 %all-to-all-start.5 = ((bf16[8,128,320]{1,2,0:T(8,128)(2,1)}), bf16[8,128,320]{1,2,0:T(8,128)(2,1)S(1)}, u32[]{:S(2)}, u32[]{:S(2)}) async-start(bf16[8,128,320]{1,2,0:T(8,128)(2,1)} %bitcast.385), calls=%async_computation.5 | async-start | bytes 1310720 | tf_op jit(solution)/shard_map/all_to_all | solution.py:182
  393.4 199.6 %reduce-scatter.3.cloned.1.call-start = ((), (), s32[]{:S(2)}) async-start(), calls=%async_computation.14 | async-start | bytes 11796480 | tf_op jit(solution)/shard_map/reduce_scatter | solution.py:539
  439.5 39.0 %collective-permute-start.22 = (bf16[256,2560]{1,0:T(8,128)(2,1)}, bf16[256,2560]{1,0:T(8,128)(2,1)}, u32[]{:S(2)}, u32[]{:S(2)}) collective-permute-start(bf16[256,2560]{1,0:T(8,128)(2,1)} %pad_maximum_fusion.11), channel_id=1, source_target_pairs={{0,8},{4,20},{8,0},{12,28},{16,24},{20,4},{24,16},{28,12},{1,9},{5... | collective-permute-start | bytes 3932168 | tf_op jit(solution)/shard_map/ppermute | solution.py:62
  482.4 31.4 %collective-permute-start.25 = (bf16[128,2560]{1,0:T(8,128)(2,1)S(1)}, bf16[128,2560]{1,0:T(8,128)(2,1)S(1)}, u32[]{:S(2)}, u32[]{:S(2)}) collective-permute-start(bf16[128,2560]{1,0:T(8,128)(2,1)S(1)} %fusion.25), channel_id=1, source_target_pairs={{0,2},{2,0},{1,3},{3,1},{4,6},{6,4},{5,7},{7,5},{8,10},{10,8},{9,1... | collective-permute-start | bytes 1966088 | tf_op jit(solution)/shard_map/ppermute | solution.py:42
  521.2 26.2 %collective-permute-start.28 = (bf16[256,2560]{1,0:T(8,128)(2,1)}, bf16[256,2560]{1,0:T(8,128)(2,1)}, u32[]{:S(2)}, u32[]{:S(2)}) collective-permute-start(bf16[256,2560]{1,0:T(8,128)(2,1)} %pad_maximum_fusion.12), channel_id=1, source_target_pairs={{0,8},{4,20},{8,0},{12,28},{16,24},{20,4},{24,16},{28,12},{1,9},{5... | collective-permute-start | bytes 3932168 | tf_op jit(solution)/shard_map/ppermute | solution.py:62
  553.8 39.1 %all-to-all-start.6 = ((bf16[8,128,832]{1,2,0:T(8,128)(2,1)}), bf16[8,128,832]{1,2,0:T(8,128)(2,1)}, u32[]{:S(2)}, u32[]{:S(2)}) async-start(bf16[8,128,832]{1,2,0:T(8,128)(2,1)} %pad_maximum_fusion.6), calls=%async_computation.6 | async-start | bytes 3407872 | tf_op jit(solution)/shard_map/all_to_all | solution.py:182
  560.6 32.4 %collective-permute-start.30 = (bf16[128,2560]{1,0:T(8,128)(2,1)}, bf16[128,2560]{1,0:T(8,128)(2,1)}, u32[]{:S(2)}, u32[]{:S(2)}) collective-permute-start(bf16[128,2560]{1,0:T(8,128)(2,1)} %slice.365), channel_id=1, source_target_pairs={{0,16},{4,12},{8,24},{12,4},{16,0},{20,28},{24,8},{28,20},{1,17},{... | collective-permute-start | bytes 1966088 | tf_op jit(solution)/shard_map/ppermute | solution.py:62
  576.3 47.4 %collective-permute-start.33 = (bf16[512,2560]{1,0:T(8,128)(2,1)}, bf16[512,2560]{1,0:T(8,128)(2,1)}, u32[]{:S(2)}, u32[]{:S(2)}) collective-permute-start(bf16[512,2560]{1,0:T(8,128)(2,1)} %pad_maximum_fusion.3), channel_id=1, source_target_pairs={{0,8},{4,20},{8,0},{12,28},{16,24},{20,4},{24,16},{28,12},{1,9},{5... | collective-permute-start | bytes 7864328 | tf_op jit(solution)/shard_map/ppermute | solution.py:62
  615.0 94.0 %all-to-all-start.7 = ((bf16[2,640,1536]{2,1,0:T(8,128)(2,1)}), bf16[2,640,1536]{2,1,0:T(8,128)(2,1)}, u32[]{:S(2)}, u32[]{:S(2)}) async-start(bf16[2,640,1536]{2,1,0:T(8,128)(2,1)} %bitcast.384), calls=%async_computation.8 | async-start | bytes 7864320 | tf_op jit(solution)/shard_map/all_to_all | solution.py:182
  620.5 186.5 %reduce-scatter.5.cloned.1.call-start = ((), (), s32[]{:S(2)}) async-start(), calls=%async_computation.15 | async-start | bytes 4915200 | tf_op jit(solution)/shard_map/reduce_scatter | solution.py:597
  641.9 67.2 %collective-permute-start.36 = (bf16[256,2560]{1,0:T(8,128)(2,1)}, bf16[256,2560]{1,0:T(8,128)(2,1)}, u32[]{:S(2)}, u32[]{:S(2)}) collective-permute-start(bf16[256,2560]{1,0:T(8,128)(2,1)} %pad_maximum_fusion.13), channel_id=1, source_target_pairs={{0,8},{4,20},{8,0},{12,28},{16,24},{20,4},{24,16},{28,12},{1,9},{5... | collective-permute-start | bytes 3932168 | tf_op jit(solution)/shard_map/ppermute | solution.py:62
  713.3 25.8 %collective-permute-start.37 = (bf16[128,2560]{1,0:T(8,128)(2,1)}, bf16[128,2560]{1,0:T(8,128)(2,1)S(1)}, u32[]{:S(2)}, u32[]{:S(2)}) collective-permute-start(bf16[128,2560]{1,0:T(8,128)(2,1)} %slice.392), channel_id=1, source_target_pairs={{0,4},{4,0},{1,5},{5,1},{2,6},{6,2},{3,7},{7,3},{8,12},{12,8},{9,1... | collective-permute-start | bytes 1966088 | tf_op jit(solution)/shard_map/ppermute | solution.py:42
  717.7 74.8 %collective-permute-start.38 = (bf16[128,2560]{1,0:T(8,128)(2,1)}, bf16[128,2560]{1,0:T(8,128)(2,1)}, u32[]{:S(2)}, u32[]{:S(2)}) collective-permute-start(bf16[128,2560]{1,0:T(8,128)(2,1)} %slice.595), channel_id=1, source_target_pairs={{0,2},{2,0},{1,3},{3,1},{4,6},{6,4},{5,7},{7,5},{8,10},{10,8},{9,1... | collective-permute-start | bytes 1966088 | tf_op jit(solution)/shard_map/ppermute | solution.py:42
  727.8 68.6 %collective-permute-start.40 = (bf16[2,640,512]{2,1,0:T(8,128)(2,1)}, bf16[2,640,512]{2,1,0:T(8,128)(2,1)}, u32[]{:S(2)}, u32[]{:S(2)}) collective-permute-start(bf16[2,640,512]{2,1,0:T(8,128)(2,1)} %get-tuple-element.280), channel_id=1, source_target_pairs={{0,0},{4,16},{8,4},{12,20},{16,8},{20,24},{24,12},{28,28},{1,1},{5... | collective-permute-start | bytes 3932168 | tf_op jit(solution)/shard_map/ppermute | solution.py:610
  739.0 57.3 %collective-permute-start.39 = (bf16[2,640,512]{2,1,0:T(8,128)(2,1)}, bf16[2,640,512]{2,1,0:T(8,128)(2,1)}, u32[]{:S(2)}, u32[]{:S(2)}) collective-permute-start(bf16[2,640,512]{2,1,0:T(8,128)(2,1)} %get-tuple-element.281), channel_id=1, source_target_pairs={{0,16},{4,0},{8,20},{12,4},{16,24},{20,8},{24,28},{28,12},{1,17},{... | collective-permute-start | bytes 3932168 | tf_op jit(solution)/shard_map/ppermute | solution.py:610
  744.8 50.1 %all-to-all-start.8 = ((f32[32,1,240]{2,1,0:T(1,128)}), f32[32,1,240]{2,1,0:T(1,128)S(1)}, u32[]{:S(2)}, u32[]{:S(2)}) async-start(f32[32,1,240]{2,1,0:T(1,128)} %reshape.550), calls=%async_computation.9 | async-start | bytes 65536 | tf_op jit(solution)/shard_map/all_to_all | solution.py:182
  (83 other events, 743.9 us)
Sparse Core Ops, SparseCore 0:
  10.9 55.2 all-gather.3
  109.1 108.6 all-gather.5
  258.2 72.9 all-gather.7
  478.6 107.1 reduce-scatter.2
  709.2 93.5 reduce-scatter.4
